TPU v7x, 512 devices: a whole 4x8x8 slice. The times are simulated.
512 devices in a mesh: row: 32 (over z, y_hi), col: 16 (over y_lo, x, core).
Axes of the slice: x: 4, y: 8 (y_hi: 4, y_lo: 2; y = y_hi * 2 + y_lo), z: 8, core: 2. Of those that a mesh axis runs over, the one named last changes fastest.
Arguments:
- signal: float32 [32, 65536], P(None, 'row'), may hold values from -8 to 8
- tile_values: bfloat16 [32, 16, 64, 128, 128], P('row', 'col'), may hold values from 1e-12 to 1, as said below
- tile_places: int32 [32, 16, 2, 64], P('row', 'col'), may hold values from 0 to 31, as said below
- tile_counts: int32 [32, 16], P('row', 'col'), may hold values from 16 to 64, as said below
Outputs:
- first_wavelet: float32 [32, 65536], P(None, 'row')
- second_wavelet: float32 [32, 65536], P(None, 'row')
- lowpass: float32 [32, 65536], P(None, 'row')
Inputs may be any that keep to these rules, and one draw needn't show every extreme that they name: `tile_values`: A is symmetric, and every node's row of A has a positive entry on the diagonal. Slots at or after a device's count hold tiles that are not part of A. `tile_places`: place 0 lies below 16, place 1 below 32; the live slots of one device name distinct places. `tile_counts`: some device is full in every draw.
All inputs are finite; a program needn't handle non-finite values.
Results may differ from a plain program's by a relative error of at most 0.0003.
Values may be sent and summed in bfloat16 or wider, within the bound.
No kernel may reach another device: no remote copies, remote signals or barrier semaphores. Data moves between devices by JAX's collectives and lax.ppermute only.
A program may use at most 64 MiB of HBM per device.

v0:
```python
import jax
import jax.numpy as jnp
from jax import lax
from jax.sharding import PartitionSpec as P

highest_precision = lax.Precision.HIGHEST


def broadcast(block, axis, holder):
    block = jnp.where(lax.axis_index(axis) == holder, block, jnp.zeros_like(block))
    return lax.psum(block, axis)


def on_device(signal, tile_values, tile_places, tile_counts):
    channels, row_len = signal.shape
    slot_count = tile_values.shape[2]
    tile_width = tile_values.shape[3]
    tile_rows = row_len // tile_width
    row_size = lax.axis_size("row")
    col_size = lax.axis_size("col")
    halves = row_size // col_size
    blocks = tile_values.reshape(slot_count, tile_width, tile_width)
    places = tile_places.reshape(2, slot_count)
    live_count = tile_counts.reshape(())
    live_slot = (lax.iota(jnp.int32, slot_count) < live_count).astype(jnp.float32)
    row_hot = (places[0][:, None] == lax.iota(jnp.int32, tile_rows)[None, :]).astype(
        jnp.float32
    ) * live_slot[:, None]

    def over_slots(partial_of):
        return partial_of(0, slot_count)

    def degree_part(start, size):
        sums = jnp.sum(blocks, axis=2, dtype=jnp.float32)
        return jnp.einsum("kt,ka->ta", row_hot, sums, precision=highest_precision)

    degree = lax.psum(over_slots(degree_part).reshape(row_len), "col")

    def walk(vector):
        scaled = (vector / degree[None, :]).astype(jnp.bfloat16)
        col_index = lax.axis_index("col")
        pieces = []
        for portion in range(halves):
            pieces.append(broadcast(scaled, "row", col_index * halves + portion))
        column = jnp.concatenate(pieces, axis=1).reshape(channels, halves * tile_rows, tile_width)

        def row_part(start, size):
            picked = jnp.take(column, places[1], axis=1)
            products = jnp.einsum(
                "kab,ckb->cka", blocks, picked, preferred_element_type=jnp.float32
            )
            return jnp.einsum("cka,kt->cta", products, row_hot, precision=highest_precision)

        partial_value = over_slots(row_part)
        spread = lax.psum(partial_value.reshape(channels, row_len), "col")
        return 0.5 * (vector + spread)

    walked = walk(signal)
    lowpass = walk(walked)
    return (jnp.abs(signal - walked), jnp.abs(walked - lowpass), lowpass)


def solution(mesh):
    in_specs = (
        P(None, "row"),
        P("row", "col", None, None, None),
        P("row", "col", None, None),
        P("row", "col"),
    )
    out_specs = (P(None, "row"), P(None, "row"), P(None, "row"))
    return jax.shard_map(
        on_device, mesh=mesh, in_specs=in_specs, out_specs=out_specs, check_vma=False
    )
```

profile of v0, /device:TPU:1, one launch (start us, length us, event | category | flops | bytes accessed | tf_op | source)
XLA Modules:
  0.0 943.2 jit_solution(6482408230794167764)
XLA Ops:
  7.2 0.0 copy-start.3
  7.2 0.0 copy-start.1
  7.2 0.0 all-reduce.13.cloned.1.call-start
  7.9 0.7 slice_bitcast_fusion
  8.6 0.0 copy-start
  8.6 2.4 convert_reduce_fusion
  11.0 0.1 convolution_bitcast_fusion
  11.1 33.8 %psum.49 = f32[2048]{0:T(1024)S(1)} all-reduce(f32[2048]{0:T(1024)S(1)} %convolution_bitcast_fusion), channel_id=1, replica_groups=mesh['row'=32,'col'=16] {'col'}, use_global_device_ids=true, to_apply=%region_1.0 | all-reduce | flops 2048 | bytes 16384 | tf_op jit(solution)/shard_map/psum | solution.py:37
  45.0 0.0 copy-done.1
  45.0 0.7 broadcast_select_fusion.3
  45.7 0.0 all-reduce.13.cloned.1.call-update
  45.7 0.0 all-reduce.7.cloned.1.call-start
  45.8 0.0 copy-done.3
  45.8 293.4 %all-reduce.13.cloned.1.call-done = (bf16[32,2048]{1,0:T(8,128)(2,1)}, bf16[32,2048]{1,0:T(8,128)(2,1)}) async-done(((bf16[32,2048]{1,0:T(8,128)(2,1)}, bf16[32,2048]{1,0:T(8,128)(2,1)}), (bf16[32,2048]{1,0:T(8,128)(2,1)}, bf16[32,2048]{1,0:T(8,128)(2,1)})) %all-reduce.13.cloned.1.call-update) | async-done | bytes 262160 | tf_op jit(solution)/shard_map/psum | solution.py:11
  339.2 1.0 copy_bitcast_fusion.3
  340.2 0.7 gather_fusion
  340.9 0.0 copy-done
  340.9 1.2 fusion.4
  342.1 1.2 fusion.12
  343.3 0.8 copy.24
  344.1 0.0 all-reduce.7.cloned.1.call-update
  344.1 0.0 all-reduce.11.cloned.1.call-start
  344.2 143.4 %all-reduce.7.cloned.1.call-done = f32[32,2048]{1,0:T(8,128)} async-done(((f32[32,2048]{1,0:T(8,128)}), f32[32,2048]{1,0:T(8,128)}) %all-reduce.7.cloned.1.call-update) | async-done | bytes 262160 | tf_op jit(solution)/shard_map/psum | solution.py:55
  487.5 1.7 broadcast_select_fusion.2
  489.2 0.7 broadcast_select_fusion
  489.9 0.0 all-reduce.11.cloned.1.call-update
  489.9 0.0 all-reduce.9.cloned.1.call-start
  489.9 296.5 %all-reduce.11.cloned.1.call-done = (bf16[32,2048]{1,0:T(8,128)(2,1)}, bf16[32,2048]{1,0:T(8,128)(2,1)}) async-done(((bf16[32,2048]{1,0:T(8,128)(2,1)}, bf16[32,2048]{1,0:T(8,128)(2,1)}), (bf16[32,2048]{1,0:T(8,128)(2,1)}, bf16[32,2048]{1,0:T(8,128)(2,1)})) %all-reduce.11.cloned.1.call-update) | async-done | bytes 262160 | tf_op jit(solution)/shard_map/psum | solution.py:11
  786.5 1.0 copy_bitcast_fusion.2
  787.5 0.7 gather_fusion.1
  788.1 0.0 copy-start.2
  788.1 1.2 fusion.7
  789.4 1.2 fusion.10
  790.6 0.8 copy.23
  791.4 0.0 all-reduce.9.cloned.1.call-update
  791.4 143.4 %all-reduce.9.cloned.1.call-done = f32[32,2048]{1,0:T(8,128)} async-done(((f32[32,2048]{1,0:T(8,128)}), f32[32,2048]{1,0:T(8,128)}) %all-reduce.9.cloned.1.call-update) | async-done | bytes 262160 | tf_op jit(solution)/shard_map/psum | solution.py:55
  934.8 0.0 copy-done.2
  934.8 1.9 subtract_abs_fusion
  (3 shorter events, 0.0 us)
Async XLA Ops:
  7.2 38.6 %copy-start.3 = (s32[1,1,2,64]{3,2,1,0:T(2,128)S(1)}, s32[1,1,2,64]{3,2,1,0:T(2,128)}, u32[]{:S(2)}) copy-start(s32[1,1,2,64]{3,2,1,0:T(2,128)} %param.8) | copy-start | bytes 1540
  7.2 37.8 %copy-start.1 = (f32[32,2048]{1,0:T(8,128)S(1)}, f32[32,2048]{1,0:T(8,128)}, u32[]{:S(2)}) copy-start(f32[32,2048]{1,0:T(8,128)} %param.6) | copy-start | bytes 786436
  7.2 332.0 %all-reduce.13.cloned.1.call-start = ((), (), s32[]{:S(2)}) async-start(), calls=%async_computation.3 | async-start | bytes 524288 | tf_op jit(solution)/shard_map/psum | solution.py:11
  8.6 332.3 %copy-start = (bf16[1,1,64,128,128]{4,3,2,1,0:T(8,128)(2,1)S(1)}, bf16[1,1,64,128,128]{4,3,2,1,0:T(8,128)(2,1)}, u32[]{:S(2)}) copy-start(bf16[1,1,64,128,128]{4,3,2,1,0:T(8,128)(2,1)} %param.7) | copy-start | bytes 6291460
  45.7 441.8 %all-reduce.7.cloned.1.call-start = ((), (), s32[]{:S(2)}) async-start(), calls=%async_computation | async-start | bytes 524288 | tf_op jit(solution)/shard_map/psum | solution.py:55
  344.1 442.3 %all-reduce.11.cloned.1.call-start = ((), (), s32[]{:S(2)}) async-start(), calls=%async_computation.2 | async-start | bytes 524288 | tf_op jit(solution)/shard_map/psum | solution.py:11
  489.9 444.9 %all-reduce.9.cloned.1.call-start = ((), (), s32[]{:S(2)}) async-start(), calls=%async_computation.1 | async-start | bytes 524288 | tf_op jit(solution)/shard_map/psum | solution.py:55
  788.1 146.7 %copy-start.2 = (f32[32,2048]{1,0:T(8,128)S(1)}, f32[32,2048]{1,0:T(8,128)}, u32[]{:S(2)}) copy-start(f32[32,2048]{1,0:T(8,128)} %all-reduce.7.cloned.1.call-done) | copy-start | bytes 786436
Sparse Core Ops, SparseCore 0:
  45.9 293.3 all-reduce.12
  344.3 143.2 all-reduce.6
  491.1 295.3 all-reduce.10
  791.5 143.2 all-reduce.8
where the time goes:
time: 943 us
  waiting for transfers between devices  877 us (93%)
  blocking collectives  33.8 us (4%)
  between operations  14.6 us (2%)
    psum x2, waiting for transfers between devices, broadcast(): return lax.psum(block, axis)  590 us
    psum x2, waiting for transfers between devices, walk(): spread = lax.psum(partial_value.reshape(channels, row_len), 'col')  287 us
    psum x1, blocking collectives, on_device(): degree = lax.psum(over_slots(degree_part).reshape(row_len), 'col')  33.8 us
  transfers between devices with their start and end apart: 4, of which 4 were waited for; matrix products, arithmetic and copies ran while one was open for 0% of the time, Pallas kernels for 0%

commit v1 on v0

v1 whole, which is shorter than its diff:
```python
import jax
import jax.numpy as jnp
from jax import lax
from jax.sharding import PartitionSpec as P

highest_precision = lax.Precision.HIGHEST


def to_columns(scaled, row_size, col_size):
    halves = row_size // col_size
    received = []
    for turn in range(halves):
        pairs = []
        for row in range(row_size):
            for col in range(col_size):
                target_row = halves * col + (turn + row) % halves
                pairs.append((row * col_size + col, target_row * col_size + row // halves))
        received.append(lax.ppermute(scaled, ("row", "col"), pairs))
    return jnp.concatenate(received, axis=0)


def reduce_scatter(partials):
    return jnp.sum(lax.all_to_all(partials, "col", 0, 0, tiled=True), axis=0)


def all_gather(piece, size):
    return lax.all_to_all(jnp.broadcast_to(piece[None], (size,) + piece.shape), "col", 0, 0, tiled=True)


def on_device(signal, tile_values, tile_places, tile_counts):
    channels, row_len = signal.shape
    slot_count = tile_values.shape[2]
    tile_width = tile_values.shape[3]
    tile_rows = row_len // tile_width
    row_size = lax.axis_size("row")
    col_size = lax.axis_size("col")
    halves = row_size // col_size
    row_index = lax.axis_index("row")
    col_index = lax.axis_index("col")
    blocks = tile_values.reshape(slot_count, tile_width, tile_width)
    places = tile_places.reshape(2, slot_count)
    live_count = tile_counts.reshape(())
    live_slot = (lax.iota(jnp.int32, slot_count) < live_count).astype(jnp.float32)
    row_hot = (places[0][:, None] == lax.iota(jnp.int32, tile_rows)[None, :]).astype(
        jnp.float32
    ) * live_slot[:, None]
    half_of = (places[1] // tile_rows + halves - row_index % halves) % halves
    pick = half_of * tile_rows + places[1] % tile_rows

    signal = signal.reshape(channels, tile_rows, tile_width).transpose(1, 0, 2)
    signal_piece = lax.dynamic_index_in_dim(signal, col_index, 0, keepdims=False)

    sums = jnp.sum(blocks, axis=2, dtype=jnp.float32)
    degree_part = jnp.einsum("kt,ka->ta", row_hot, sums, precision=highest_precision)
    degree = jnp.sum(all_gather(degree_part, col_size).reshape(col_size, tile_rows, tile_width), axis=0)

    def walk(vector, piece):
        scaled = (vector / degree[:, None, :]).astype(jnp.bfloat16)
        column = to_columns(scaled, row_size, col_size)
        picked = jnp.take(column, pick, axis=0)
        products = jnp.einsum("kab,kcb->kca", blocks, picked, preferred_element_type=jnp.float32)
        partials = jnp.einsum("kca,kt->tca", products, row_hot, precision=highest_precision)
        spread = reduce_scatter(partials)
        return 0.5 * (piece + spread)

    walked_piece = walk(signal, signal_piece)
    walked = all_gather(walked_piece, col_size).reshape(tile_rows, channels, tile_width)
    lowpass_piece = walk(walked, walked_piece)
    lowpass = all_gather(lowpass_piece, col_size).reshape(tile_rows, channels, tile_width)

    def back(array):
        return array.transpose(1, 0, 2).reshape(channels, row_len)

    return (back(jnp.abs(signal - walked)), back(jnp.abs(walked - lowpass)), back(lowpass))


def solution(mesh):
    in_specs = (
        P(None, "row"),
        P("row", "col", None, None, None),
        P("row", "col", None, None),
        P("row", "col"),
    )
    out_specs = (P(None, "row"), P(None, "row"), P(None, "row"))
    return jax.shard_map(
        on_device, mesh=mesh, in_specs=in_specs, out_specs=out_specs, check_vma=False
    )
```

time: 943 us -> 138 us (0.15)
  waiting for transfers between devices: 877 us -> 24.1 us
  starting transfers between devices: 0.16 us -> 49.3 us
  blocking collectives: 33.8 us -> 49.3 us
  between operations: 14.6 us -> 1.53 us
    psum x4 -> x0, waiting for transfers between devices: 877 us -> none  [the longest x2 590 us: broadcast(): return lax.psum(block, axis)]
    all_to_all x0 -> x3, blocking collectives: none -> 49.3 us  [the longest x1 28 us: reduce_scatter(): return jnp.sum(lax.all_to_all(partials, 'col', 0, 0, tiled=True), axis=0)]
    all_to_all x0 -> x2, starting transfers between devices: none -> 35.5 us  [the longest x1 25.4 us: reduce_scatter(): return jnp.sum(lax.all_to_all(partials, 'col', 0, 0, tiled=True), axis=0)]
    psum x1 -> x0, blocking collectives: 33.8 us -> none  [on_device(): degree = lax.psum(over_slots(degree_part).reshape(row_len), 'col')]
    ppermute x0 -> x4, starting transfers between devices: none -> 13.8 us  [to_columns(): received.append(lax.ppermute(scaled, ('row', 'col'), pairs))]
    all_to_all x0 -> x2, waiting for transfers between devices: none -> 13.3 us  [the longest x1 7.09 us: reduce_scatter(): return jnp.sum(lax.all_to_all(partials, 'col', 0, 0, tiled=True), axis=0)]
    ppermute x0 -> x4, waiting for transfers between devices: none -> 10.8 us  [to_columns(): received.append(lax.ppermute(scaled, ('row', 'col'), pairs))]
  transfers between devices with their start and end apart: 4 -> 6, of which waited for: 4 -> 6; matrix products, arithmetic and copies ran while one was open for 0% -> 0% of each run, Pallas kernels for 0% -> 0%
where the time goes in v1:
time: 138 us; the launch traced here: 137 us
  starting transfers between devices  49.3 us (36%)
  blocking collectives  49.3 us (36%)
  waiting for transfers between devices  24.1 us (17%)
  local copies, waits for them, and re-layouts  5.23 us (4%)
  matrix products  4.96 us (4%)
  other arithmetic  2.65 us (2%)
  between operations  1.53 us (1%)
    all_to_all x1, blocking collectives, reduce_scatter(): return jnp.sum(lax.all_to_all(partials, 'col', 0, 0, tiled=True), axis=0)  28 us
    all_to_all x1, starting transfers between devices, reduce_scatter(): return jnp.sum(lax.all_to_all(partials, 'col', 0, 0, tiled=True), axis=0)  25.4 us
    all_to_all x2, blocking collectives, all_gather(): lax.all_to_all(jnp.broadcast_to(piece[None], (size,) + piece.shape), 'col...  21.3 us
    ppermute x4, starting transfers between devices, to_columns(): received.append(lax.ppermute(scaled, ('row', 'col'), pairs))  13.8 us
    ppermute x4, waiting for transfers between devices, to_columns(): received.append(lax.ppermute(scaled, ('row', 'col'), pairs))  10.8 us
    all_to_all x1, starting transfers between devices, all_gather(): lax.all_to_all(jnp.broadcast_to(piece[None], (size,) + piece.shape), 'col...  10.2 us
    all_to_all x1, waiting for transfers between devices, reduce_scatter(): return jnp.sum(lax.all_to_all(partials, 'col', 0, 0, tiled=True), axis=0)  7.09 us
    all_to_all x1, waiting for transfers between devices, all_gather(): lax.all_to_all(jnp.broadcast_to(piece[None], (size,) + piece.shape), 'col...  6.23 us
  transfers between devices with their start and end apart: 6, of which 6 were waited for; matrix products, arithmetic and copies ran while one was open for 0% of the time, Pallas kernels for 0%

profile of v1, /device:TPU:1, one launch (start us, length us, event | category | flops | bytes accessed | tf_op | source)
XLA Modules:
  0.0 137.0 jit_solution(8794143832290592253)
XLA Ops:
  0.6 0.0 copy-start.2
  0.6 0.0 copy-start.1
  1.4 0.7 slice_bitcast_fusion
  2.0 0.0 copy-start
  2.0 2.4 %convert_reduce_fusion = f32[64,128]{1,0:T(8,128)S(1)} fusion(bf16[1,1,64,128,128]{4,3,2,1,0:T(8,128)(2,1)} %param.7), kind=kLoop, calls=%fused_computation.2 | loop fusion | flops 2088960 | bytes 2129920 | tf_op jit(solution)/shard_map/reduce_sum | solution.py:53
  4.4 0.1 fusion.19
  4.5 0.7 broadcast_in_dim.15
  5.2 10.2 %all-to-all-start = ((f32[16,16,128]{2,1,0:T(8,128)}), f32[16,16,128]{2,1,0:T(8,128)S(1)}, u32[]{:S(2)}, u32[]{:S(2)}) async-start(f32[16,16,128]{2,1,0:T(8,128)} %broadcast_in_dim.15), calls=%async_computation | async-start | bytes 262144 | tf_op jit(solution)/shard_map/all_to_all | solution.py:27
  15.4 6.2 %all-to-all-done = f32[16,16,128]{2,1,0:T(8,128)S(1)} async-done(((f32[16,16,128]{2,1,0:T(8,128)}), f32[16,16,128]{2,1,0:T(8,128)S(1)}, u32[]{:S(2)}, u32[]{:S(2)}) %all-to-all-start) | async-done | bytes 131104 | tf_op jit(solution)/shard_map/all_to_all | solution.py:27
  21.6 0.0 copy-done.1
  21.7 2.1 %collective-permute-start.1 = (bf16[16,32,128]{2,1,0:T(8,128)(2,1)S(1)}, bf16[16,32,128]{2,1,0:T(8,128)(2,1)S(1)}, u32[]{:S(2)}, u32[]{:S(2)}) collective-permute-start(bf16[16,32,128]{2,1,0:T(8,128)(2,1)S(1)} %fusion.14), channel_id=1, source_target_pairs={{0,16},{1,48},{2,80},{3,112},{4,144},{5,176},{6,208},{7,240},{8,27... | collective-permute-start | bytes 393224 | tf_op jit(solution)/shard_map/ppermute | solution.py:18
  23.8 4.2 %collective-permute-start = (bf16[16,32,128]{2,1,0:T(8,128)(2,1)S(1)}, bf16[16,32,128]{2,1,0:T(8,128)(2,1)S(1)}, u32[]{:S(2)}, u32[]{:S(2)}) collective-permute-start(bf16[16,32,128]{2,1,0:T(8,128)(2,1)S(1)} %fusion.14), channel_id=1, source_target_pairs={{0,0},{1,32},{2,64},{3,96},{4,128},{5,160},{6,192},{7,224},{8,256}... | collective-permute-start | bytes 393224 | tf_op jit(solution)/shard_map/ppermute | solution.py:18
  28.0 0.0 copy-done.2
  28.0 2.1 %collective-permute-done.1 = bf16[16,32,128]{2,1,0:T(8,128)(2,1)S(1)} collective-permute-done((bf16[16,32,128]{2,1,0:T(8,128)(2,1)S(1)}, bf16[16,32,128]{2,1,0:T(8,128)(2,1)S(1)}, u32[]{:S(2)}, u32[]{:S(2)}) %collective-permute-start.1) | collective-permute-done | bytes 131104 | tf_op jit(solution)/shard_map/ppermute | solution.py:18
  30.1 4.1 %collective-permute-done = bf16[16,32,128]{2,1,0:T(8,128)(2,1)S(1)} collective-permute-done((bf16[16,32,128]{2,1,0:T(8,128)(2,1)S(1)}, bf16[16,32,128]{2,1,0:T(8,128)(2,1)S(1)}, u32[]{:S(2)}, u32[]{:S(2)}) %collective-permute-start) | collective-permute-done | bytes 131104 | tf_op jit(solution)/shard_map/ppermute | solution.py:18
  34.2 0.7 gather_fusion
  34.9 0.0 copy-done
  34.9 1.2 fusion.2
  36.1 1.2 fusion.6
  37.3 0.8 copy.23
  38.1 25.4 %all-to-all-start.1 = ((f32[16,32,128]{2,1,0:T(8,128)}), f32[16,32,128]{2,1,0:T(8,128)S(1)}, u32[]{:S(2)}, u32[]{:S(2)}) async-start(f32[16,32,128]{2,1,0:T(8,128)} %copy.23), calls=%async_computation.1 | async-start | bytes 524288 | tf_op jit(solution)/shard_map/all_to_all | solution.py:23
  63.5 7.1 %all-to-all-done.1 = f32[16,32,128]{2,1,0:T(8,128)S(1)} async-done(((f32[16,32,128]{2,1,0:T(8,128)}), f32[16,32,128]{2,1,0:T(8,128)S(1)}, u32[]{:S(2)}, u32[]{:S(2)}) %all-to-all-start.1) | async-done | bytes 262176 | tf_op jit(solution)/shard_map/all_to_all | solution.py:23
  70.7 10.6 %all_to_all.25 = f32[16,32,128]{2,1,0:T(8,128)S(1)} all-to-all(f32[16,32,128]{2,1,0:T(8,128)S(1)} %broadcast_in_dim.16), channel_id=1, replica_groups=mesh['row'=32,'col'=16] {'col'}, dimensions={0} | all-to-all | bytes 524288 | tf_op jit(solution)/shard_map/all_to_all | solution.py:27
  81.4 1.9 %collective-permute-start.3 = (bf16[16,32,128]{2,1,0:T(8,128)(2,1)S(1)}, bf16[16,32,128]{2,1,0:T(8,128)(2,1)S(1)}, u32[]{:S(2)}, u32[]{:S(2)}) collective-permute-start(bf16[16,32,128]{2,1,0:T(8,128)(2,1)S(1)} %divide_convert_fusion), channel_id=1, source_target_pairs={{0,16},{1,48},{2,80},{3,112},{4,144},{5,176},{6,208},{7,240},{8,27... | collective-permute-start | bytes 393224 | tf_op jit(solution)/shard_map/ppermute | solution.py:18
  83.3 5.6 %collective-permute-start.2 = (bf16[16,32,128]{2,1,0:T(8,128)(2,1)S(1)}, bf16[16,32,128]{2,1,0:T(8,128)(2,1)S(1)}, u32[]{:S(2)}, u32[]{:S(2)}) collective-permute-start(bf16[16,32,128]{2,1,0:T(8,128)(2,1)S(1)} %divide_convert_fusion), channel_id=1, source_target_pairs={{0,0},{1,32},{2,64},{3,96},{4,128},{5,160},{6,192},{7,224},{8,256}... | collective-permute-start | bytes 393224 | tf_op jit(solution)/shard_map/ppermute | solution.py:18
  88.9 0.9 collective-permute-done.3
  89.8 3.7 %collective-permute-done.2 = bf16[16,32,128]{2,1,0:T(8,128)(2,1)S(1)} collective-permute-done((bf16[16,32,128]{2,1,0:T(8,128)(2,1)S(1)}, bf16[16,32,128]{2,1,0:T(8,128)(2,1)S(1)}, u32[]{:S(2)}, u32[]{:S(2)}) %collective-permute-start.2) | collective-permute-done | bytes 131104 | tf_op jit(solution)/shard_map/ppermute | solution.py:18
  93.5 0.7 gather_fusion.1
  94.2 1.2 fusion
  95.4 1.2 fusion.4
  96.6 0.1 copy.26
  96.7 28.0 %all_to_all.26 = f32[16,32,128]{2,1,0:T(8,128)S(1)} all-to-all(f32[16,32,128]{2,1,0:T(8,128)S(1)} %copy.26), channel_id=1, replica_groups=mesh['row'=32,'col'=16] {'col'}, dimensions={0} | all-to-all | bytes 524288 | tf_op jit(solution)/shard_map/all_to_all | solution.py:23
  124.8 10.6 %all_to_all.27 = f32[16,32,128]{2,1,0:T(8,128)S(1)} all-to-all(f32[16,32,128]{2,1,0:T(8,128)S(1)} %broadcast_in_dim.17), channel_id=1, replica_groups=mesh['row'=32,'col'=16] {'col'}, dimensions={0} | all-to-all | bytes 524288 | tf_op jit(solution)/shard_map/all_to_all | solution.py:27
  135.4 0.1 abs_bitcast_fusion
  135.5 0.8 copy_bitcast_fusion.1
  136.3 0.7 copy_bitcast_fusion
  (16 shorter events, 0.3 us)
Async XLA Ops:
  0.6 27.3 %copy-start.2 = (s32[1,1,2,64]{3,2,1,0:T(2,128)S(1)}, s32[1,1,2,64]{3,2,1,0:T(2,128)}, u32[]{:S(2)}) copy-start(s32[1,1,2,64]{3,2,1,0:T(2,128)} %param.8) | copy-start | bytes 1540
  0.6 21.0 %copy-start.1 = (f32[32,2048]{1,0:T(8,128)S(1)}, f32[32,2048]{1,0:T(8,128)}, u32[]{:S(2)}) copy-start(f32[32,2048]{1,0:T(8,128)} %param.6) | copy-start | bytes 786436
  2.0 32.8 %copy-start = (bf16[1,1,64,128,128]{4,3,2,1,0:T(8,128)(2,1)S(1)}, bf16[1,1,64,128,128]{4,3,2,1,0:T(8,128)(2,1)}, u32[]{:S(2)}) copy-start(bf16[1,1,64,128,128]{4,3,2,1,0:T(8,128)(2,1)} %param.7) | copy-start | bytes 6291460
  5.2 16.4 %all-to-all-start = ((f32[16,16,128]{2,1,0:T(8,128)}), f32[16,16,128]{2,1,0:T(8,128)S(1)}, u32[]{:S(2)}, u32[]{:S(2)}) async-start(f32[16,16,128]{2,1,0:T(8,128)} %broadcast_in_dim.15), calls=%async_computation | async-start | bytes 262144 | tf_op jit(solution)/shard_map/all_to_all | solution.py:27
  21.7 8.4 %collective-permute-start.1 = (bf16[16,32,128]{2,1,0:T(8,128)(2,1)S(1)}, bf16[16,32,128]{2,1,0:T(8,128)(2,1)S(1)}, u32[]{:S(2)}, u32[]{:S(2)}) collective-permute-start(bf16[16,32,128]{2,1,0:T(8,128)(2,1)S(1)} %fusion.14), channel_id=1, source_target_pairs={{0,16},{1,48},{2,80},{3,112},{4,144},{5,176},{6,208},{7,240},{8,27... | collective-permute-start | bytes 393224 | tf_op jit(solution)/shard_map/ppermute | solution.py:18
  23.8 10.4 %collective-permute-start = (bf16[16,32,128]{2,1,0:T(8,128)(2,1)S(1)}, bf16[16,32,128]{2,1,0:T(8,128)(2,1)S(1)}, u32[]{:S(2)}, u32[]{:S(2)}) collective-permute-start(bf16[16,32,128]{2,1,0:T(8,128)(2,1)S(1)} %fusion.14), channel_id=1, source_target_pairs={{0,0},{1,32},{2,64},{3,96},{4,128},{5,160},{6,192},{7,224},{8,256}... | collective-permute-start | bytes 393224 | tf_op jit(solution)/shard_map/ppermute | solution.py:18
  38.1 32.5 %all-to-all-start.1 = ((f32[16,32,128]{2,1,0:T(8,128)}), f32[16,32,128]{2,1,0:T(8,128)S(1)}, u32[]{:S(2)}, u32[]{:S(2)}) async-start(f32[16,32,128]{2,1,0:T(8,128)} %copy.23), calls=%async_computation.1 | async-start | bytes 524288 | tf_op jit(solution)/shard_map/all_to_all | solution.py:23
  81.4 8.4 %collective-permute-start.3 = (bf16[16,32,128]{2,1,0:T(8,128)(2,1)S(1)}, bf16[16,32,128]{2,1,0:T(8,128)(2,1)S(1)}, u32[]{:S(2)}, u32[]{:S(2)}) collective-permute-start(bf16[16,32,128]{2,1,0:T(8,128)(2,1)S(1)} %divide_convert_fusion), channel_id=1, source_target_pairs={{0,16},{1,48},{2,80},{3,112},{4,144},{5,176},{6,208},{7,240},{8,27... | collective-permute-start | bytes 393224 | tf_op jit(solution)/shard_map/ppermute | solution.py:18
  83.3 10.2 %collective-permute-start.2 = (bf16[16,32,128]{2,1,0:T(8,128)(2,1)S(1)}, bf16[16,32,128]{2,1,0:T(8,128)(2,1)S(1)}, u32[]{:S(2)}, u32[]{:S(2)}) collective-permute-start(bf16[16,32,128]{2,1,0:T(8,128)(2,1)S(1)} %divide_convert_fusion), channel_id=1, source_target_pairs={{0,0},{1,32},{2,64},{3,96},{4,128},{5,160},{6,192},{7,224},{8,256}... | collective-permute-start | bytes 393224 | tf_op jit(solution)/shard_map/ppermute | solution.py:18

commit v2 on v1

v2 whole, which is shorter than its diff:
```python
import jax
import jax.numpy as jnp
from jax import lax
from jax.sharding import PartitionSpec as P

highest_precision = lax.Precision.HIGHEST


def exchange(partials, axis):
    return lax.all_to_all(partials, axis, 0, 0, tiled=True)


def all_gather(piece, axis):
    return exchange(jnp.broadcast_to(piece[None], (lax.axis_size(axis),) + piece.shape), axis)


def on_device(signal, tile_values, tile_places, tile_counts):
    channels, row_len = signal.shape
    slot_count = tile_values.shape[2]
    tile_width = tile_values.shape[3]
    tile_rows = row_len // tile_width
    row_size = lax.axis_size("row")
    col_size = lax.axis_size("col")
    halves = row_size // col_size
    col_index = lax.axis_index("col")
    blocks = tile_values.reshape(slot_count, tile_width, tile_width)
    places = tile_places.reshape(2, slot_count)
    live_count = tile_counts.reshape(())
    live_slot = (lax.iota(jnp.int32, slot_count) < live_count).astype(jnp.float32)
    row_hot = (places[0][:, None] == lax.iota(jnp.int32, tile_rows)[None, :]).astype(
        jnp.float32
    ) * live_slot[:, None]
    col_hot = (places[1][:, None] == lax.iota(jnp.int32, halves * tile_rows)[None, :]).astype(
        jnp.float32
    ) * live_slot[:, None]
    to_column = [
        (row * col_size + col, ((row % halves) * tile_rows + col) * col_size + row // halves)
        for row in range(row_size)
        for col in range(col_size)
    ]
    to_row = [(target, source) for source, target in to_column]

    signal = signal.reshape(channels, tile_rows, tile_width).transpose(1, 0, 2)
    signal_piece = lax.ppermute(
        lax.dynamic_index_in_dim(signal, col_index, 0, keepdims=False), ("row", "col"), to_column
    )

    sums = jnp.sum(blocks, axis=2, dtype=jnp.float32)
    degree_part = jnp.einsum("kt,ka->ta", row_hot, sums, precision=highest_precision)
    degree = jnp.sum(all_gather(degree_part, "col").reshape(col_size, tile_rows, tile_width), axis=0)
    degree_piece = lax.ppermute(
        lax.dynamic_index_in_dim(degree, col_index, 0, keepdims=True), ("row", "col"), to_column
    )

    scaled = (signal / degree[:, None, :]).astype(jnp.bfloat16)
    picked = jnp.take(scaled, places[0], axis=0)
    products = jnp.einsum("kab,kca->kcb", blocks, picked, preferred_element_type=jnp.float32)
    partials = jnp.einsum("kcb,kt->tcb", products, col_hot, precision=highest_precision)
    spread = jnp.sum(exchange(partials, "row"), axis=0)
    walked_piece = 0.5 * (signal_piece + spread)

    scaled = (walked_piece / degree_piece).astype(jnp.bfloat16)
    column = all_gather(scaled, "row").reshape(halves * tile_rows, channels, tile_width)
    walked_piece = lax.ppermute(walked_piece, ("row", "col"), to_row)
    picked = jnp.take(column, places[1], axis=0)
    products = jnp.einsum("kab,kcb->kca", blocks, picked, preferred_element_type=jnp.float32)
    partials = jnp.einsum("kca,kt->tca", products, row_hot, precision=highest_precision)
    spread = jnp.sum(exchange(partials, "col"), axis=0)
    lowpass_piece = 0.5 * (walked_piece + spread)

    both = all_gather(jnp.stack([walked_piece, lowpass_piece]), "col")
    both = both.reshape(tile_rows, 2, channels, tile_width)
    walked = both[:, 0]
    lowpass = both[:, 1]

    def back(array):
        return array.transpose(1, 0, 2).reshape(channels, row_len)

    return (back(jnp.abs(signal - walked)), back(jnp.abs(walked - lowpass)), back(lowpass))


def solution(mesh):
    in_specs = (
        P(None, "row"),
        P("row", "col", None, None, None),
        P("row", "col", None, None),
        P("row", "col"),
    )
    out_specs = (P(None, "row"), P(None, "row"), P(None, "row"))
    return jax.shard_map(
        on_device, mesh=mesh, in_specs=in_specs, out_specs=out_specs, check_vma=False
    )
```

time: 138 us -> 119 us (0.86)
  blocking collectives: 49.3 us -> 21.2 us
  starting transfers between devices: 49.3 us -> 53.8 us
  waiting for transfers between devices: 24.1 us -> 27.4 us
  local copies, waits for them, and re-layouts: 5.23 us -> 7.18 us
    all_to_all x3 -> x1, blocking collectives: 49.3 us -> 21.2 us  [exchange(): return lax.all_to_all(partials, axis, 0, 0, tiled=True)]
    all_to_all x2 -> x4, waiting for transfers between devices: 13.3 us -> 27.4 us  [exchange(): return lax.all_to_all(partials, axis, 0, 0, tiled=True)]
    ppermute x4 -> x3, waiting for transfers between devices: 10.8 us -> 0.01 us  [the longest x1 0.01 us: on_device(): lax.ppermute(lax.dynamic_index_in_dim(signal, col_index, 0, keepdims=Fals...]
    ppermute x4 -> x3, starting transfers between devices: 13.8 us -> 16.5 us  [the longest x1 7.29 us: on_device(): lax.ppermute(lax.dynamic_index_in_dim(degree, col_index, 0, keepdims=True...]
    all_to_all x2 -> x4, starting transfers between devices: 35.5 us -> 37.3 us  [exchange(): return lax.all_to_all(partials, axis, 0, 0, tiled=True)]
  transfers between devices with their start and end apart: 6 -> 7, of which waited for: 6 -> 4; matrix products, arithmetic and copies ran while one was open for 0% -> 0% of each run, Pallas kernels for 0% -> 0%
where the time goes in v2:
time: 119 us; the launch traced here: 118 us
  starting transfers between devices  53.8 us (45%)
  waiting for transfers between devices  27.4 us (23%)
  blocking collectives  21.2 us (18%)
  local copies, waits for them, and re-layouts  7.18 us (6%)
  matrix products  4.49 us (4%)
  other arithmetic  2.45 us (2%)
  between operations  1.54 us (1%)
    all_to_all x4, starting transfers between devices, exchange(): return lax.all_to_all(partials, axis, 0, 0, tiled=True)  37.3 us
    all_to_all x4, waiting for transfers between devices, exchange(): return lax.all_to_all(partials, axis, 0, 0, tiled=True)  27.4 us
    all_to_all x1, blocking collectives, exchange(): return lax.all_to_all(partials, axis, 0, 0, tiled=True)  21.2 us
    ppermute x1, starting transfers between devices, on_device(): lax.ppermute(lax.dynamic_index_in_dim(degree, col_index, 0, keepdims=True...  7.29 us
    ppermute x1, starting transfers between devices, on_device(): lax.ppermute(lax.dynamic_index_in_dim(signal, col_index, 0, keepdims=Fals...  5.14 us
    ppermute x1, starting transfers between devices, on_device(): walked_piece = lax.ppermute(walked_piece, ('row', 'col'), to_row)  4.04 us
  transfers between devices with their start and end apart: 7, of which 4 were waited for; matrix products, arithmetic and copies ran while one was open for 0% of the time, Pallas kernels for 0%

profile of v2, /device:TPU:1, one launch (start us, length us, event | category | flops | bytes accessed | tf_op | source)
XLA Modules:
  0.0 118.1 jit_solution(3941067826924020424)
XLA Ops:
  0.6 0.0 copy-start.2
  0.6 0.0 copy-start
  0.7 0.0 copy-start.1
  0.7 0.9 slice_bitcast_fusion.3
  2.2 2.2 %convert_reduce_fusion = f32[64,128]{1,0:T(8,128)S(1)} fusion(bf16[1,1,64,128,128]{4,3,2,1,0:T(8,128)(2,1)} %param.5), kind=kLoop, calls=%fused_computation.2 | loop fusion | flops 2088960 | bytes 2129920 | tf_op jit(solution)/shard_map/reduce_sum | solution.py:48
  4.4 0.1 fusion.23
  4.5 0.7 broadcast_in_dim.25
  5.2 10.2 %all-to-all-start = ((f32[16,16,128]{2,1,0:T(8,128)}), f32[16,16,128]{2,1,0:T(8,128)S(1)}, u32[]{:S(2)}, u32[]{:S(2)}) async-start(f32[16,16,128]{2,1,0:T(8,128)} %broadcast_in_dim.25), calls=%async_computation | async-start | bytes 262144 | tf_op jit(solution)/shard_map/all_to_all | solution.py:10
  15.4 0.0 copy-done.2
  15.4 6.2 %all-to-all-done = f32[16,16,128]{2,1,0:T(8,128)S(1)} async-done(((f32[16,16,128]{2,1,0:T(8,128)}), f32[16,16,128]{2,1,0:T(8,128)S(1)}, u32[]{:S(2)}, u32[]{:S(2)}) %all-to-all-start) | async-done | bytes 131104 | tf_op jit(solution)/shard_map/all_to_all | solution.py:10
  21.6 0.0 copy-done.1
  21.7 0.7 gather_fusion
  22.4 0.0 copy-done
  22.4 0.7 fusion.2
  23.1 1.2 %fusion.6 = f32[32,32,128]{2,0,1:T(8,128)S(1)} fusion(f32[64,32,128]{2,1,0:T(8,128)S(1)} %fusion.2, f32[64]{0:T(128)S(1)} %compare_convert_fusion, s32[64]{0:T(128)S(1)} %get-tuple-element.11), kind=kOutput, calls=%fused_computation.9 | convolution fusion | flops 100667392 | bytes 1573376 | tf_op jit(solution)/shard_map/kcb,kt->tcb/dot_general | solution.py:58
  24.3 1.1 copy.25
  25.4 11.4 %all-to-all-start.1 = ((f32[32,32,128]{2,1,0:T(8,128)}), f32[32,32,128]{2,1,0:T(8,128)S(1)}, u32[]{:S(2)}, u32[]{:S(2)}) async-start(f32[32,32,128]{2,1,0:T(8,128)} %copy.25), calls=%async_computation.1 | async-start | bytes 1048576 | tf_op jit(solution)/shard_map/all_to_all | solution.py:10
  36.9 5.1 %collective-permute-start = (f32[32,128]{1,0:T(8,128)S(1)}, f32[32,128]{1,0:T(8,128)S(1)}, u32[]{:S(2)}, u32[]{:S(2)}) collective-permute-start(f32[32,128]{1,0:T(8,128)S(1)} %bitcast.104), channel_id=1, source_target_pairs={{0,0},{1,16},{2,32},{3,48},{4,64},{5,80},{6,96},{7,112},{8,128},{9... | collective-permute-start | bytes 49160 | tf_op jit(solution)/shard_map/ppermute | solution.py:44
  42.0 7.3 %collective-permute-start.2 = (f32[1,128]{1,0:T(1,128)S(1)}, f32[1,128]{1,0:T(1,128)S(1)}, u32[]{:S(2)}, u32[]{:S(2)}) collective-permute-start(f32[1,128]{1,0:T(1,128)S(1)} %constant_dynamic-slice_fusion), channel_id=1, source_target_pairs={{0,0},{1,16},{2,32},{3,48},{4,64},{5,80},{6,96},{7,112},{8,128},{9... | collective-permute-start | bytes 1544 | tf_op jit(solution)/shard_map/ppermute | solution.py:51
  49.3 5.4 %all-to-all-done.1 = f32[32,32,128]{2,1,0:T(8,128)S(1)} async-done(((f32[32,32,128]{2,1,0:T(8,128)}), f32[32,32,128]{2,1,0:T(8,128)S(1)}, u32[]{:S(2)}, u32[]{:S(2)}) %all-to-all-start.1) | async-done | bytes 524320 | tf_op jit(solution)/shard_map/all_to_all | solution.py:10
  54.8 0.0 collective-permute-done
  54.8 0.0 collective-permute-done.2
  54.8 0.7 broadcast_in_dim.28
  55.6 9.3 %all-to-all-start.2 = ((bf16[32,32,128]{2,1,0:T(8,128)(2,1)}), bf16[32,32,128]{2,1,0:T(8,128)(2,1)S(1)}, u32[]{:S(2)}, u32[]{:S(2)}) async-start(bf16[32,32,128]{2,1,0:T(8,128)(2,1)} %broadcast_in_dim.28), calls=%async_computation.2 | async-start | bytes 524288 | tf_op jit(solution)/shard_map/all_to_all | solution.py:10
  64.9 12.7 %all-to-all-done.2 = bf16[32,32,128]{2,1,0:T(8,128)(2,1)S(1)} async-done(((bf16[32,32,128]{2,1,0:T(8,128)(2,1)}), bf16[32,32,128]{2,1,0:T(8,128)(2,1)S(1)}, u32[]{:S(2)}, u32[]{:S(2)}) %all-to-all-start.2) | async-done | bytes 262176 | tf_op jit(solution)/shard_map/all_to_all | solution.py:10
  77.5 0.7 gather_fusion.1
  78.2 1.2 %fusion = f32[64,32,128]{2,1,0:T(8,128)S(1)} fusion(bf16[1,1,64,128,128]{4,3,2,1,0:T(8,128)(2,1)S(1)} %copy-done, bf16[64,32,128]{2,1,0:T(8,128)(2,1)S(1)} %gather_fusion.1, pred[64]{0:T(512)(128)(4,1)S(1)} %get-tuple-element.7), kind=kOutput, calls=%fused_computation.3 | convolution fusion | flops 67371008 | bytes 3670080 | tf_op jit(solution)/shard_map/kab,kcb->kca/dot_general | solution.py:66
  79.4 1.2 %fusion.4 = f32[16,32,128]{2,0,1:T(8,128)S(1)} fusion(f32[64,32,128]{2,1,0:T(8,128)S(1)} %fusion, f32[64]{0:T(128)S(1)} %compare_convert_fusion, s32[64]{0:T(128)S(1)} %get-tuple-element.12), kind=kOutput, calls=%fused_computation.7 | convolution fusion | flops 50333696 | bytes 1311232 | tf_op jit(solution)/shard_map/kca,kt->tca/dot_general | solution.py:67
  80.6 0.8 copy.27
  81.4 6.5 %all-to-all-start.3 = ((f32[16,32,128]{2,1,0:T(8,128)}), f32[16,32,128]{2,1,0:T(8,128)S(1)}, u32[]{:S(2)}, u32[]{:S(2)}) async-start(f32[16,32,128]{2,1,0:T(8,128)} %copy.27), calls=%async_computation.3 | async-start | bytes 524288 | tf_op jit(solution)/shard_map/all_to_all | solution.py:10
  87.9 4.0 %collective-permute-start.1 = (f32[32,128]{1,0:T(8,128)S(1)}, f32[32,128]{1,0:T(8,128)S(1)}, u32[]{:S(2)}, u32[]{:S(2)}) collective-permute-start(f32[32,128]{1,0:T(8,128)S(1)} %get-tuple-element.4), channel_id=1, source_target_pairs={{0,0},{16,1},{32,2},{48,3},{64,4},{80,5},{96,6},{112,7},{128,8},{1... | collective-permute-start | bytes 49160 | tf_op jit(solution)/shard_map/ppermute | solution.py:64
  92.0 3.1 %all-to-all-done.3 = f32[16,32,128]{2,1,0:T(8,128)S(1)} async-done(((f32[16,32,128]{2,1,0:T(8,128)}), f32[16,32,128]{2,1,0:T(8,128)S(1)}, u32[]{:S(2)}, u32[]{:S(2)}) %all-to-all-start.3) | async-done | bytes 262176 | tf_op jit(solution)/shard_map/all_to_all | solution.py:10
  95.1 0.0 collective-permute-done.1
  95.1 0.1 broadcast_in_dim.46
  95.2 21.2 %all_to_all.25 = f32[16,2,32,128]{3,2,1,0:T(8,128)S(1)} all-to-all(f32[16,2,32,128]{3,2,1,0:T(8,128)S(1)} %broadcast_in_dim.46), channel_id=1, replica_groups=mesh['row'=32,'col'=16] {'col'}, dimensions={0} | all-to-all | bytes 1048576 | tf_op jit(solution)/shard_map/all_to_all | solution.py:10
  116.4 0.1 fusion.18
  116.5 0.8 copy_bitcast_fusion.1
  117.3 0.7 copy_bitcast_fusion
  (15 shorter events, 0.3 us)
Async XLA Ops:
  0.6 14.8 %copy-start.2 = (s32[1,1,2,64]{3,2,1,0:T(2,128)S(1)}, s32[1,1,2,64]{3,2,1,0:T(2,128)}, u32[]{:S(2)}) copy-start(s32[1,1,2,64]{3,2,1,0:T(2,128)} %param.6) | copy-start | bytes 1540
  0.6 21.7 %copy-start = (bf16[1,1,64,128,128]{4,3,2,1,0:T(8,128)(2,1)S(1)}, bf16[1,1,64,128,128]{4,3,2,1,0:T(8,128)(2,1)}, u32[]{:S(2)}) copy-start(bf16[1,1,64,128,128]{4,3,2,1,0:T(8,128)(2,1)} %param.5) | copy-start | bytes 6291460
  0.7 21.0 %copy-start.1 = (f32[32,2048]{1,0:T(8,128)S(1)}, f32[32,2048]{1,0:T(8,128)}, u32[]{:S(2)}) copy-start(f32[32,2048]{1,0:T(8,128)} %param.4) | copy-start | bytes 786436
  5.2 16.4 %all-to-all-start = ((f32[16,16,128]{2,1,0:T(8,128)}), f32[16,16,128]{2,1,0:T(8,128)S(1)}, u32[]{:S(2)}, u32[]{:S(2)}) async-start(f32[16,16,128]{2,1,0:T(8,128)} %broadcast_in_dim.25), calls=%async_computation | async-start | bytes 262144 | tf_op jit(solution)/shard_map/all_to_all | solution.py:10
  25.4 29.3 %all-to-all-start.1 = ((f32[32,32,128]{2,1,0:T(8,128)}), f32[32,32,128]{2,1,0:T(8,128)S(1)}, u32[]{:S(2)}, u32[]{:S(2)}) async-start(f32[32,32,128]{2,1,0:T(8,128)} %copy.25), calls=%async_computation.1 | async-start | bytes 1048576 | tf_op jit(solution)/shard_map/all_to_all | solution.py:10
  36.9 17.9 %collective-permute-start = (f32[32,128]{1,0:T(8,128)S(1)}, f32[32,128]{1,0:T(8,128)S(1)}, u32[]{:S(2)}, u32[]{:S(2)}) collective-permute-start(f32[32,128]{1,0:T(8,128)S(1)} %bitcast.104), channel_id=1, source_target_pairs={{0,0},{1,16},{2,32},{3,48},{4,64},{5,80},{6,96},{7,112},{8,128},{9... | collective-permute-start | bytes 49160 | tf_op jit(solution)/shard_map/ppermute | solution.py:44
  42.0 12.8 %collective-permute-start.2 = (f32[1,128]{1,0:T(1,128)S(1)}, f32[1,128]{1,0:T(1,128)S(1)}, u32[]{:S(2)}, u32[]{:S(2)}) collective-permute-start(f32[1,128]{1,0:T(1,128)S(1)} %constant_dynamic-slice_fusion), channel_id=1, source_target_pairs={{0,0},{1,16},{2,32},{3,48},{4,64},{5,80},{6,96},{7,112},{8,128},{9... | collective-permute-start | bytes 1544 | tf_op jit(solution)/shard_map/ppermute | solution.py:51
  55.6 22.0 %all-to-all-start.2 = ((bf16[32,32,128]{2,1,0:T(8,128)(2,1)}), bf16[32,32,128]{2,1,0:T(8,128)(2,1)S(1)}, u32[]{:S(2)}, u32[]{:S(2)}) async-start(bf16[32,32,128]{2,1,0:T(8,128)(2,1)} %broadcast_in_dim.28), calls=%async_computation.2 | async-start | bytes 524288 | tf_op jit(solution)/shard_map/all_to_all | solution.py:10
  81.4 13.7 %all-to-all-start.3 = ((f32[16,32,128]{2,1,0:T(8,128)}), f32[16,32,128]{2,1,0:T(8,128)S(1)}, u32[]{:S(2)}, u32[]{:S(2)}) async-start(f32[16,32,128]{2,1,0:T(8,128)} %copy.27), calls=%async_computation.3 | async-start | bytes 524288 | tf_op jit(solution)/shard_map/all_to_all | solution.py:10
  87.9 7.2 %collective-permute-start.1 = (f32[32,128]{1,0:T(8,128)S(1)}, f32[32,128]{1,0:T(8,128)S(1)}, u32[]{:S(2)}, u32[]{:S(2)}) collective-permute-start(f32[32,128]{1,0:T(8,128)S(1)} %get-tuple-element.4), channel_id=1, source_target_pairs={{0,0},{16,1},{32,2},{48,3},{64,4},{80,5},{96,6},{112,7},{128,8},{1... | collective-permute-start | bytes 49160 | tf_op jit(solution)/shard_map/ppermute | solution.py:64

commit v3 on v2

v3 whole, which is shorter than its diff:
```python
import functools

import jax
import jax.numpy as jnp
from jax import lax
from jax.experimental import pallas as pl
from jax.experimental.pallas import tpu as pltpu
from jax.sharding import PartitionSpec as P

CHUNKS = 8
VMEM_BYTES = 12 * 1024 * 1024


def exchange(partials, axis):
    return lax.all_to_all(partials, axis, 0, 0, tiled=True)


def all_gather(piece, axis):
    return exchange(jnp.broadcast_to(piece[None], (lax.axis_size(axis),) + piece.shape), axis)


def place(places, which, slot):
    return places[0, 0, which, slot]


def degree_kernel(places, counts, tiles, held, out, sems):
    slot_count = tiles.shape[2]
    step = slot_count // CHUNKS
    copies = []
    for chunk in range(CHUNKS):
        span = pl.ds(chunk * step, step)
        copies.append(pltpu.make_async_copy(tiles.at[0, 0, span], held.at[span], sems.at[chunk]))
        copies[-1].start()
    rows, width = out.shape[1:]
    ids = lax.broadcasted_iota(jnp.int32, (rows, width), 0)
    total = jnp.zeros((rows, width), jnp.float32)
    for slot in range(slot_count):
        if slot % step == 0:
            copies[slot // step].wait()
        row = jnp.where(slot < counts[0, 0], place(places, 0, slot), rows)
        hot = jnp.where(ids == row, 1.0, 0.0).astype(jnp.bfloat16)
        total += lax.dot_general(
            hot, held[slot], (((1,), (1,)), ((), ())), preferred_element_type=jnp.float32
        )
    for target in range(out.shape[0]):
        out[target] = total


def first_kernel(halves, places, counts, signal, gathered, held, out, piece, scaled, degree):
    slot_count, width, _ = held.shape
    rows = gathered.shape[1]
    row_index = lax.axis_index("row")
    col_index = lax.axis_index("col")
    total = gathered[0]
    for source in range(1, gathered.shape[0]):
        total += gathered[source]
    degree[...] = total
    piece[...] = degree[pl.ds(col_index, 1), :]
    for tile in range(rows):
        block = signal[:, tile * width : (tile + 1) * width]
        scaled[tile] = (block / degree[tile : tile + 1, :]).astype(jnp.bfloat16)
        for half in range(halves):
            own = row_index == col_index * halves + half
            out[half * rows + tile] = jnp.where(own, block, 0.0)
    for slot in range(slot_count):
        left = scaled[place(places, 0, slot)]
        left = jnp.where(slot < counts[0, 0], left, jnp.zeros_like(left))
        target = place(places, 1, slot)
        out[target] += lax.dot_general(
            left, held[slot], (((1,), (0,)), ((), ())), preferred_element_type=jnp.float32
        )


def second_kernel(places, counts, column, held, out):
    for tile in range(out.shape[0]):
        out[tile] = jnp.zeros(out.shape[1:], jnp.float32)
    for slot in range(held.shape[0]):
        left = column[place(places, 1, slot)]
        left = jnp.where(slot < counts[0, 0], left, jnp.zeros_like(left))
        target = place(places, 0, slot)
        out[target] += lax.dot_general(
            left, held[slot], (((1,), (1,)), ((), ())), preferred_element_type=jnp.float32
        )


def output_kernel(signal, both, first, second, low):
    rows, _, _, width = both.shape
    for tile in range(rows):
        span = slice(tile * width, (tile + 1) * width)
        walked = both[tile, 0]
        lowpass = both[tile, 1]
        first[:, span] = jnp.abs(signal[:, span] - walked)
        second[:, span] = jnp.abs(walked - lowpass)
        low[:, span] = lowpass


def in_vmem():
    return pl.BlockSpec(memory_space=pltpu.VMEM)


def in_smem():
    return pl.BlockSpec(memory_space=pltpu.SMEM)


def on_device(signal, tile_values, tile_places, tile_counts):
    channels, row_len = signal.shape
    slot_count, width = tile_values.shape[2:4]
    rows = row_len // width
    row_size = lax.axis_size("row")
    col_size = lax.axis_size("col")
    halves = row_size // col_size
    params = pltpu.CompilerParams(vmem_limit_bytes=VMEM_BYTES)
    to_column = [
        (row * col_size + col, ((row % halves) * rows + col) * col_size + row // halves)
        for row in range(row_size)
        for col in range(col_size)
    ]
    to_row = [(target, source) for source, target in to_column]

    held, degree_part = pl.pallas_call(
        degree_kernel,
        out_shape=(
            pltpu.VMEM((slot_count, width, width), jnp.bfloat16),
            jax.ShapeDtypeStruct((col_size, rows, width), jnp.float32),
        ),
        in_specs=[in_smem(), in_smem(), pl.BlockSpec(memory_space=pltpu.HBM)],
        out_specs=(in_vmem(), in_vmem()),
        scratch_shapes=[pltpu.SemaphoreType.DMA((CHUNKS,))],
        compiler_params=params,
        name="degree",
    )(tile_places, tile_counts, tile_values)
    gathered = exchange(degree_part, "col")

    partials, degree_piece = pl.pallas_call(
        functools.partial(first_kernel, halves),
        out_shape=(
            jax.ShapeDtypeStruct((halves * rows, channels, width), jnp.float32),
            jax.ShapeDtypeStruct((1, width), jnp.float32),
        ),
        in_specs=[in_smem(), in_smem(), in_vmem(), in_vmem(), in_vmem()],
        out_specs=(in_vmem(), in_vmem()),
        scratch_shapes=[
            pltpu.VMEM((rows, channels, width), jnp.bfloat16),
            pltpu.VMEM((rows, width), jnp.float32),
        ],
        compiler_params=params,
        name="first",
    )(tile_places, tile_counts, signal, gathered, held)
    received = exchange(partials, "row")
    degree_piece = lax.ppermute(degree_piece, ("row", "col"), to_column)
    walked_piece = 0.5 * jnp.sum(received, axis=0)
    scaled = (walked_piece / degree_piece).astype(jnp.bfloat16)

    column = all_gather(scaled, "row").reshape(halves * rows, channels, width)
    walked_piece = lax.ppermute(walked_piece, ("row", "col"), to_row)
    column, walked_piece = lax.optimization_barrier((column, walked_piece))
    partials = pl.pallas_call(
        second_kernel,
        out_shape=jax.ShapeDtypeStruct((rows, channels, width), jnp.float32),
        in_specs=[in_smem(), in_smem(), in_vmem(), in_vmem()],
        out_specs=in_vmem(),
        compiler_params=params,
        name="second",
    )(tile_places, tile_counts, column, held)
    spread = jnp.sum(exchange(partials, "col"), axis=0)
    lowpass_piece = 0.5 * (walked_piece + spread)

    both = all_gather(jnp.stack([walked_piece, lowpass_piece]), "col")
    both = both.reshape(rows, 2, channels, width)
    return pl.pallas_call(
        output_kernel,
        out_shape=(jax.ShapeDtypeStruct((channels, row_len), jnp.float32),) * 3,
        in_specs=[in_vmem(), in_vmem()],
        out_specs=(in_vmem(),) * 3,
        compiler_params=params,
        name="outputs",
    )(signal, both)


def solution(mesh):
    in_specs = (
        P(None, "row"),
        P("row", "col", None, None, None),
        P("row", "col", None, None),
        P("row", "col"),
    )
    out_specs = (P(None, "row"), P(None, "row"), P(None, "row"))
    return jax.shard_map(
        on_device, mesh=mesh, in_specs=in_specs, out_specs=out_specs, check_vma=False
    )
```

time: 119 us -> 106 us (0.89)
  blocking collectives: 21.2 us -> 40.8 us
  starting transfers between devices: 53.8 us -> 34.9 us
  waiting for transfers between devices: 27.4 us -> 17.5 us
  Pallas kernels: 0 us -> 7.91 us
  matrix products: 4.49 us -> 0 us
  local copies, waits for them, and re-layouts: 7.18 us -> 3.06 us
  other arithmetic: 2.45 us -> 0.09 us
    all_to_all x1 -> x3, blocking collectives: 21.2 us -> 40.8 us  [exchange(): return lax.all_to_all(partials, axis, 0, 0, tiled=True)]
    all_to_all x4 -> x2, starting transfers between devices: 37.3 us -> 21.2 us  [exchange(): return lax.all_to_all(partials, axis, 0, 0, tiled=True)]
    all_to_all x4 -> x2, waiting for transfers between devices: 27.4 us -> 16.6 us  [exchange(): return lax.all_to_all(partials, axis, 0, 0, tiled=True)]
    pallas_call x0 -> x4, Pallas kernels: none -> 7.91 us  [the longest x1 3.17 us: on_device(): pl.pallas_call(degree_kernel, out_shape=(pltpu.VMEM((slot_count, width, w...]
    ppermute x2 -> x1, starting transfers between devices: 12.4 us -> 5.14 us  [on_device(): degree_piece = lax.ppermute(degree_piece, ('row', 'col'), to_column)]
    ppermute x1, starting transfers between devices: 4.04 us -> 8.54 us  [on_device(): walked_piece = lax.ppermute(walked_piece, ('row', 'col'), to_row)]
    dot_general x5 -> x0, matrix products: 4.49 us -> none  [the longest x1 1.23 us: on_device(): jnp.einsum('kab,kcb->kca', blocks, picked, preferred_element_type=jnp.flo...]
    reduce_sum x3 -> x1, other arithmetic: 2.28 us -> 0.05 us  [on_device(): walked_piece = 0.5 * jnp.sum(received, axis=0)]
  transfers between devices with their start and end apart: 7 -> 4, of which waited for: 4 -> 3; matrix products, arithmetic and copies ran while one was open for 0% -> 0% of each run, Pallas kernels for 0% -> 0%
where the time goes in v3:
time: 106 us
  blocking collectives  40.8 us (38%)
  starting transfers between devices  34.9 us (33%)
  waiting for transfers between devices  17.5 us (17%)
  Pallas kernels  7.91 us (7%)
  local copies, waits for them, and re-layouts  3.06 us (3%)
  between operations  1.37 us (1%)
    all_to_all x3, blocking collectives, exchange(): return lax.all_to_all(partials, axis, 0, 0, tiled=True)  40.8 us
    all_to_all x2, starting transfers between devices, exchange(): return lax.all_to_all(partials, axis, 0, 0, tiled=True)  21.2 us
    all_to_all x2, waiting for transfers between devices, exchange(): return lax.all_to_all(partials, axis, 0, 0, tiled=True)  16.6 us
    ppermute x1, starting transfers between devices, on_device(): walked_piece = lax.ppermute(walked_piece, ('row', 'col'), to_row)  8.54 us
    ppermute x1, starting transfers between devices, on_device(): degree_piece = lax.ppermute(degree_piece, ('row', 'col'), to_column)  5.14 us
    pallas_call x1, Pallas kernels, on_device(): pl.pallas_call(degree_kernel, out_shape=(pltpu.VMEM((slot_count, width, w...  3.17 us
    unnamed x8, local copies, waits for them, and re-layouts  2.27 us
  transfers between devices with their start and end apart: 4, of which 3 were waited for; matrix products, arithmetic and copies ran while one was open for 0% of the time, Pallas kernels for 0%

profile of v3, /device:TPU:1, one launch (start us, length us, event | category | flops | bytes accessed | tf_op | source)
XLA Modules:
  0.0 105.6 jit_solution(6657878389156340125)
XLA Ops:
  1.3 0.0 copy-start
  1.3 1.6 %copy-done = bf16[1,1,64,128,128]{4,3,2,1,0:T(8,128)(2,1)S(1)} copy-done((bf16[1,1,64,128,128]{4,3,2,1,0:T(8,128)(2,1)S(1)}, bf16[1,1,64,128,128]{4,3,2,1,0:T(8,128)(2,1)}, u32[]{:S(2)}) %copy-start) | copy-done | bytes 2097176
  2.9 0.0 copy-start.2
  2.9 0.7 copy-done.2
  3.5 0.0 copy-start.1
  3.6 3.2 %degree.1 = (bf16[64,128,128]{2,1,0:T(8,128)(2,1)S(1)}, f32[16,16,128]{2,1,0:T(8,128)S(1)}) custom-call(s32[1,1,2,64]{3,2,1,0:T(2,128)S(1)} %copy-done.2, s32[1,1]{1,0:T(1,128)S(6)} %copy.7.counts, bf16[1,1,64,128,128]{4,3,2,1,0:T(8,128)(2,1)S(1)} %copy-done), custom_call_target="tpu_custom_call" | custom-call | tf_op jit(solution)/shard_map/degree/pallas_call | solution.py:120
  6.7 15.5 %all_to_all.25.gathered = f32[16,16,128]{2,1,0:T(8,128)S(1)} all-to-all(f32[16,16,128]{2,1,0:T(8,128)S(1)} %get-tuple-element.9), channel_id=1, replica_groups=mesh['row'=32,'col'=16] {'col'}, dimensions={0} | all-to-all | bytes 262144 | tf_op jit(solution)/shard_map/all_to_all | solution.py:15
  22.2 0.0 copy-done.1
  22.2 0.0 copy-start.3
  22.2 2.1 %first.1 = (f32[32,32,128]{2,1,0:T(8,128)}, f32[1,128]{1,0:T(1,128)S(1)}) custom-call(s32[1,1,2,64]{3,2,1,0:T(2,128)S(1)} %copy-done.2, s32[1,1]{1,0:T(1,128)S(6)} %copy.7.counts, f32[32,2048]{1,0:T(8,128)S(1)} %copy-done.1, f32[16,16,128]{2,1,0:T(8,128)S(1)} %all_to_all.25.gathered, bf16[64,128,128]{2,1,0:T(8,128)(2,1)S(1)} %get-tuple-element.10.held), custom_call_target="tpu_custom_call" | custom-call | tf_op jit(solution)/shard_map/first/pallas_call | solution.py:134
  24.3 12.0 %all-to-all-start.1 = ((f32[32,32,128]{2,1,0:T(8,128)}), f32[32,32,128]{2,1,0:T(8,128)S(1)}, u32[]{:S(2)}, u32[]{:S(2)}) async-start(f32[32,32,128]{2,1,0:T(8,128)} %get-tuple-element.11), calls=%async_computation.1 | async-start | bytes 1048576 | tf_op jit(solution)/shard_map/all_to_all | solution.py:15
  36.4 5.1 %collective-permute-start = (f32[1,128]{1,0:T(1,128)S(1)}, f32[1,128]{1,0:T(1,128)S(1)}, u32[]{:S(2)}, u32[]{:S(2)}) collective-permute-start(f32[1,128]{1,0:T(1,128)S(1)} %get-tuple-element.12), channel_id=1, source_target_pairs={{0,0},{1,16},{2,32},{3,48},{4,64},{5,80},{6,96},{7,112},{8,128},{9... | collective-permute-start | bytes 1544 | tf_op jit(solution)/shard_map/ppermute | solution.py:150
  41.5 12.3 %all-to-all-done.1 = f32[32,32,128]{2,1,0:T(8,128)S(1)} async-done(((f32[32,32,128]{2,1,0:T(8,128)}), f32[32,32,128]{2,1,0:T(8,128)S(1)}, u32[]{:S(2)}, u32[]{:S(2)}) %all-to-all-start.1) | async-done | bytes 524320 | tf_op jit(solution)/shard_map/all_to_all | solution.py:15
  53.9 0.0 collective-permute-done
  53.9 0.7 broadcast_in_dim.4
  54.7 9.2 %all-to-all-start.2 = ((bf16[32,32,128]{2,1,0:T(8,128)(2,1)}), bf16[32,32,128]{2,1,0:T(8,128)(2,1)S(1)}, u32[]{:S(2)}, u32[]{:S(2)}) async-start(bf16[32,32,128]{2,1,0:T(8,128)(2,1)} %broadcast_in_dim.4), calls=%async_computation.2 | async-start | bytes 524288 | tf_op jit(solution)/shard_map/all_to_all | solution.py:15
  63.9 8.5 %collective-permute-start.1 = (f32[32,128]{1,0:T(8,128)S(1)}, f32[32,128]{1,0:T(8,128)S(1)}, u32[]{:S(2)}, u32[]{:S(2)}) collective-permute-start(f32[32,128]{1,0:T(8,128)S(1)} %get-tuple-element.15), channel_id=1, source_target_pairs={{0,0},{16,1},{32,2},{48,3},{64,4},{80,5},{96,6},{112,7},{128,8},{1... | collective-permute-start | bytes 49160 | tf_op jit(solution)/shard_map/ppermute | solution.py:155
  72.4 0.8 collective-permute-done.1
  73.3 4.3 %all-to-all-done.2.column = bf16[32,32,128]{2,1,0:T(8,128)(2,1)S(1)} async-done(((bf16[32,32,128]{2,1,0:T(8,128)(2,1)}), bf16[32,32,128]{2,1,0:T(8,128)(2,1)S(1)}, u32[]{:S(2)}, u32[]{:S(2)}) %all-to-all-start.2) | async-done | bytes 262176 | tf_op jit(solution)/shard_map/all_to_all | solution.py:15
  77.6 0.0 copy-done.3
  77.6 1.7 %second.1 = f32[16,32,128]{2,1,0:T(8,128)S(1)} custom-call(s32[1,1,2,64]{3,2,1,0:T(2,128)S(1)} %copy-done.3, s32[1,1]{1,0:T(1,128)S(6)} %copy.7.counts, bf16[32,32,128]{2,1,0:T(8,128)(2,1)S(1)} %all-to-all-done.2.column, bf16[64,128,128]{2,1,0:T(8,128)(2,1)S(1)} %get-tuple-element.10.held), custom_call_target="tpu_custom_call" | custom-call | tf_op jit(solution)/shard_map/second/pallas_call | solution.py:157
  79.3 12.0 %all_to_all.26 = f32[16,32,128]{2,1,0:T(8,128)S(1)} all-to-all(f32[16,32,128]{2,1,0:T(8,128)S(1)} %second.1), channel_id=1, replica_groups=mesh['row'=32,'col'=16] {'col'}, dimensions={0} | all-to-all | bytes 524288 | tf_op jit(solution)/shard_map/all_to_all | solution.py:15
  91.3 0.1 broadcast_in_dim.5
  91.4 13.3 %all_to_all.27.both = f32[16,2,32,128]{3,2,1,0:T(8,128)S(1)} all-to-all(f32[16,2,32,128]{3,2,1,0:T(8,128)S(1)} %broadcast_in_dim.5), channel_id=1, replica_groups=mesh['row'=32,'col'=16] {'col'}, dimensions={0} | all-to-all | bytes 1048576 | tf_op jit(solution)/shard_map/all_to_all | solution.py:15
  104.7 0.9 outputs.1
  (5 shorter events, 0.1 us)
Async XLA Ops:
  1.3 1.6 %copy-start = (bf16[1,1,64,128,128]{4,3,2,1,0:T(8,128)(2,1)S(1)}, bf16[1,1,64,128,128]{4,3,2,1,0:T(8,128)(2,1)}, u32[]{:S(2)}) copy-start(bf16[1,1,64,128,128]{4,3,2,1,0:T(8,128)(2,1)} %tiles.1) | copy-start | bytes 6291460
  2.9 0.7 copy-start.2
  3.5 18.7 %copy-start.1 = (f32[32,2048]{1,0:T(8,128)S(1)}, f32[32,2048]{1,0:T(8,128)}, u32[]{:S(2)}) copy-start(f32[32,2048]{1,0:T(8,128)} %signal.3) | copy-start | bytes 786436
  22.2 55.3 %copy-start.3 = (s32[1,1,2,64]{3,2,1,0:T(2,128)S(1)}, s32[1,1,2,64]{3,2,1,0:T(2,128)}, u32[]{:S(2)}) copy-start(s32[1,1,2,64]{3,2,1,0:T(2,128)} %places.5) | copy-start | bytes 1540
  24.3 29.6 %all-to-all-start.1 = ((f32[32,32,128]{2,1,0:T(8,128)}), f32[32,32,128]{2,1,0:T(8,128)S(1)}, u32[]{:S(2)}, u32[]{:S(2)}) async-start(f32[32,32,128]{2,1,0:T(8,128)} %get-tuple-element.11), calls=%async_computation.1 | async-start | bytes 1048576 | tf_op jit(solution)/shard_map/all_to_all | solution.py:15
  36.4 17.5 %collective-permute-start = (f32[1,128]{1,0:T(1,128)S(1)}, f32[1,128]{1,0:T(1,128)S(1)}, u32[]{:S(2)}, u32[]{:S(2)}) collective-permute-start(f32[1,128]{1,0:T(1,128)S(1)} %get-tuple-element.12), channel_id=1, source_target_pairs={{0,0},{1,16},{2,32},{3,48},{4,64},{5,80},{6,96},{7,112},{8,128},{9... | collective-permute-start | bytes 1544 | tf_op jit(solution)/shard_map/ppermute | solution.py:150
  54.7 22.9 %all-to-all-start.2 = ((bf16[32,32,128]{2,1,0:T(8,128)(2,1)}), bf16[32,32,128]{2,1,0:T(8,128)(2,1)S(1)}, u32[]{:S(2)}, u32[]{:S(2)}) async-start(bf16[32,32,128]{2,1,0:T(8,128)(2,1)} %broadcast_in_dim.4), calls=%async_computation.2 | async-start | bytes 524288 | tf_op jit(solution)/shard_map/all_to_all | solution.py:15
  63.9 9.4 %collective-permute-start.1 = (f32[32,128]{1,0:T(8,128)S(1)}, f32[32,128]{1,0:T(8,128)S(1)}, u32[]{:S(2)}, u32[]{:S(2)}) collective-permute-start(f32[32,128]{1,0:T(8,128)S(1)} %get-tuple-element.15), channel_id=1, source_target_pairs={{0,0},{16,1},{32,2},{48,3},{64,4},{80,5},{96,6},{112,7},{128,8},{1... | collective-permute-start | bytes 49160 | tf_op jit(solution)/shard_map/ppermute | solution.py:155

commit v4 on v3

--- a/solution.py
+++ b/solution.py
@@ -23,27 +23,33 @@
     return places[0, 0, which, slot]
 
 
-def degree_kernel(places, counts, tiles, held, out, sems):
+def degree_kernel(counts, places_hbm, tiles, held, out, places, sums, small, sems):
     slot_count = tiles.shape[2]
+    copy_places = pltpu.make_async_copy(places_hbm, places, small)
+    copy_places.start()
     step = slot_count // CHUNKS
     copies = []
     for chunk in range(CHUNKS):
         span = pl.ds(chunk * step, step)
         copies.append(pltpu.make_async_copy(tiles.at[0, 0, span], held.at[span], sems.at[chunk]))
         copies[-1].start()
-    rows, width = out.shape[1:]
-    ids = lax.broadcasted_iota(jnp.int32, (rows, width), 0)
-    total = jnp.zeros((rows, width), jnp.float32)
-    for slot in range(slot_count):
-        if slot % step == 0:
-            copies[slot // step].wait()
-        row = jnp.where(slot < counts[0, 0], place(places, 0, slot), rows)
-        hot = jnp.where(ids == row, 1.0, 0.0).astype(jnp.bfloat16)
-        total += lax.dot_general(
-            hot, held[slot], (((1,), (1,)), ((), ())), preferred_element_type=jnp.float32
+    targets, rows, width = out.shape
+    sums[...] = jnp.zeros_like(sums)
+    ones = jnp.ones((8, width), jnp.bfloat16)
+    copy_places.wait()
+    for chunk in range(CHUNKS):
+        copies[chunk].wait()
+        block = held[chunk * step : (chunk + 1) * step].reshape(step * width, width)
+        found = lax.dot_general(
+            ones, block, (((1,), (1,)), ((), ())), preferred_element_type=jnp.float32
         )
-    for target in range(out.shape[0]):
-        out[target] = total
+        for index in range(step):
+            slot = chunk * step + index
+            row = jnp.where(slot < counts[0, 0], place(places, 0, slot), rows)
+            sums[row] += found[:, index * width : (index + 1) * width]
+    for row in range(rows):
+        for target in range(targets):
+            out[target, row : row + 1, :] = sums[row, 0:1, :]
 
 
 def first_kernel(halves, places, counts, signal, gathered, held, out, piece, scaled, degree):
@@ -117,18 +123,27 @@
     ]
     to_row = [(target, source) for source, target in to_column]
 
-    held, degree_part = pl.pallas_call(
+    held, degree_part, places = pl.pallas_call(
         degree_kernel,
         out_shape=(
             pltpu.VMEM((slot_count, width, width), jnp.bfloat16),
             jax.ShapeDtypeStruct((col_size, rows, width), jnp.float32),
+            pltpu.SMEM(tile_places.shape, jnp.int32),
         ),
-        in_specs=[in_smem(), in_smem(), pl.BlockSpec(memory_space=pltpu.HBM)],
-        out_specs=(in_vmem(), in_vmem()),
-        scratch_shapes=[pltpu.SemaphoreType.DMA((CHUNKS,))],
+        in_specs=[in_smem()] + [pl.BlockSpec(memory_space=pltpu.HBM)] * 2,
+        out_specs=(in_vmem(), in_vmem(), in_smem()),
+        scratch_shapes=[
+            pltpu.VMEM((rows + 1, 8, width), jnp.float32),
+            pltpu.SemaphoreType.DMA,
+            pltpu.SemaphoreType.DMA((CHUNKS,)),
+        ],
         compiler_params=params,
         name="degree",
-    )(tile_places, tile_counts, tile_values)
+    )(
+        tile_counts,
+        pltpu.with_memory_space_constraint(tile_places, pltpu.HBM),
+        pltpu.with_memory_space_constraint(tile_values, pltpu.HBM),
+    )
     gathered = exchange(degree_part, "col")
 
     partials, degree_piece = pl.pallas_call(
@@ -145,7 +160,7 @@
         ],
         compiler_params=params,
         name="first",
-    )(tile_places, tile_counts, signal, gathered, held)
+    )(places, tile_counts, signal, gathered, held)
     received = exchange(partials, "row")
     degree_piece = lax.ppermute(degree_piece, ("row", "col"), to_column)
     walked_piece = 0.5 * jnp.sum(received, axis=0)
@@ -161,7 +176,7 @@
         out_specs=in_vmem(),
         compiler_params=params,
         name="second",
-    )(tile_places, tile_counts, column, held)
+    )(places, tile_counts, column, held)
     spread = jnp.sum(exchange(partials, "col"), axis=0)
     lowpass_piece = 0.5 * (walked_piece + spread)
 

time: 106 us -> 102 us (0.962)
  local copies, waits for them, and re-layouts: 3.06 us -> 0.79 us
  Pallas kernels: 7.91 us -> 6.34 us
    unnamed x8 -> x2, local copies, waits for them, and re-layouts: 2.27 us -> 0.01 us
where the time goes in v4:
time: 102 us
  blocking collectives  40.7 us (40%)
  starting transfers between devices  35 us (34%)
  waiting for transfers between devices  17.5 us (17%)
  Pallas kernels  6.34 us (6%)
  between operations  1.41 us (1%)
    all_to_all x3, blocking collectives, exchange(): return lax.all_to_all(partials, axis, 0, 0, tiled=True)  40.7 us
    all_to_all x2, starting transfers between devices, exchange(): return lax.all_to_all(partials, axis, 0, 0, tiled=True)  21.3 us
    all_to_all x2, waiting for transfers between devices, exchange(): return lax.all_to_all(partials, axis, 0, 0, tiled=True)  16.7 us
    ppermute x1, starting transfers between devices, on_device(): walked_piece = lax.ppermute(walked_piece, ('row', 'col'), to_row)  8.54 us
    ppermute x1, starting transfers between devices, on_device(): degree_piece = lax.ppermute(degree_piece, ('row', 'col'), to_column)  5.14 us
    pallas_call x1, Pallas kernels, on_device(): pl.pallas_call(degree_kernel, out_shape=(pltpu.VMEM((slot_count, width, w...  2.69 us
  transfers between devices with their start and end apart: 4, of which 3 were waited for; matrix products, arithmetic and copies ran while one was open for 0% of the time, Pallas kernels for 0%

profile of v4, /device:TPU:1, one launch (start us, length us, event | category | flops | bytes accessed | tf_op | source)
XLA Modules:
  0.0 101.8 jit_solution(16317228449661901865)
XLA Ops:
  0.6 0.0 copy-start
  1.3 2.7 %degree.1 = (bf16[64,128,128]{2,1,0:T(8,128)(2,1)S(1)}, f32[16,16,128]{2,1,0:T(8,128)S(1)}, s32[1,1,2,64]{3,2,1,0:T(2,128)S(4)}) custom-call(s32[1,1]{1,0:T(1,128)S(6)} %copy.7.counts, s32[1,1,2,64]{3,2,1,0:T(2,128)} %places_hbm.1, bf16[1,1,64,128,128]{4,3,2,1,0:T(8,128)(2,1)} %tiles.1), custom_call_target="tpu_custom_call" | custom-call | tf_op jit(solution)/shard_map/degree/pallas_call | solution.py:126
  4.0 15.5 %all_to_all.25.gathered = f32[16,16,128]{2,1,0:T(8,128)S(1)} all-to-all(f32[16,16,128]{2,1,0:T(8,128)S(1)} %get-tuple-element.11), channel_id=1, replica_groups=mesh['row'=32,'col'=16] {'col'}, dimensions={0} | all-to-all | bytes 262144 | tf_op jit(solution)/shard_map/all_to_all | solution.py:15
  19.5 0.0 copy-done
  19.5 1.5 %first.1 = (f32[32,32,128]{2,1,0:T(8,128)}, f32[1,128]{1,0:T(1,128)S(1)}) custom-call(s32[1,1,2,64]{3,2,1,0:T(2,128)S(4)} %get-tuple-element.10.places, s32[1,1]{1,0:T(1,128)S(6)} %copy.7.counts, f32[32,2048]{1,0:T(8,128)S(1)} %copy-done, f32[16,16,128]{2,1,0:T(8,128)S(1)} %all_to_all.25.gathered, bf16[64,128,128]{2,1,0:T(8,128)(2,1)S(1)} %get-tuple-element.12.held), custom_call_target="tpu_custom_call" | custom-call | tf_op jit(solution)/shard_map/first/pallas_call | solution.py:149
  21.0 12.1 %all-to-all-start.1 = ((f32[32,32,128]{2,1,0:T(8,128)}), f32[32,32,128]{2,1,0:T(8,128)S(1)}, u32[]{:S(2)}, u32[]{:S(2)}) async-start(f32[32,32,128]{2,1,0:T(8,128)} %get-tuple-element.13), calls=%async_computation.1 | async-start | bytes 1048576 | tf_op jit(solution)/shard_map/all_to_all | solution.py:15
  33.1 5.1 %collective-permute-start = (f32[1,128]{1,0:T(1,128)S(1)}, f32[1,128]{1,0:T(1,128)S(1)}, u32[]{:S(2)}, u32[]{:S(2)}) collective-permute-start(f32[1,128]{1,0:T(1,128)S(1)} %get-tuple-element.14), channel_id=1, source_target_pairs={{0,0},{1,16},{2,32},{3,48},{4,64},{5,80},{6,96},{7,112},{8,128},{9... | collective-permute-start | bytes 1544 | tf_op jit(solution)/shard_map/ppermute | solution.py:165
  38.3 12.4 %all-to-all-done.1 = f32[32,32,128]{2,1,0:T(8,128)S(1)} async-done(((f32[32,32,128]{2,1,0:T(8,128)}), f32[32,32,128]{2,1,0:T(8,128)S(1)}, u32[]{:S(2)}, u32[]{:S(2)}) %all-to-all-start.1) | async-done | bytes 524320 | tf_op jit(solution)/shard_map/all_to_all | solution.py:15
  50.7 0.0 collective-permute-done
  50.7 0.7 broadcast_in_dim.4
  51.4 9.2 %all-to-all-start.2 = ((bf16[32,32,128]{2,1,0:T(8,128)(2,1)}), bf16[32,32,128]{2,1,0:T(8,128)(2,1)S(1)}, u32[]{:S(2)}, u32[]{:S(2)}) async-start(bf16[32,32,128]{2,1,0:T(8,128)(2,1)} %broadcast_in_dim.4), calls=%async_computation.2 | async-start | bytes 524288 | tf_op jit(solution)/shard_map/all_to_all | solution.py:15
  60.6 8.5 %collective-permute-start.1 = (f32[32,128]{1,0:T(8,128)S(1)}, f32[32,128]{1,0:T(8,128)S(1)}, u32[]{:S(2)}, u32[]{:S(2)}) collective-permute-start(f32[32,128]{1,0:T(8,128)S(1)} %get-tuple-element.17), channel_id=1, source_target_pairs={{0,0},{16,1},{32,2},{48,3},{64,4},{80,5},{96,6},{112,7},{128,8},{1... | collective-permute-start | bytes 49160 | tf_op jit(solution)/shard_map/ppermute | solution.py:170
  69.2 0.8 collective-permute-done.1
  70.0 4.3 %all-to-all-done.2.column = bf16[32,32,128]{2,1,0:T(8,128)(2,1)S(1)} async-done(((bf16[32,32,128]{2,1,0:T(8,128)(2,1)}), bf16[32,32,128]{2,1,0:T(8,128)(2,1)S(1)}, u32[]{:S(2)}, u32[]{:S(2)}) %all-to-all-start.2) | async-done | bytes 262176 | tf_op jit(solution)/shard_map/all_to_all | solution.py:15
  74.3 1.2 %second.1 = f32[16,32,128]{2,1,0:T(8,128)S(1)} custom-call(s32[1,1,2,64]{3,2,1,0:T(2,128)S(4)} %get-tuple-element.10.places, s32[1,1]{1,0:T(1,128)S(6)} %copy.7.counts, bf16[32,32,128]{2,1,0:T(8,128)(2,1)S(1)} %all-to-all-done.2.column, bf16[64,128,128]{2,1,0:T(8,128)(2,1)S(1)} %get-tuple-element.12.held), custom_call_target="tpu_custom_call" | custom-call | tf_op jit(solution)/shard_map/second/pallas_call | solution.py:172
  75.5 12.0 %all_to_all.26 = f32[16,32,128]{2,1,0:T(8,128)S(1)} all-to-all(f32[16,32,128]{2,1,0:T(8,128)S(1)} %second.1), channel_id=1, replica_groups=mesh['row'=32,'col'=16] {'col'}, dimensions={0} | all-to-all | bytes 524288 | tf_op jit(solution)/shard_map/all_to_all | solution.py:15
  87.5 0.1 broadcast_in_dim.5
  87.6 13.3 %all_to_all.27.both = f32[16,2,32,128]{3,2,1,0:T(8,128)S(1)} all-to-all(f32[16,2,32,128]{3,2,1,0:T(8,128)S(1)} %broadcast_in_dim.5), channel_id=1, replica_groups=mesh['row'=32,'col'=16] {'col'}, dimensions={0} | all-to-all | bytes 1048576 | tf_op jit(solution)/shard_map/all_to_all | solution.py:15
  100.9 0.9 outputs.1
  (5 shorter events, 0.1 us)
Async XLA Ops:
  0.6 18.9 %copy-start = (f32[32,2048]{1,0:T(8,128)S(1)}, f32[32,2048]{1,0:T(8,128)}, u32[]{:S(2)}) copy-start(f32[32,2048]{1,0:T(8,128)} %signal.3) | copy-start | bytes 786436
  21.0 29.6 %all-to-all-start.1 = ((f32[32,32,128]{2,1,0:T(8,128)}), f32[32,32,128]{2,1,0:T(8,128)S(1)}, u32[]{:S(2)}, u32[]{:S(2)}) async-start(f32[32,32,128]{2,1,0:T(8,128)} %get-tuple-element.13), calls=%async_computation.1 | async-start | bytes 1048576 | tf_op jit(solution)/shard_map/all_to_all | solution.py:15
  33.1 17.6 %collective-permute-start = (f32[1,128]{1,0:T(1,128)S(1)}, f32[1,128]{1,0:T(1,128)S(1)}, u32[]{:S(2)}, u32[]{:S(2)}) collective-permute-start(f32[1,128]{1,0:T(1,128)S(1)} %get-tuple-element.14), channel_id=1, source_target_pairs={{0,0},{1,16},{2,32},{3,48},{4,64},{5,80},{6,96},{7,112},{8,128},{9... | collective-permute-start | bytes 1544 | tf_op jit(solution)/shard_map/ppermute | solution.py:165
  51.4 22.9 %all-to-all-start.2 = ((bf16[32,32,128]{2,1,0:T(8,128)(2,1)}), bf16[32,32,128]{2,1,0:T(8,128)(2,1)S(1)}, u32[]{:S(2)}, u32[]{:S(2)}) async-start(bf16[32,32,128]{2,1,0:T(8,128)(2,1)} %broadcast_in_dim.4), calls=%async_computation.2 | async-start | bytes 524288 | tf_op jit(solution)/shard_map/all_to_all | solution.py:15
  60.6 9.4 %collective-permute-start.1 = (f32[32,128]{1,0:T(8,128)S(1)}, f32[32,128]{1,0:T(8,128)S(1)}, u32[]{:S(2)}, u32[]{:S(2)}) collective-permute-start(f32[32,128]{1,0:T(8,128)S(1)} %get-tuple-element.17), channel_id=1, source_target_pairs={{0,0},{16,1},{32,2},{48,3},{64,4},{80,5},{96,6},{112,7},{128,8},{1... | collective-permute-start | bytes 49160 | tf_op jit(solution)/shard_map/ppermute | solution.py:170

commit v5 on v4

--- a/solution.py
+++ b/solution.py
@@ -168,7 +168,6 @@
 
     column = all_gather(scaled, "row").reshape(halves * rows, channels, width)
     walked_piece = lax.ppermute(walked_piece, ("row", "col"), to_row)
-    column, walked_piece = lax.optimization_barrier((column, walked_piece))
     partials = pl.pallas_call(
         second_kernel,
         out_shape=jax.ShapeDtypeStruct((rows, channels, width), jnp.float32),
@@ -177,6 +176,7 @@
         compiler_params=params,
         name="second",
     )(places, tile_counts, column, held)
+    partials, walked_piece = lax.optimization_barrier((partials, walked_piece))
     spread = jnp.sum(exchange(partials, "col"), axis=0)
     lowpass_piece = 0.5 * (walked_piece + spread)
 

time: 102 us -> 101 us (level)
  transfers between devices with their start and end apart: 4 -> 4, of which waited for: 3 -> 2; matrix products, arithmetic and copies ran while one was open for 0% -> 0% of each run, Pallas kernels for 0% -> 1%
where the time goes in v5:
time: 101 us
  blocking collectives  39.8 us (39%)
  starting transfers between devices  35 us (35%)
  waiting for transfers between devices  17.5 us (17%)
  Pallas kernels  6.33 us (6%)
  between operations  1.42 us (1%)
    all_to_all x3, blocking collectives, exchange(): return lax.all_to_all(partials, axis, 0, 0, tiled=True)  39.8 us
    all_to_all x2, starting transfers between devices, exchange(): return lax.all_to_all(partials, axis, 0, 0, tiled=True)  21.3 us
    all_to_all x2, waiting for transfers between devices, exchange(): return lax.all_to_all(partials, axis, 0, 0, tiled=True)  17.5 us
    ppermute x1, starting transfers between devices, on_device(): walked_piece = lax.ppermute(walked_piece, ('row', 'col'), to_row)  8.54 us
    ppermute x1, starting transfers between devices, on_device(): degree_piece = lax.ppermute(degree_piece, ('row', 'col'), to_column)  5.14 us
    pallas_call x1, Pallas kernels, on_device(): pl.pallas_call(degree_kernel, out_shape=(pltpu.VMEM((slot_count, width, w...  2.69 us
  transfers between devices with their start and end apart: 4, of which 2 were waited for; matrix products, arithmetic and copies ran while one was open for 0% of the time, Pallas kernels for 1%

profile of v5, /device:TPU:1, one launch (start us, length us, event | category | flops | bytes accessed | tf_op | source)
XLA Modules:
  0.0 100.9 jit_solution(2392003958957224505)
XLA Ops:
  0.6 0.0 copy-start
  1.3 2.7 %degree.1 = (bf16[64,128,128]{2,1,0:T(8,128)(2,1)S(1)}, f32[16,16,128]{2,1,0:T(8,128)S(1)}, s32[1,1,2,64]{3,2,1,0:T(2,128)S(4)}) custom-call(s32[1,1]{1,0:T(1,128)S(6)} %copy.7.counts, s32[1,1,2,64]{3,2,1,0:T(2,128)} %places_hbm.1, bf16[1,1,64,128,128]{4,3,2,1,0:T(8,128)(2,1)} %tiles.1), custom_call_target="tpu_custom_call" | custom-call | tf_op jit(solution)/shard_map/degree/pallas_call | solution.py:126
  4.0 15.5 %all_to_all.25.gathered = f32[16,16,128]{2,1,0:T(8,128)S(1)} all-to-all(f32[16,16,128]{2,1,0:T(8,128)S(1)} %get-tuple-element.11), channel_id=1, replica_groups=mesh['row'=32,'col'=16] {'col'}, dimensions={0} | all-to-all | bytes 262144 | tf_op jit(solution)/shard_map/all_to_all | solution.py:15
  19.5 0.0 copy-done
  19.5 1.5 %first.1 = (f32[32,32,128]{2,1,0:T(8,128)}, f32[1,128]{1,0:T(1,128)S(1)}) custom-call(s32[1,1,2,64]{3,2,1,0:T(2,128)S(4)} %get-tuple-element.10.places, s32[1,1]{1,0:T(1,128)S(6)} %copy.7.counts, f32[32,2048]{1,0:T(8,128)S(1)} %copy-done, f32[16,16,128]{2,1,0:T(8,128)S(1)} %all_to_all.25.gathered, bf16[64,128,128]{2,1,0:T(8,128)(2,1)S(1)} %get-tuple-element.12.held), custom_call_target="tpu_custom_call" | custom-call | tf_op jit(solution)/shard_map/first/pallas_call | solution.py:149
  21.0 12.1 %all-to-all-start.1 = ((f32[32,32,128]{2,1,0:T(8,128)}), f32[32,32,128]{2,1,0:T(8,128)S(1)}, u32[]{:S(2)}, u32[]{:S(2)}) async-start(f32[32,32,128]{2,1,0:T(8,128)} %get-tuple-element.13), calls=%async_computation.1 | async-start | bytes 1048576 | tf_op jit(solution)/shard_map/all_to_all | solution.py:15
  33.1 5.1 %collective-permute-start = (f32[1,128]{1,0:T(1,128)S(1)}, f32[1,128]{1,0:T(1,128)S(1)}, u32[]{:S(2)}, u32[]{:S(2)}) collective-permute-start(f32[1,128]{1,0:T(1,128)S(1)} %get-tuple-element.14), channel_id=1, source_target_pairs={{0,0},{1,16},{2,32},{3,48},{4,64},{5,80},{6,96},{7,112},{8,128},{9... | collective-permute-start | bytes 1544 | tf_op jit(solution)/shard_map/ppermute | solution.py:165
  38.3 12.3 %all-to-all-done.1 = f32[32,32,128]{2,1,0:T(8,128)S(1)} async-done(((f32[32,32,128]{2,1,0:T(8,128)}), f32[32,32,128]{2,1,0:T(8,128)S(1)}, u32[]{:S(2)}, u32[]{:S(2)}) %all-to-all-start.1) | async-done | bytes 524320 | tf_op jit(solution)/shard_map/all_to_all | solution.py:15
  50.6 0.0 collective-permute-done
  50.6 0.7 broadcast_in_dim.4
  51.4 9.2 %all-to-all-start.2 = ((bf16[32,32,128]{2,1,0:T(8,128)(2,1)}), bf16[32,32,128]{2,1,0:T(8,128)(2,1)S(1)}, u32[]{:S(2)}, u32[]{:S(2)}) async-start(bf16[32,32,128]{2,1,0:T(8,128)(2,1)} %broadcast_in_dim.4), calls=%async_computation.2 | async-start | bytes 524288 | tf_op jit(solution)/shard_map/all_to_all | solution.py:15
  60.6 8.5 %collective-permute-start.1 = (f32[32,128]{1,0:T(8,128)S(1)}, f32[32,128]{1,0:T(8,128)S(1)}, u32[]{:S(2)}, u32[]{:S(2)}) collective-permute-start(f32[32,128]{1,0:T(8,128)S(1)} %get-tuple-element.17), channel_id=1, source_target_pairs={{0,0},{16,1},{32,2},{48,3},{64,4},{80,5},{96,6},{112,7},{128,8},{1... | collective-permute-start | bytes 49160 | tf_op jit(solution)/shard_map/ppermute | solution.py:170
  69.2 5.1 %all-to-all-done.2.column = bf16[32,32,128]{2,1,0:T(8,128)(2,1)S(1)} async-done(((bf16[32,32,128]{2,1,0:T(8,128)(2,1)}), bf16[32,32,128]{2,1,0:T(8,128)(2,1)S(1)}, u32[]{:S(2)}, u32[]{:S(2)}) %all-to-all-start.2) | async-done | bytes 262176 | tf_op jit(solution)/shard_map/all_to_all | solution.py:15
  74.3 1.2 %second.1 = f32[16,32,128]{2,1,0:T(8,128)S(1)} custom-call(s32[1,1,2,64]{3,2,1,0:T(2,128)S(4)} %get-tuple-element.10.places, s32[1,1]{1,0:T(1,128)S(6)} %copy.7.counts, bf16[32,32,128]{2,1,0:T(8,128)(2,1)S(1)} %all-to-all-done.2.column, bf16[64,128,128]{2,1,0:T(8,128)(2,1)S(1)} %get-tuple-element.12.held), custom_call_target="tpu_custom_call" | custom-call | tf_op jit(solution)/shard_map/second/pallas_call | solution.py:171
  75.5 0.0 collective-permute-done.1
  75.5 11.0 %all_to_all.26 = f32[16,32,128]{2,1,0:T(8,128)S(1)} all-to-all(f32[16,32,128]{2,1,0:T(8,128)S(1)} %second.1), channel_id=1, replica_groups=mesh['row'=32,'col'=16] {'col'}, dimensions={0} | all-to-all | bytes 524288 | tf_op jit(solution)/shard_map/all_to_all | solution.py:15
  86.6 0.1 broadcast_in_dim.5
  86.6 13.3 %all_to_all.27.both = f32[16,2,32,128]{3,2,1,0:T(8,128)S(1)} all-to-all(f32[16,2,32,128]{3,2,1,0:T(8,128)S(1)} %broadcast_in_dim.5), channel_id=1, replica_groups=mesh['row'=32,'col'=16] {'col'}, dimensions={0} | all-to-all | bytes 1048576 | tf_op jit(solution)/shard_map/all_to_all | solution.py:15
  99.9 0.9 outputs.1
  (5 shorter events, 0.1 us)
Async XLA Ops:
  0.6 18.9 %copy-start = (f32[32,2048]{1,0:T(8,128)S(1)}, f32[32,2048]{1,0:T(8,128)}, u32[]{:S(2)}) copy-start(f32[32,2048]{1,0:T(8,128)} %signal.3) | copy-start | bytes 786436
  21.0 29.6 %all-to-all-start.1 = ((f32[32,32,128]{2,1,0:T(8,128)}), f32[32,32,128]{2,1,0:T(8,128)S(1)}, u32[]{:S(2)}, u32[]{:S(2)}) async-start(f32[32,32,128]{2,1,0:T(8,128)} %get-tuple-element.13), calls=%async_computation.1 | async-start | bytes 1048576 | tf_op jit(solution)/shard_map/all_to_all | solution.py:15
  33.1 17.5 %collective-permute-start = (f32[1,128]{1,0:T(1,128)S(1)}, f32[1,128]{1,0:T(1,128)S(1)}, u32[]{:S(2)}, u32[]{:S(2)}) collective-permute-start(f32[1,128]{1,0:T(1,128)S(1)} %get-tuple-element.14), channel_id=1, source_target_pairs={{0,0},{1,16},{2,32},{3,48},{4,64},{5,80},{6,96},{7,112},{8,128},{9... | collective-permute-start | bytes 1544 | tf_op jit(solution)/shard_map/ppermute | solution.py:165
  51.4 22.9 %all-to-all-start.2 = ((bf16[32,32,128]{2,1,0:T(8,128)(2,1)}), bf16[32,32,128]{2,1,0:T(8,128)(2,1)S(1)}, u32[]{:S(2)}, u32[]{:S(2)}) async-start(bf16[32,32,128]{2,1,0:T(8,128)(2,1)} %broadcast_in_dim.4), calls=%async_computation.2 | async-start | bytes 524288 | tf_op jit(solution)/shard_map/all_to_all | solution.py:15
  60.6 14.9 %collective-permute-start.1 = (f32[32,128]{1,0:T(8,128)S(1)}, f32[32,128]{1,0:T(8,128)S(1)}, u32[]{:S(2)}, u32[]{:S(2)}) collective-permute-start(f32[32,128]{1,0:T(8,128)S(1)} %get-tuple-element.17), channel_id=1, source_target_pairs={{0,0},{16,1},{32,2},{48,3},{64,4},{80,5},{96,6},{112,7},{128,8},{1... | collective-permute-start | bytes 49160 | tf_op jit(solution)/shard_map/ppermute | solution.py:170

commit v6 on v5

--- a/solution.py
+++ b/solution.py
@@ -8,6 +8,7 @@
 from jax.sharding import PartitionSpec as P
 
 CHUNKS = 8
+PARTS = 4
 VMEM_BYTES = 12 * 1024 * 1024
 
 
@@ -48,8 +49,10 @@
             row = jnp.where(slot < counts[0, 0], place(places, 0, slot), rows)
             sums[row] += found[:, index * width : (index + 1) * width]
     for row in range(rows):
-        for target in range(targets):
-            out[target, row : row + 1, :] = sums[row, 0:1, :]
+        out[0, row : row + 1, :] = sums[row, 0:1, :]
+    total = out[0]
+    for target in range(1, targets):
+        out[target] = total
 
 
 def first_kernel(halves, places, counts, signal, gathered, held, out, piece, scaled, degree):
@@ -89,15 +92,37 @@
         )
 
 
-def output_kernel(signal, both, first, second, low):
+def middle_kernel(received, degree, walked, copies):
+    total = received[0]
+    for source in range(1, received.shape[0]):
+        total += received[source]
+    total = 0.5 * total
+    walked[...] = total
+    scaled = (total / degree[...]).astype(jnp.bfloat16)
+    for target in range(copies.shape[0]):
+        copies[target] = scaled
+
+
+def output_kernel(signal, both, first, second, low, held, sems):
     rows, _, _, width = both.shape
-    for tile in range(rows):
-        span = slice(tile * width, (tile + 1) * width)
-        walked = both[tile, 0]
-        lowpass = both[tile, 1]
-        first[:, span] = jnp.abs(signal[:, span] - walked)
-        second[:, span] = jnp.abs(walked - lowpass)
-        low[:, span] = lowpass
+    step = rows // PARTS
+    copies = []
+    for part in range(PARTS):
+        for tile in range(part * step, (part + 1) * step):
+            span = slice(tile * width, (tile + 1) * width)
+            walked = both[tile, 0]
+            lowpass = both[tile, 1]
+            held[0, :, span] = jnp.abs(signal[:, span] - walked)
+            held[1, :, span] = jnp.abs(walked - lowpass)
+            held[2, :, span] = lowpass
+        span = pl.ds(part * step * width, step * width)
+        for index, target in enumerate((first, second, low)):
+            copies.append(
+                pltpu.make_async_copy(held.at[index, :, span], target.at[:, span], sems.at[part, index])
+            )
+            copies[-1].start()
+    for copy in copies:
+        copy.wait()
 
 
 def in_vmem():
@@ -163,10 +188,19 @@
     )(places, tile_counts, signal, gathered, held)
     received = exchange(partials, "row")
     degree_piece = lax.ppermute(degree_piece, ("row", "col"), to_column)
-    walked_piece = 0.5 * jnp.sum(received, axis=0)
-    scaled = (walked_piece / degree_piece).astype(jnp.bfloat16)
-
-    column = all_gather(scaled, "row").reshape(halves * rows, channels, width)
+    walked_piece, scaled = pl.pallas_call(
+        middle_kernel,
+        out_shape=(
+            jax.ShapeDtypeStruct((channels, width), jnp.float32),
+            jax.ShapeDtypeStruct((row_size, channels, width), jnp.bfloat16),
+        ),
+        in_specs=[in_vmem(), in_vmem()],
+        out_specs=(in_vmem(), in_vmem()),
+        compiler_params=params,
+        name="middle",
+    )(received, degree_piece)
+
+    column = exchange(scaled, "row")
     walked_piece = lax.ppermute(walked_piece, ("row", "col"), to_row)
     partials = pl.pallas_call(
         second_kernel,
@@ -186,7 +220,11 @@
         output_kernel,
         out_shape=(jax.ShapeDtypeStruct((channels, row_len), jnp.float32),) * 3,
         in_specs=[in_vmem(), in_vmem()],
-        out_specs=(in_vmem(),) * 3,
+        out_specs=(pl.BlockSpec(memory_space=pltpu.HBM),) * 3,
+        scratch_shapes=[
+            pltpu.VMEM((3, channels, row_len), jnp.float32),
+            pltpu.SemaphoreType.DMA((PARTS, 3)),
+        ],
         compiler_params=params,
         name="outputs",
     )(signal, both)

time: 101 us -> 101 us (level)
    ppermute x1, waiting for transfers between devices: 0.01 us -> 11.8 us  [on_device(): degree_piece = lax.ppermute(degree_piece, ('row', 'col'), to_column)]
    all_to_all x2, waiting for transfers between devices: 17.5 us -> 5.66 us  [exchange(): return lax.all_to_all(partials, axis, 0, 0, tiled=True)]
  transfers between devices with their start and end apart: 4 -> 4, of which waited for: 2 -> 3; matrix products, arithmetic and copies ran while one was open for 0% -> 0% of each run, Pallas kernels for 1% -> 1%
where the time goes in v6:
time: 101 us
  blocking collectives  39.8 us (39%)
  starting transfers between devices  35 us (35%)
  waiting for transfers between devices  17.5 us (17%)
  Pallas kernels  7.1 us (7%)
  between operations  1.41 us (1%)
    all_to_all x3, blocking collectives, exchange(): return lax.all_to_all(partials, axis, 0, 0, tiled=True)  39.8 us
    all_to_all x2, starting transfers between devices, exchange(): return lax.all_to_all(partials, axis, 0, 0, tiled=True)  21.4 us
    ppermute x1, waiting for transfers between devices, on_device(): degree_piece = lax.ppermute(degree_piece, ('row', 'col'), to_column)  11.8 us
    ppermute x1, starting transfers between devices, on_device(): walked_piece = lax.ppermute(walked_piece, ('row', 'col'), to_row)  8.54 us
    all_to_all x2, waiting for transfers between devices, exchange(): return lax.all_to_all(partials, axis, 0, 0, tiled=True)  5.66 us
    ppermute x1, starting transfers between devices, on_device(): degree_piece = lax.ppermute(degree_piece, ('row', 'col'), to_column)  5.13 us
    pallas_call x1, Pallas kernels, on_device(): pl.pallas_call(degree_kernel, out_shape=(pltpu.VMEM((slot_count, width, w...  2.65 us
  transfers between devices with their start and end apart: 4, of which 3 were waited for; matrix products, arithmetic and copies ran while one was open for 0% of the time, Pallas kernels for 1%

profile of v6, /device:TPU:1, one launch (start us, length us, event | category | flops | bytes accessed | tf_op | source)
XLA Modules:
  0.0 100.9 jit_solution(9403320481321013013)
XLA Ops:
  0.6 0.0 copy-start
  1.3 2.7 %degree.1 = (bf16[64,128,128]{2,1,0:T(8,128)(2,1)S(1)}, f32[16,16,128]{2,1,0:T(8,128)S(1)}, s32[1,1,2,64]{3,2,1,0:T(2,128)S(4)}) custom-call(s32[1,1]{1,0:T(1,128)S(6)} %copy.7.counts, s32[1,1,2,64]{3,2,1,0:T(2,128)} %places_hbm.1, bf16[1,1,64,128,128]{4,3,2,1,0:T(8,128)(2,1)} %tiles.1), custom_call_target="tpu_custom_call" | custom-call | tf_op jit(solution)/shard_map/degree/pallas_call | solution.py:151
  4.0 15.4 %all_to_all.25.gathered = f32[16,16,128]{2,1,0:T(8,128)S(1)} all-to-all(f32[16,16,128]{2,1,0:T(8,128)S(1)} %get-tuple-element.13), channel_id=1, replica_groups=mesh['row'=32,'col'=16] {'col'}, dimensions={0} | all-to-all | bytes 262144 | tf_op jit(solution)/shard_map/all_to_all | solution.py:16
  19.4 0.0 copy-done
  19.4 1.5 %first.1 = (f32[32,32,128]{2,1,0:T(8,128)}, f32[1,128]{1,0:T(1,128)S(1)}) custom-call(s32[1,1,2,64]{3,2,1,0:T(2,128)S(4)} %get-tuple-element.12.places, s32[1,1]{1,0:T(1,128)S(6)} %copy.7.counts, f32[32,2048]{1,0:T(8,128)S(1)} %copy-done, f32[16,16,128]{2,1,0:T(8,128)S(1)} %all_to_all.25.gathered, bf16[64,128,128]{2,1,0:T(8,128)(2,1)S(1)} %get-tuple-element.14.held), custom_call_target="tpu_custom_call" | custom-call | tf_op jit(solution)/shard_map/first/pallas_call | solution.py:174
  20.9 12.1 %all-to-all-start.1 = ((f32[32,32,128]{2,1,0:T(8,128)}), f32[32,32,128]{2,1,0:T(8,128)S(1)}, u32[]{:S(2)}, u32[]{:S(2)}) async-start(f32[32,32,128]{2,1,0:T(8,128)} %get-tuple-element.15), calls=%async_computation.1 | async-start | bytes 1048576 | tf_op jit(solution)/shard_map/all_to_all | solution.py:16
  33.1 5.1 %collective-permute-start = (f32[1,128]{1,0:T(1,128)S(1)}, f32[1,128]{1,0:T(1,128)S(1)}, u32[]{:S(2)}, u32[]{:S(2)}) collective-permute-start(f32[1,128]{1,0:T(1,128)S(1)} %get-tuple-element.16), channel_id=1, source_target_pairs={{0,0},{1,16},{2,32},{3,48},{4,64},{5,80},{6,96},{7,112},{8,128},{9... | collective-permute-start | bytes 1544 | tf_op jit(solution)/shard_map/ppermute | solution.py:190
  38.2 11.8 %collective-permute-done.degree = f32[1,128]{1,0:T(1,128)S(1)} collective-permute-done((f32[1,128]{1,0:T(1,128)S(1)}, f32[1,128]{1,0:T(1,128)S(1)}, u32[]{:S(2)}, u32[]{:S(2)}) %collective-permute-start) | collective-permute-done | bytes 544 | tf_op jit(solution)/shard_map/ppermute | solution.py:190
  50.1 0.5 all-to-all-done.1.received
  50.6 0.8 middle.1
  51.3 9.3 %all-to-all-start.2 = ((bf16[32,32,128]{2,1,0:T(8,128)(2,1)}), bf16[32,32,128]{2,1,0:T(8,128)(2,1)S(1)}, u32[]{:S(2)}, u32[]{:S(2)}) async-start(bf16[32,32,128]{2,1,0:T(8,128)(2,1)} %get-tuple-element.17), calls=%async_computation.2 | async-start | bytes 524288 | tf_op jit(solution)/shard_map/all_to_all | solution.py:16
  60.6 8.5 %collective-permute-start.1 = (f32[32,128]{1,0:T(8,128)S(1)}, f32[32,128]{1,0:T(8,128)S(1)}, u32[]{:S(2)}, u32[]{:S(2)}) collective-permute-start(f32[32,128]{1,0:T(8,128)S(1)} %get-tuple-element.18), channel_id=1, source_target_pairs={{0,0},{16,1},{32,2},{48,3},{64,4},{80,5},{96,6},{112,7},{128,8},{1... | collective-permute-start | bytes 49160 | tf_op jit(solution)/shard_map/ppermute | solution.py:204
  69.1 5.2 %all-to-all-done.2.column = bf16[32,32,128]{2,1,0:T(8,128)(2,1)S(1)} async-done(((bf16[32,32,128]{2,1,0:T(8,128)(2,1)}), bf16[32,32,128]{2,1,0:T(8,128)(2,1)S(1)}, u32[]{:S(2)}, u32[]{:S(2)}) %all-to-all-start.2) | async-done | bytes 262176 | tf_op jit(solution)/shard_map/all_to_all | solution.py:16
  74.3 1.2 %second.1 = f32[16,32,128]{2,1,0:T(8,128)S(1)} custom-call(s32[1,1,2,64]{3,2,1,0:T(2,128)S(4)} %get-tuple-element.12.places, s32[1,1]{1,0:T(1,128)S(6)} %copy.7.counts, bf16[32,32,128]{2,1,0:T(8,128)(2,1)S(1)} %all-to-all-done.2.column, bf16[64,128,128]{2,1,0:T(8,128)(2,1)S(1)} %get-tuple-element.14.held), custom_call_target="tpu_custom_call" | custom-call | tf_op jit(solution)/shard_map/second/pallas_call | solution.py:205
  75.5 0.0 collective-permute-done.1
  75.5 11.0 %all_to_all.26 = f32[16,32,128]{2,1,0:T(8,128)S(1)} all-to-all(f32[16,32,128]{2,1,0:T(8,128)S(1)} %second.1), channel_id=1, replica_groups=mesh['row'=32,'col'=16] {'col'}, dimensions={0} | all-to-all | bytes 524288 | tf_op jit(solution)/shard_map/all_to_all | solution.py:16
  86.6 0.1 broadcast_in_dim.2
  86.6 13.3 %all_to_all.27.both = f32[16,2,32,128]{3,2,1,0:T(8,128)S(1)} all-to-all(f32[16,2,32,128]{3,2,1,0:T(8,128)S(1)} %broadcast_in_dim.2), channel_id=1, replica_groups=mesh['row'=32,'col'=16] {'col'}, dimensions={0} | all-to-all | bytes 1048576 | tf_op jit(solution)/shard_map/all_to_all | solution.py:16
  99.9 1.0 outputs.1
  (3 shorter events, 0.0 us)
Async XLA Ops:
  0.6 18.8 %copy-start = (f32[32,2048]{1,0:T(8,128)S(1)}, f32[32,2048]{1,0:T(8,128)}, u32[]{:S(2)}) copy-start(f32[32,2048]{1,0:T(8,128)} %signal.3) | copy-start | bytes 786436
  20.9 29.6 %all-to-all-start.1 = ((f32[32,32,128]{2,1,0:T(8,128)}), f32[32,32,128]{2,1,0:T(8,128)S(1)}, u32[]{:S(2)}, u32[]{:S(2)}) async-start(f32[32,32,128]{2,1,0:T(8,128)} %get-tuple-element.15), calls=%async_computation.1 | async-start | bytes 1048576 | tf_op jit(solution)/shard_map/all_to_all | solution.py:16
  33.1 17.0 %collective-permute-start = (f32[1,128]{1,0:T(1,128)S(1)}, f32[1,128]{1,0:T(1,128)S(1)}, u32[]{:S(2)}, u32[]{:S(2)}) collective-permute-start(f32[1,128]{1,0:T(1,128)S(1)} %get-tuple-element.16), channel_id=1, source_target_pairs={{0,0},{1,16},{2,32},{3,48},{4,64},{5,80},{6,96},{7,112},{8,128},{9... | collective-permute-start | bytes 1544 | tf_op jit(solution)/shard_map/ppermute | solution.py:190
  51.3 23.0 %all-to-all-start.2 = ((bf16[32,32,128]{2,1,0:T(8,128)(2,1)}), bf16[32,32,128]{2,1,0:T(8,128)(2,1)S(1)}, u32[]{:S(2)}, u32[]{:S(2)}) async-start(bf16[32,32,128]{2,1,0:T(8,128)(2,1)} %get-tuple-element.17), calls=%async_computation.2 | async-start | bytes 524288 | tf_op jit(solution)/shard_map/all_to_all | solution.py:16
  60.6 14.9 %collective-permute-start.1 = (f32[32,128]{1,0:T(8,128)S(1)}, f32[32,128]{1,0:T(8,128)S(1)}, u32[]{:S(2)}, u32[]{:S(2)}) collective-permute-start(f32[32,128]{1,0:T(8,128)S(1)} %get-tuple-element.18), channel_id=1, source_target_pairs={{0,0},{16,1},{32,2},{48,3},{64,4},{80,5},{96,6},{112,7},{128,8},{1... | collective-permute-start | bytes 49160 | tf_op jit(solution)/shard_map/ppermute | solution.py:204

commit v7 on v5

--- a/solution.py
+++ b/solution.py
@@ -52,29 +52,50 @@
             out[target, row : row + 1, :] = sums[row, 0:1, :]
 
 
-def first_kernel(halves, places, counts, signal, gathered, held, out, piece, scaled, degree):
+def first_kernel(halves, places, counts, signal, gathered, held, out, scaled, degree, sums):
     slot_count, width, _ = held.shape
     rows = gathered.shape[1]
+    channels = signal.shape[0]
     row_index = lax.axis_index("row")
     col_index = lax.axis_index("col")
     total = gathered[0]
     for source in range(1, gathered.shape[0]):
         total += gathered[source]
     degree[...] = total
-    piece[...] = degree[pl.ds(col_index, 1), :]
     for tile in range(rows):
         block = signal[:, tile * width : (tile + 1) * width]
-        scaled[tile] = (block / degree[tile : tile + 1, :]).astype(jnp.bfloat16)
+        nodes = degree[tile : tile + 1, :]
+        scaled[tile] = (block / nodes).astype(jnp.bfloat16)
         for half in range(halves):
             own = row_index == col_index * halves + half
-            out[half * rows + tile] = jnp.where(own, block, 0.0)
+            sums[half * rows + tile] = jnp.where(own, block, 0.0)
+            out[half * rows + tile, channels] = jnp.where(own, nodes, 0.0)
     for slot in range(slot_count):
         left = scaled[place(places, 0, slot)]
         left = jnp.where(slot < counts[0, 0], left, jnp.zeros_like(left))
         target = place(places, 1, slot)
-        out[target] += lax.dot_general(
+        sums[target] += lax.dot_general(
             left, held[slot], (((1,), (0,)), ((), ())), preferred_element_type=jnp.float32
         )
+    for tile in range(halves * rows):
+        for channel in range(channels):
+            out[tile, channel] = sums[tile, channel : channel + 1, :]
+
+
+def middle_kernel(received, walked, copies):
+    sources, channels = received.shape[0], received.shape[1] - 1
+
+    def summed(channel):
+        total = received[0, channel]
+        for source in range(1, sources):
+            total += received[source, channel]
+        return total
+
+    for channel in range(channels):
+        walked[channel : channel + 1, :] = 0.5 * summed(channel)
+    scaled = (walked[...] / summed(channels)).astype(jnp.bfloat16)
+    for target in range(copies.shape[0]):
+        copies[target] = scaled
 
 
 def second_kernel(places, counts, column, held, out):
@@ -116,12 +137,11 @@
     col_size = lax.axis_size("col")
     halves = row_size // col_size
     params = pltpu.CompilerParams(vmem_limit_bytes=VMEM_BYTES)
-    to_column = [
-        (row * col_size + col, ((row % halves) * rows + col) * col_size + row // halves)
+    to_row = [
+        (((row % halves) * rows + col) * col_size + row // halves, row * col_size + col)
         for row in range(row_size)
         for col in range(col_size)
     ]
-    to_row = [(target, source) for source, target in to_column]
 
     held, degree_part, places = pl.pallas_call(
         degree_kernel,
@@ -146,27 +166,32 @@
     )
     gathered = exchange(degree_part, "col")
 
-    partials, degree_piece = pl.pallas_call(
+    partials = pl.pallas_call(
         functools.partial(first_kernel, halves),
-        out_shape=(
-            jax.ShapeDtypeStruct((halves * rows, channels, width), jnp.float32),
-            jax.ShapeDtypeStruct((1, width), jnp.float32),
-        ),
+        out_shape=jax.ShapeDtypeStruct((halves * rows, channels + 1, 1, width), jnp.float32),
         in_specs=[in_smem(), in_smem(), in_vmem(), in_vmem(), in_vmem()],
-        out_specs=(in_vmem(), in_vmem()),
+        out_specs=in_vmem(),
         scratch_shapes=[
             pltpu.VMEM((rows, channels, width), jnp.bfloat16),
             pltpu.VMEM((rows, width), jnp.float32),
+            pltpu.VMEM((halves * rows, channels, width), jnp.float32),
         ],
         compiler_params=params,
         name="first",
     )(places, tile_counts, signal, gathered, held)
-    received = exchange(partials, "row")
-    degree_piece = lax.ppermute(degree_piece, ("row", "col"), to_column)
-    walked_piece = 0.5 * jnp.sum(received, axis=0)
-    scaled = (walked_piece / degree_piece).astype(jnp.bfloat16)
-
-    column = all_gather(scaled, "row").reshape(halves * rows, channels, width)
+    walked_piece, scaled = pl.pallas_call(
+        middle_kernel,
+        out_shape=(
+            jax.ShapeDtypeStruct((channels, width), jnp.float32),
+            jax.ShapeDtypeStruct((row_size, channels, width), jnp.bfloat16),
+        ),
+        in_specs=[in_vmem()],
+        out_specs=(in_vmem(), in_vmem()),
+        compiler_params=params,
+        name="middle",
+    )(exchange(partials, "row"))
+
+    column = exchange(scaled, "row")
     walked_piece = lax.ppermute(walked_piece, ("row", "col"), to_row)
     partials = pl.pallas_call(
         second_kernel,

time: 101 us -> 99.9 us (0.989)
  blocking collectives: 39.8 us -> 71.8 us
  starting transfers between devices: 35 us -> 16.2 us
  waiting for transfers between devices: 17.5 us -> 3.51 us
    all_to_all x3 -> x4, blocking collectives: 39.8 us -> 71.8 us  [exchange(): return lax.all_to_all(partials, axis, 0, 0, tiled=True)]
    all_to_all x2 -> x1, starting transfers between devices: 21.3 us -> 7.33 us  [exchange(): return lax.all_to_all(partials, axis, 0, 0, tiled=True)]
    all_to_all x2 -> x1, waiting for transfers between devices: 17.5 us -> 3.51 us  [exchange(): return lax.all_to_all(partials, axis, 0, 0, tiled=True)]
    ppermute x1 -> x0, starting transfers between devices: 5.14 us -> none  [on_device(): degree_piece = lax.ppermute(degree_piece, ('row', 'col'), to_column)]
  transfers between devices with their start and end apart: 4 -> 2, of which waited for: 2 -> 1; matrix products, arithmetic and copies ran while one was open for 0% -> 0% of each run, Pallas kernels for 1% -> 1%
where the time goes in v7:
time: 99.9 us; the launch traced here: 99.5 us
  blocking collectives  71.8 us (72%)
  starting transfers between devices  16.2 us (16%)
  Pallas kernels  6.53 us (7%)
  waiting for transfers between devices  3.51 us (4%)
  between operations  1.4 us (1%)
    all_to_all x4, blocking collectives, exchange(): return lax.all_to_all(partials, axis, 0, 0, tiled=True)  71.8 us
    ppermute x1, starting transfers between devices, on_device(): walked_piece = lax.ppermute(walked_piece, ('row', 'col'), to_row)  8.91 us
    all_to_all x1, starting transfers between devices, exchange(): return lax.all_to_all(partials, axis, 0, 0, tiled=True)  7.33 us
    all_to_all x1, waiting for transfers between devices, exchange(): return lax.all_to_all(partials, axis, 0, 0, tiled=True)  3.51 us
    pallas_call x1, Pallas kernels, on_device(): pl.pallas_call(degree_kernel, out_shape=(pltpu.VMEM((slot_count, width, w...  2.7 us
  transfers between devices with their start and end apart: 2, of which 1 were waited for; matrix products, arithmetic and copies ran while one was open for 0% of the time, Pallas kernels for 1%

profile of v7, /device:TPU:1, one launch (start us, length us, event | category | flops | bytes accessed | tf_op | source)
XLA Modules:
  0.0 99.5 jit_solution(2622886392815339397)
XLA Ops:
  0.6 0.0 copy-start
  1.3 2.7 %degree.1 = (bf16[64,128,128]{2,1,0:T(8,128)(2,1)S(1)}, f32[16,16,128]{2,1,0:T(8,128)S(1)}, s32[1,1,2,64]{3,2,1,0:T(2,128)S(4)}) custom-call(s32[1,1]{1,0:T(1,128)S(6)} %copy.7.counts, s32[1,1,2,64]{3,2,1,0:T(2,128)} %places_hbm.1, bf16[1,1,64,128,128]{4,3,2,1,0:T(8,128)(2,1)} %tiles.1), custom_call_target="tpu_custom_call" | custom-call | tf_op jit(solution)/shard_map/degree/pallas_call | solution.py:146
  4.0 15.4 %all_to_all.25.gathered = f32[16,16,128]{2,1,0:T(8,128)S(1)} all-to-all(f32[16,16,128]{2,1,0:T(8,128)S(1)} %get-tuple-element.11), channel_id=1, replica_groups=mesh['row'=32,'col'=16] {'col'}, dimensions={0} | all-to-all | bytes 262144 | tf_op jit(solution)/shard_map/all_to_all | solution.py:15
  19.5 0.0 copy-done
  19.5 0.7 first.1
  20.2 29.6 %all_to_all.26.received = f32[32,33,1,128]{3,2,1,0:T(1,128)S(1)} all-to-all(f32[32,33,1,128]{3,2,1,0:T(1,128)S(1)} %first.1), channel_id=1, replica_groups=mesh['row'=32,'col'=16] {'row'}, dimensions={0} | all-to-all | bytes 1081344 | tf_op jit(solution)/shard_map/all_to_all | solution.py:15
  49.8 0.9 middle.1
  50.8 7.3 %all-to-all-start.2 = ((bf16[32,32,128]{2,1,0:T(8,128)(2,1)}), bf16[32,32,128]{2,1,0:T(8,128)(2,1)S(1)}, u32[]{:S(2)}, u32[]{:S(2)}) async-start(bf16[32,32,128]{2,1,0:T(8,128)(2,1)} %get-tuple-element.13), calls=%async_computation.2 | async-start | bytes 524288 | tf_op jit(solution)/shard_map/all_to_all | solution.py:15
  58.1 8.9 %collective-permute-start = (f32[32,128]{1,0:T(8,128)S(1)}, f32[32,128]{1,0:T(8,128)S(1)}, u32[]{:S(2)}, u32[]{:S(2)}) collective-permute-start(f32[32,128]{1,0:T(8,128)S(1)} %get-tuple-element.14), channel_id=1, source_target_pairs={{0,0},{16,1},{32,2},{48,3},{64,4},{80,5},{96,6},{112,7},{128,8},{1... | collective-permute-start | bytes 49160 | tf_op jit(solution)/shard_map/ppermute | solution.py:195
  67.0 3.5 %all-to-all-done.2.column = bf16[32,32,128]{2,1,0:T(8,128)(2,1)S(1)} async-done(((bf16[32,32,128]{2,1,0:T(8,128)(2,1)}), bf16[32,32,128]{2,1,0:T(8,128)(2,1)S(1)}, u32[]{:S(2)}, u32[]{:S(2)}) %all-to-all-start.2) | async-done | bytes 262176 | tf_op jit(solution)/shard_map/all_to_all | solution.py:15
  70.5 1.2 %second.1 = f32[16,32,128]{2,1,0:T(8,128)S(1)} custom-call(s32[1,1,2,64]{3,2,1,0:T(2,128)S(4)} %get-tuple-element.10.places, s32[1,1]{1,0:T(1,128)S(6)} %copy.7.counts, bf16[32,32,128]{2,1,0:T(8,128)(2,1)S(1)} %all-to-all-done.2.column, bf16[64,128,128]{2,1,0:T(8,128)(2,1)S(1)} %get-tuple-element.12.held), custom_call_target="tpu_custom_call" | custom-call | tf_op jit(solution)/shard_map/second/pallas_call | solution.py:196
  71.7 0.0 collective-permute-done
  71.7 13.5 %all_to_all.27 = f32[16,32,128]{2,1,0:T(8,128)S(1)} all-to-all(f32[16,32,128]{2,1,0:T(8,128)S(1)} %second.1), channel_id=1, replica_groups=mesh['row'=32,'col'=16] {'col'}, dimensions={0} | all-to-all | bytes 524288 | tf_op jit(solution)/shard_map/all_to_all | solution.py:15
  85.3 0.1 broadcast_in_dim.2
  85.3 13.3 %all_to_all.28.both = f32[16,2,32,128]{3,2,1,0:T(8,128)S(1)} all-to-all(f32[16,2,32,128]{3,2,1,0:T(8,128)S(1)} %broadcast_in_dim.2), channel_id=1, replica_groups=mesh['row'=32,'col'=16] {'col'}, dimensions={0} | all-to-all | bytes 1048576 | tf_op jit(solution)/shard_map/all_to_all | solution.py:15
  98.6 0.9 outputs.1
  (3 shorter events, 0.0 us)
Async XLA Ops:
  0.6 18.9 %copy-start = (f32[32,2048]{1,0:T(8,128)S(1)}, f32[32,2048]{1,0:T(8,128)}, u32[]{:S(2)}) copy-start(f32[32,2048]{1,0:T(8,128)} %signal.3) | copy-start | bytes 786436
  50.8 19.8 %all-to-all-start.2 = ((bf16[32,32,128]{2,1,0:T(8,128)(2,1)}), bf16[32,32,128]{2,1,0:T(8,128)(2,1)S(1)}, u32[]{:S(2)}, u32[]{:S(2)}) async-start(bf16[32,32,128]{2,1,0:T(8,128)(2,1)} %get-tuple-element.13), calls=%async_computation.2 | async-start | bytes 524288 | tf_op jit(solution)/shard_map/all_to_all | solution.py:15
  58.1 13.6 %collective-permute-start = (f32[32,128]{1,0:T(8,128)S(1)}, f32[32,128]{1,0:T(8,128)S(1)}, u32[]{:S(2)}, u32[]{:S(2)}) collective-permute-start(f32[32,128]{1,0:T(8,128)S(1)} %get-tuple-element.14), channel_id=1, source_target_pairs={{0,0},{16,1},{32,2},{48,3},{64,4},{80,5},{96,6},{112,7},{128,8},{1... | collective-permute-start | bytes 49160 | tf_op jit(solution)/shard_map/ppermute | solution.py:195

commit v8 on v7

--- a/solution.py
+++ b/solution.py
@@ -5,9 +5,11 @@
 from jax import lax
 from jax.experimental import pallas as pl
 from jax.experimental.pallas import tpu as pltpu
-from jax.sharding import PartitionSpec as P
+from jax.sharding import Mesh, PartitionSpec as P
 
 CHUNKS = 8
+CORES = 2
+COL = ("chip", "core")
 VMEM_BYTES = 12 * 1024 * 1024
 
 
@@ -57,7 +59,7 @@
     rows = gathered.shape[1]
     channels = signal.shape[0]
     row_index = lax.axis_index("row")
-    col_index = lax.axis_index("col")
+    col_index = lax.axis_index("chip") * CORES + lax.axis_index("core")
     total = gathered[0]
     for source in range(1, gathered.shape[0]):
         total += gathered[source]
@@ -111,11 +113,11 @@
 
 
 def output_kernel(signal, both, first, second, low):
-    rows, _, _, width = both.shape
-    for tile in range(rows):
+    cores, chips, _, _, width = both.shape
+    for tile in range(chips * cores):
         span = slice(tile * width, (tile + 1) * width)
-        walked = both[tile, 0]
-        lowpass = both[tile, 1]
+        walked = both[tile % cores, tile // cores, 0]
+        lowpass = both[tile % cores, tile // cores, 1]
         first[:, span] = jnp.abs(signal[:, span] - walked)
         second[:, span] = jnp.abs(walked - lowpass)
         low[:, span] = lowpass
@@ -134,7 +136,7 @@
     slot_count, width = tile_values.shape[2:4]
     rows = row_len // width
     row_size = lax.axis_size("row")
-    col_size = lax.axis_size("col")
+    col_size = lax.axis_size(COL)
     halves = row_size // col_size
     params = pltpu.CompilerParams(vmem_limit_bytes=VMEM_BYTES)
     to_row = [
@@ -164,7 +166,7 @@
         pltpu.with_memory_space_constraint(tile_places, pltpu.HBM),
         pltpu.with_memory_space_constraint(tile_values, pltpu.HBM),
     )
-    gathered = exchange(degree_part, "col")
+    gathered = exchange(degree_part, COL)
 
     partials = pl.pallas_call(
         functools.partial(first_kernel, halves),
@@ -192,7 +194,7 @@
     )(exchange(partials, "row"))
 
     column = exchange(scaled, "row")
-    walked_piece = lax.ppermute(walked_piece, ("row", "col"), to_row)
+    walked_piece = lax.ppermute(walked_piece, ("row",) + COL, to_row)
     partials = pl.pallas_call(
         second_kernel,
         out_shape=jax.ShapeDtypeStruct((rows, channels, width), jnp.float32),
@@ -202,11 +204,11 @@
         name="second",
     )(places, tile_counts, column, held)
     partials, walked_piece = lax.optimization_barrier((partials, walked_piece))
-    spread = jnp.sum(exchange(partials, "col"), axis=0)
+    spread = jnp.sum(exchange(partials, COL), axis=0)
     lowpass_piece = 0.5 * (walked_piece + spread)
 
-    both = all_gather(jnp.stack([walked_piece, lowpass_piece]), "col")
-    both = both.reshape(rows, 2, channels, width)
+    both = all_gather(jnp.stack([walked_piece, lowpass_piece]), "chip")
+    both = lax.all_gather(both, "core")
     return pl.pallas_call(
         output_kernel,
         out_shape=(jax.ShapeDtypeStruct((channels, row_len), jnp.float32),) * 3,
@@ -218,11 +220,13 @@
 
 
 def solution(mesh):
+    row_size, col_size = mesh.devices.shape
+    mesh = Mesh(mesh.devices.reshape(row_size, col_size // CORES, CORES), ("row",) + COL)
     in_specs = (
         P(None, "row"),
-        P("row", "col", None, None, None),
-        P("row", "col", None, None),
-        P("row", "col"),
+        P("row", COL, None, None, None),
+        P("row", COL, None, None),
+        P("row", COL),
     )
     out_specs = (P(None, "row"), P(None, "row"), P(None, "row"))
     return jax.shard_map(

time: 99.9 us -> 99.2 us (level)
    all_to_all x4, blocking collectives: 71.8 us -> 67.3 us  [exchange(): return lax.all_to_all(partials, axis, 0, 0, tiled=True)]
    all_gather x0 -> x1, blocking collectives: none -> 3.77 us  [on_device(): both = lax.all_gather(both, 'core')]
where the time goes in v8:
time: 99.2 us; the launch traced here: 98.8 us
  blocking collectives  71.1 us (72%)
  starting transfers between devices  16.2 us (16%)
  Pallas kernels  6.53 us (7%)
  waiting for transfers between devices  3.57 us (4%)
  between operations  1.4 us (1%)
    all_to_all x4, blocking collectives, exchange(): return lax.all_to_all(partials, axis, 0, 0, tiled=True)  67.3 us
    ppermute x1, starting transfers between devices, on_device(): walked_piece = lax.ppermute(walked_piece, ('row',) + COL, to_row)  8.86 us
    all_to_all x1, starting transfers between devices, exchange(): return lax.all_to_all(partials, axis, 0, 0, tiled=True)  7.35 us
    all_gather x1, blocking collectives, on_device(): both = lax.all_gather(both, 'core')  3.77 us
    all_to_all x1, waiting for transfers between devices, exchange(): return lax.all_to_all(partials, axis, 0, 0, tiled=True)  3.57 us
    pallas_call x1, Pallas kernels, on_device(): pl.pallas_call(degree_kernel, out_shape=(pltpu.VMEM((slot_count, width, w...  2.71 us
  transfers between devices with their start and end apart: 2, of which 1 were waited for; matrix products, arithmetic and copies ran while one was open for 0% of the time, Pallas kernels for 1%

profile of v8, /device:TPU:1, one launch (start us, length us, event | category | flops | bytes accessed | tf_op | source)
XLA Modules:
  0.0 98.8 jit_solution(1457371411152031276)
XLA Ops:
  0.6 0.0 copy-start
  1.3 2.7 %degree.1 = (bf16[64,128,128]{2,1,0:T(8,128)(2,1)S(1)}, f32[16,16,128]{2,1,0:T(8,128)S(1)}, s32[1,1,2,64]{3,2,1,0:T(2,128)S(4)}) custom-call(s32[1,1]{1,0:T(1,128)S(6)} %copy.7.counts, s32[1,1,2,64]{3,2,1,0:T(2,128)} %places_hbm.1, bf16[1,1,64,128,128]{4,3,2,1,0:T(8,128)(2,1)} %tiles.1), custom_call_target="tpu_custom_call" | custom-call | tf_op jit(solution)/shard_map/degree/pallas_call | solution.py:148
  4.0 15.4 %all_to_all.25.gathered = f32[16,16,128]{2,1,0:T(8,128)S(1)} all-to-all(f32[16,16,128]{2,1,0:T(8,128)S(1)} %get-tuple-element.11), channel_id=1, replica_groups=mesh['row'=32,'chip'=8,'core'=2] {'chip','core'}, dimensions={0} | all-to-all | bytes 262144 | tf_op jit(solution)/shard_map/all_to_all | solution.py:17
  19.5 0.0 copy-done
  19.5 0.7 first.1
  20.2 29.6 %all_to_all.26.received = f32[32,33,1,128]{3,2,1,0:T(1,128)S(1)} all-to-all(f32[32,33,1,128]{3,2,1,0:T(1,128)S(1)} %first.1), channel_id=1, replica_groups=mesh['row'=32,'chip'=8,'core'=2] {'row'}, dimensions={0} | all-to-all | bytes 1081344 | tf_op jit(solution)/shard_map/all_to_all | solution.py:17
  49.8 0.9 middle.1
  50.7 7.3 %all-to-all-start.2 = ((bf16[32,32,128]{2,1,0:T(8,128)(2,1)}), bf16[32,32,128]{2,1,0:T(8,128)(2,1)S(1)}, u32[]{:S(2)}, u32[]{:S(2)}) async-start(bf16[32,32,128]{2,1,0:T(8,128)(2,1)} %get-tuple-element.13), calls=%async_computation.2 | async-start | bytes 524288 | tf_op jit(solution)/shard_map/all_to_all | solution.py:17
  58.1 8.9 %collective-permute-start = (f32[32,128]{1,0:T(8,128)S(1)}, f32[32,128]{1,0:T(8,128)S(1)}, u32[]{:S(2)}, u32[]{:S(2)}) collective-permute-start(f32[32,128]{1,0:T(8,128)S(1)} %get-tuple-element.14), channel_id=1, source_target_pairs={{0,0},{16,1},{32,2},{48,3},{64,4},{80,5},{96,6},{112,7},{128,8},{1... | collective-permute-start | bytes 49160 | tf_op jit(solution)/shard_map/ppermute | solution.py:197
  67.0 3.6 %all-to-all-done.2.column = bf16[32,32,128]{2,1,0:T(8,128)(2,1)S(1)} async-done(((bf16[32,32,128]{2,1,0:T(8,128)(2,1)}), bf16[32,32,128]{2,1,0:T(8,128)(2,1)S(1)}, u32[]{:S(2)}, u32[]{:S(2)}) %all-to-all-start.2) | async-done | bytes 262176 | tf_op jit(solution)/shard_map/all_to_all | solution.py:17
  70.5 1.2 %second.1 = f32[16,32,128]{2,1,0:T(8,128)S(1)} custom-call(s32[1,1,2,64]{3,2,1,0:T(2,128)S(4)} %get-tuple-element.10.places, s32[1,1]{1,0:T(1,128)S(6)} %copy.7.counts, bf16[32,32,128]{2,1,0:T(8,128)(2,1)S(1)} %all-to-all-done.2.column, bf16[64,128,128]{2,1,0:T(8,128)(2,1)S(1)} %get-tuple-element.12.held), custom_call_target="tpu_custom_call" | custom-call | tf_op jit(solution)/shard_map/second/pallas_call | solution.py:198
  71.7 0.0 collective-permute-done
  71.7 13.5 %all_to_all.27 = f32[16,32,128]{2,1,0:T(8,128)S(1)} all-to-all(f32[16,32,128]{2,1,0:T(8,128)S(1)} %second.1), channel_id=1, replica_groups=mesh['row'=32,'chip'=8,'core'=2] {'chip','core'}, dimensions={0} | all-to-all | bytes 524288 | tf_op jit(solution)/shard_map/all_to_all | solution.py:17
  85.3 8.8 %all_to_all.28 = f32[8,2,32,128]{3,2,1,0:T(8,128)S(1)} all-to-all(f32[8,2,32,128]{3,2,1,0:T(8,128)S(1)} %broadcast_in_dim.2), channel_id=1, replica_groups=mesh['row'=32,'chip'=8,'core'=2] {'chip'}, dimensions={0} | all-to-all | bytes 524288 | tf_op jit(solution)/shard_map/all_to_all | solution.py:17
  94.1 3.8 %all-gather = f32[16,2,32,128]{3,2,1,0:T(8,128)S(1)} all-gather(f32[8,2,32,128]{3,2,1,0:T(8,128)S(1)} %all_to_all.28), channel_id=2, replica_groups=mesh['row'=32,'chip'=8,'core'=2] {'core'}, dimensions={0}, use_global_device_ids=true | all-gather | bytes 786432 | tf_op jit(solution)/shard_map/all_gather | solution.py:211
  97.9 0.9 outputs.1
  (4 shorter events, 0.1 us)
Async XLA Ops:
  0.6 18.9 %copy-start = (f32[32,2048]{1,0:T(8,128)S(1)}, f32[32,2048]{1,0:T(8,128)}, u32[]{:S(2)}) copy-start(f32[32,2048]{1,0:T(8,128)} %signal.3) | copy-start | bytes 786436
  50.7 19.8 %all-to-all-start.2 = ((bf16[32,32,128]{2,1,0:T(8,128)(2,1)}), bf16[32,32,128]{2,1,0:T(8,128)(2,1)S(1)}, u32[]{:S(2)}, u32[]{:S(2)}) async-start(bf16[32,32,128]{2,1,0:T(8,128)(2,1)} %get-tuple-element.13), calls=%async_computation.2 | async-start | bytes 524288 | tf_op jit(solution)/shard_map/all_to_all | solution.py:17
  58.1 13.6 %collective-permute-start = (f32[32,128]{1,0:T(8,128)S(1)}, f32[32,128]{1,0:T(8,128)S(1)}, u32[]{:S(2)}, u32[]{:S(2)}) collective-permute-start(f32[32,128]{1,0:T(8,128)S(1)} %get-tuple-element.14), channel_id=1, source_target_pairs={{0,0},{16,1},{32,2},{48,3},{64,4},{80,5},{96,6},{112,7},{128,8},{1... | collective-permute-start | bytes 49160 | tf_op jit(solution)/shard_map/ppermute | solution.py:197

commit v9 on v8

--- a/solution.py
+++ b/solution.py
@@ -7,7 +7,7 @@
 from jax.experimental.pallas import tpu as pltpu
 from jax.sharding import Mesh, PartitionSpec as P
 
-CHUNKS = 8
+CHUNKS = 2
 CORES = 2
 COL = ("chip", "core")
 VMEM_BYTES = 12 * 1024 * 1024
@@ -71,7 +71,8 @@
         for half in range(halves):
             own = row_index == col_index * halves + half
             sums[half * rows + tile] = jnp.where(own, block, 0.0)
-            out[half * rows + tile, channels] = jnp.where(own, nodes, 0.0)
+            end = (half * rows + tile + 1) * (channels + 1)
+            out[end - 1 : end, :] = jnp.where(own, nodes, 0.0)
     for slot in range(slot_count):
         left = scaled[place(places, 0, slot)]
         left = jnp.where(slot < counts[0, 0], left, jnp.zeros_like(left))
@@ -80,22 +81,21 @@
             left, held[slot], (((1,), (0,)), ((), ())), preferred_element_type=jnp.float32
         )
     for tile in range(halves * rows):
-        for channel in range(channels):
-            out[tile, channel] = sums[tile, channel : channel + 1, :]
+        start = tile * (channels + 1)
+        out[start : start + channels, :] = sums[tile]
 
 
 def middle_kernel(received, walked, copies):
-    sources, channels = received.shape[0], received.shape[1] - 1
-
-    def summed(channel):
-        total = received[0, channel]
-        for source in range(1, sources):
-            total += received[source, channel]
-        return total
-
-    for channel in range(channels):
-        walked[channel : channel + 1, :] = 0.5 * summed(channel)
-    scaled = (walked[...] / summed(channels)).astype(jnp.bfloat16)
+    channels = walked.shape[0]
+    sources = received.shape[0] // (channels + 1)
+    total, degree = 0.0, 0.0
+    for source in range(sources):
+        start = source * (channels + 1)
+        total += received[start : start + channels, :]
+        degree += received[start + channels : start + channels + 1, :]
+    total = 0.5 * total
+    walked[...] = total
+    scaled = (total / degree).astype(jnp.bfloat16)
     for target in range(copies.shape[0]):
         copies[target] = scaled
 
@@ -170,7 +170,7 @@
 
     partials = pl.pallas_call(
         functools.partial(first_kernel, halves),
-        out_shape=jax.ShapeDtypeStruct((halves * rows, channels + 1, 1, width), jnp.float32),
+        out_shape=jax.ShapeDtypeStruct((halves * rows * (channels + 1), width), jnp.float32),
         in_specs=[in_smem(), in_smem(), in_vmem(), in_vmem(), in_vmem()],
         out_specs=in_vmem(),
         scratch_shapes=[
@@ -181,6 +181,7 @@
         compiler_params=params,
         name="first",
     )(places, tile_counts, signal, gathered, held)
+    received = exchange(partials.reshape(row_size, channels + 1, 1, width), "row")
     walked_piece, scaled = pl.pallas_call(
         middle_kernel,
         out_shape=(
@@ -191,7 +192,7 @@
         out_specs=(in_vmem(), in_vmem()),
         compiler_params=params,
         name="middle",
-    )(exchange(partials, "row"))
+    )(received.reshape(row_size * (channels + 1), width))
 
     column = exchange(scaled, "row")
     walked_piece = lax.ppermute(walked_piece, ("row",) + COL, to_row)

time: 99.2 us -> 98.5 us (level)
  no operation moved by 1% of the time
where the time goes in v9:
time: 98.5 us; the launch traced here: 98.1 us
  blocking collectives  71.1 us (72%)
  starting transfers between devices  16.2 us (16%)
  Pallas kernels  5.81 us (6%)
  waiting for transfers between devices  3.57 us (4%)
  between operations  1.4 us (1%)
    all_to_all x4, blocking collectives, exchange(): return lax.all_to_all(partials, axis, 0, 0, tiled=True)  67.3 us
    ppermute x1, starting transfers between devices, on_device(): walked_piece = lax.ppermute(walked_piece, ('row',) + COL, to_row)  8.86 us
    all_to_all x1, starting transfers between devices, exchange(): return lax.all_to_all(partials, axis, 0, 0, tiled=True)  7.34 us
    all_gather x1, blocking collectives, on_device(): both = lax.all_gather(both, 'core')  3.77 us
    all_to_all x1, waiting for transfers between devices, exchange(): return lax.all_to_all(partials, axis, 0, 0, tiled=True)  3.57 us
    pallas_call x1, Pallas kernels, on_device(): pl.pallas_call(degree_kernel, out_shape=(pltpu.VMEM((slot_count, width, w...  2.16 us
  transfers between devices with their start and end apart: 2, of which 1 were waited for; matrix products, arithmetic and copies ran while one was open for 0% of the time, Pallas kernels for 1%

profile of v9, /device:TPU:1, one launch (start us, length us, event | category | flops | bytes accessed | tf_op | source)
XLA Modules:
  0.0 98.1 jit_solution(16060909452020495560)
XLA Ops:
  0.6 0.0 copy-start
  1.3 2.2 %degree.1 = (bf16[64,128,128]{2,1,0:T(8,128)(2,1)S(1)}, f32[16,16,128]{2,1,0:T(8,128)S(1)}, s32[1,1,2,64]{3,2,1,0:T(2,128)S(4)}) custom-call(s32[1,1]{1,0:T(1,128)S(6)} %copy.8.counts, s32[1,1,2,64]{3,2,1,0:T(2,128)} %places_hbm.1, bf16[1,1,64,128,128]{4,3,2,1,0:T(8,128)(2,1)} %tiles.1), custom_call_target="tpu_custom_call" | custom-call | tf_op jit(solution)/shard_map/degree/pallas_call | solution.py:148
  3.5 15.5 %all_to_all.25.gathered = f32[16,16,128]{2,1,0:T(8,128)S(1)} all-to-all(f32[16,16,128]{2,1,0:T(8,128)S(1)} %get-tuple-element.11), channel_id=1, replica_groups=mesh['row'=32,'chip'=8,'core'=2] {'chip','core'}, dimensions={0} | all-to-all | bytes 262144 | tf_op jit(solution)/shard_map/all_to_all | solution.py:17
  19.0 0.0 copy-done
  19.0 0.7 first.1
  19.7 29.5 %all_to_all.26 = f32[32,33,1,128]{3,2,1,0:T(1,128)S(1)} all-to-all(f32[32,33,1,128]{3,2,1,0:T(1,128)S(1)} %bitcast.7), channel_id=1, replica_groups=mesh['row'=32,'chip'=8,'core'=2] {'row'}, dimensions={0} | all-to-all | bytes 1081344 | tf_op jit(solution)/shard_map/all_to_all | solution.py:17
  49.3 0.8 middle.1
  50.0 7.3 %all-to-all-start.2 = ((bf16[32,32,128]{2,1,0:T(8,128)(2,1)}), bf16[32,32,128]{2,1,0:T(8,128)(2,1)S(1)}, u32[]{:S(2)}, u32[]{:S(2)}) async-start(bf16[32,32,128]{2,1,0:T(8,128)(2,1)} %get-tuple-element.13), calls=%async_computation.2 | async-start | bytes 524288 | tf_op jit(solution)/shard_map/all_to_all | solution.py:17
  57.4 8.9 %collective-permute-start = (f32[32,128]{1,0:T(8,128)S(1)}, f32[32,128]{1,0:T(8,128)S(1)}, u32[]{:S(2)}, u32[]{:S(2)}) collective-permute-start(f32[32,128]{1,0:T(8,128)S(1)} %get-tuple-element.14), channel_id=1, source_target_pairs={{0,0},{16,1},{32,2},{48,3},{64,4},{80,5},{96,6},{112,7},{128,8},{1... | collective-permute-start | bytes 49160 | tf_op jit(solution)/shard_map/ppermute | solution.py:198
  66.2 3.6 %all-to-all-done.2.column = bf16[32,32,128]{2,1,0:T(8,128)(2,1)S(1)} async-done(((bf16[32,32,128]{2,1,0:T(8,128)(2,1)}), bf16[32,32,128]{2,1,0:T(8,128)(2,1)S(1)}, u32[]{:S(2)}, u32[]{:S(2)}) %all-to-all-start.2) | async-done | bytes 262176 | tf_op jit(solution)/shard_map/all_to_all | solution.py:17
  69.8 1.2 %second.1 = f32[16,32,128]{2,1,0:T(8,128)S(1)} custom-call(s32[1,1,2,64]{3,2,1,0:T(2,128)S(4)} %get-tuple-element.10.places, s32[1,1]{1,0:T(1,128)S(6)} %copy.8.counts, bf16[32,32,128]{2,1,0:T(8,128)(2,1)S(1)} %all-to-all-done.2.column, bf16[64,128,128]{2,1,0:T(8,128)(2,1)S(1)} %get-tuple-element.12.held), custom_call_target="tpu_custom_call" | custom-call | tf_op jit(solution)/shard_map/second/pallas_call | solution.py:199
  71.0 0.0 collective-permute-done
  71.0 13.5 %all_to_all.27 = f32[16,32,128]{2,1,0:T(8,128)S(1)} all-to-all(f32[16,32,128]{2,1,0:T(8,128)S(1)} %second.1), channel_id=1, replica_groups=mesh['row'=32,'chip'=8,'core'=2] {'chip','core'}, dimensions={0} | all-to-all | bytes 524288 | tf_op jit(solution)/shard_map/all_to_all | solution.py:17
  84.6 8.8 %all_to_all.28 = f32[8,2,32,128]{3,2,1,0:T(8,128)S(1)} all-to-all(f32[8,2,32,128]{3,2,1,0:T(8,128)S(1)} %broadcast_in_dim.2), channel_id=1, replica_groups=mesh['row'=32,'chip'=8,'core'=2] {'chip'}, dimensions={0} | all-to-all | bytes 524288 | tf_op jit(solution)/shard_map/all_to_all | solution.py:17
  93.4 3.8 %all-gather = f32[16,2,32,128]{3,2,1,0:T(8,128)S(1)} all-gather(f32[8,2,32,128]{3,2,1,0:T(8,128)S(1)} %all_to_all.28), channel_id=2, replica_groups=mesh['row'=32,'chip'=8,'core'=2] {'core'}, dimensions={0}, use_global_device_ids=true | all-gather | bytes 786432 | tf_op jit(solution)/shard_map/all_gather | solution.py:212
  97.2 0.9 outputs.1
  (4 shorter events, 0.1 us)
Async XLA Ops:
  0.6 18.3 %copy-start = (f32[32,2048]{1,0:T(8,128)S(1)}, f32[32,2048]{1,0:T(8,128)}, u32[]{:S(2)}) copy-start(f32[32,2048]{1,0:T(8,128)} %signal.3) | copy-start | bytes 786436
  50.0 19.8 %all-to-all-start.2 = ((bf16[32,32,128]{2,1,0:T(8,128)(2,1)}), bf16[32,32,128]{2,1,0:T(8,128)(2,1)S(1)}, u32[]{:S(2)}, u32[]{:S(2)}) async-start(bf16[32,32,128]{2,1,0:T(8,128)(2,1)} %get-tuple-element.13), calls=%async_computation.2 | async-start | bytes 524288 | tf_op jit(solution)/shard_map/all_to_all | solution.py:17
  57.4 13.6 %collective-permute-start = (f32[32,128]{1,0:T(8,128)S(1)}, f32[32,128]{1,0:T(8,128)S(1)}, u32[]{:S(2)}, u32[]{:S(2)}) collective-permute-start(f32[32,128]{1,0:T(8,128)S(1)} %get-tuple-element.14), channel_id=1, source_target_pairs={{0,0},{16,1},{32,2},{48,3},{64,4},{80,5},{96,6},{112,7},{128,8},{1... | collective-permute-start | bytes 49160 | tf_op jit(solution)/shard_map/ppermute | solution.py:198

commit v10 on v9

--- a/solution.py
+++ b/solution.py
@@ -9,7 +9,9 @@
 
 CHUNKS = 2
 CORES = 2
+LINES = 4
 COL = ("chip", "core")
+ROW = ("line", "plane")
 VMEM_BYTES = 12 * 1024 * 1024
 
 
@@ -58,7 +60,7 @@
     slot_count, width, _ = held.shape
     rows = gathered.shape[1]
     channels = signal.shape[0]
-    row_index = lax.axis_index("row")
+    row_index = lax.axis_index("plane") * LINES + lax.axis_index("line")
     col_index = lax.axis_index("chip") * CORES + lax.axis_index("core")
     total = gathered[0]
     for source in range(1, gathered.shape[0]):
@@ -135,15 +137,17 @@
     channels, row_len = signal.shape
     slot_count, width = tile_values.shape[2:4]
     rows = row_len // width
-    row_size = lax.axis_size("row")
+    row_size = lax.axis_size(ROW)
+    planes = row_size // LINES
     col_size = lax.axis_size(COL)
     halves = row_size // col_size
     params = pltpu.CompilerParams(vmem_limit_bytes=VMEM_BYTES)
-    to_row = [
-        (((row % halves) * rows + col) * col_size + row // halves, row * col_size + col)
-        for row in range(row_size)
-        for col in range(col_size)
-    ]
+    to_row = []
+    for row in range(row_size):
+        for col in range(col_size):
+            piece = (row % halves) * rows + col
+            source = (piece % planes) * LINES + piece // planes
+            to_row.append((source * col_size + row // halves, row * col_size + col))
 
     held, degree_part, places = pl.pallas_call(
         degree_kernel,
@@ -181,7 +185,7 @@
         compiler_params=params,
         name="first",
     )(places, tile_counts, signal, gathered, held)
-    received = exchange(partials.reshape(row_size, channels + 1, 1, width), "row")
+    received = exchange(partials.reshape(row_size, channels + 1, 1, width), ROW)
     walked_piece, scaled = pl.pallas_call(
         middle_kernel,
         out_shape=(
@@ -194,8 +198,8 @@
         name="middle",
     )(received.reshape(row_size * (channels + 1), width))
 
-    column = exchange(scaled, "row")
-    walked_piece = lax.ppermute(walked_piece, ("row",) + COL, to_row)
+    column = exchange(scaled, ROW)
+    walked_piece = lax.ppermute(walked_piece, ("plane", "line") + COL, to_row)
     partials = pl.pallas_call(
         second_kernel,
         out_shape=jax.ShapeDtypeStruct((rows, channels, width), jnp.float32),
@@ -222,14 +226,16 @@
 
 def solution(mesh):
     row_size, col_size = mesh.devices.shape
-    mesh = Mesh(mesh.devices.reshape(row_size, col_size // CORES, CORES), ("row",) + COL)
+    shape = (row_size // LINES, LINES, col_size // CORES, CORES)
+    mesh = Mesh(mesh.devices.reshape(shape), ("plane", "line") + COL)
+    rows = ("plane", "line")
     in_specs = (
-        P(None, "row"),
-        P("row", COL, None, None, None),
-        P("row", COL, None, None),
-        P("row", COL),
+        P(None, rows),
+        P(rows, COL, None, None, None),
+        P(rows, COL, None, None),
+        P(rows, COL),
     )
-    out_specs = (P(None, "row"), P(None, "row"), P(None, "row"))
+    out_specs = (P(None, rows), P(None, rows), P(None, rows))
     return jax.shard_map(
         on_device, mesh=mesh, in_specs=in_specs, out_specs=out_specs, check_vma=False
     )

time: 98.5 us -> 98 us (level)
  blocking collectives: 71.1 us -> 70.1 us
where the time goes in v10:
time: 98 us; the launch traced here: 97.6 us
  blocking collectives  70.1 us (72%)
  starting transfers between devices  16.1 us (16%)
  Pallas kernels  5.8 us (6%)
  waiting for transfers between devices  4.08 us (4%)
  between operations  1.4 us (1%)
    all_to_all x4, blocking collectives, exchange(): return lax.all_to_all(partials, axis, 0, 0, tiled=True)  66.4 us
    ppermute x1, starting transfers between devices, on_device(): walked_piece = lax.ppermute(walked_piece, ('plane', 'line') + COL, to_row)  8.45 us
    all_to_all x1, starting transfers between devices, exchange(): return lax.all_to_all(partials, axis, 0, 0, tiled=True)  7.69 us
    all_to_all x1, waiting for transfers between devices, exchange(): return lax.all_to_all(partials, axis, 0, 0, tiled=True)  4.08 us
    all_gather x1, blocking collectives, on_device(): both = lax.all_gather(both, 'core')  3.77 us
    pallas_call x1, Pallas kernels, on_device(): pl.pallas_call(degree_kernel, out_shape=(pltpu.VMEM((slot_count, width, w...  2.16 us
  transfers between devices with their start and end apart: 2, of which 1 were waited for; matrix products, arithmetic and copies ran while one was open for 0% of the time, Pallas kernels for 1%

profile of v10, /device:TPU:1, one launch (start us, length us, event | category | flops | bytes accessed | tf_op | source)
XLA Modules:
  0.0 97.6 jit_solution(4829561788654165387)
XLA Ops:
  0.6 0.0 copy-start
  1.3 2.2 %degree.1 = (bf16[64,128,128]{2,1,0:T(8,128)(2,1)S(1)}, f32[16,16,128]{2,1,0:T(8,128)S(1)}, s32[1,1,2,64]{3,2,1,0:T(2,128)S(4)}) custom-call(s32[1,1]{1,0:T(1,128)S(6)} %copy.8.counts, s32[1,1,2,64]{3,2,1,0:T(2,128)} %places_hbm.1, bf16[1,1,64,128,128]{4,3,2,1,0:T(8,128)(2,1)} %tiles.1), custom_call_target="tpu_custom_call" | custom-call | tf_op jit(solution)/shard_map/degree/pallas_call | solution.py:152
  3.5 15.5 %all_to_all.25.gathered = f32[16,16,128]{2,1,0:T(8,128)S(1)} all-to-all(f32[16,16,128]{2,1,0:T(8,128)S(1)} %get-tuple-element.11), channel_id=1, replica_groups=mesh['plane'=8,'line'=4,'chip'=8,'core'=2] {'chip','core'}, dimensions={0} | all-to-all | bytes 262144 | tf_op jit(solution)/shard_map/all_to_all | solution.py:19
  19.0 0.0 copy-done
  19.0 0.7 first.1
  19.7 29.6 %all_to_all.26 = f32[32,33,1,128]{3,2,1,0:T(1,128)S(1)} all-to-all(f32[32,33,1,128]{3,2,1,0:T(1,128)S(1)} %bitcast.7), channel_id=1, replica_groups=mesh['plane'=8,'line'=4,'chip'=8,'core'=2] {'line','plane'}, dimensions={0} | all-to-all | bytes 1081344 | tf_op jit(solution)/shard_map/all_to_all | solution.py:19
  49.3 0.8 middle.1
  50.1 7.7 %all-to-all-start.2 = ((bf16[32,32,128]{2,1,0:T(8,128)(2,1)}), bf16[32,32,128]{2,1,0:T(8,128)(2,1)S(1)}, u32[]{:S(2)}, u32[]{:S(2)}) async-start(bf16[32,32,128]{2,1,0:T(8,128)(2,1)} %get-tuple-element.13), calls=%async_computation.2 | async-start | bytes 524288 | tf_op jit(solution)/shard_map/all_to_all | solution.py:19
  57.8 8.5 %collective-permute-start = (f32[32,128]{1,0:T(8,128)S(1)}, f32[32,128]{1,0:T(8,128)S(1)}, u32[]{:S(2)}, u32[]{:S(2)}) collective-permute-start(f32[32,128]{1,0:T(8,128)S(1)} %get-tuple-element.14), channel_id=1, source_target_pairs={{0,0},{64,1},{128,2},{192,3},{256,4},{320,5},{384,6},{448,7},{16,8... | collective-permute-start | bytes 49160 | tf_op jit(solution)/shard_map/ppermute | solution.py:202
  66.2 4.1 %all-to-all-done.2.column = bf16[32,32,128]{2,1,0:T(8,128)(2,1)S(1)} async-done(((bf16[32,32,128]{2,1,0:T(8,128)(2,1)}), bf16[32,32,128]{2,1,0:T(8,128)(2,1)S(1)}, u32[]{:S(2)}, u32[]{:S(2)}) %all-to-all-start.2) | async-done | bytes 262176 | tf_op jit(solution)/shard_map/all_to_all | solution.py:19
  70.3 1.2 %second.1 = f32[16,32,128]{2,1,0:T(8,128)S(1)} custom-call(s32[1,1,2,64]{3,2,1,0:T(2,128)S(4)} %get-tuple-element.10.places, s32[1,1]{1,0:T(1,128)S(6)} %copy.8.counts, bf16[32,32,128]{2,1,0:T(8,128)(2,1)S(1)} %all-to-all-done.2.column, bf16[64,128,128]{2,1,0:T(8,128)(2,1)S(1)} %get-tuple-element.12.held), custom_call_target="tpu_custom_call" | custom-call | tf_op jit(solution)/shard_map/second/pallas_call | solution.py:203
  71.5 0.0 collective-permute-done
  71.5 12.5 %all_to_all.27 = f32[16,32,128]{2,1,0:T(8,128)S(1)} all-to-all(f32[16,32,128]{2,1,0:T(8,128)S(1)} %second.1), channel_id=1, replica_groups=mesh['plane'=8,'line'=4,'chip'=8,'core'=2] {'chip','core'}, dimensions={0} | all-to-all | bytes 524288 | tf_op jit(solution)/shard_map/all_to_all | solution.py:19
  84.1 8.8 %all_to_all.28 = f32[8,2,32,128]{3,2,1,0:T(8,128)S(1)} all-to-all(f32[8,2,32,128]{3,2,1,0:T(8,128)S(1)} %broadcast_in_dim.2), channel_id=1, replica_groups=mesh['plane'=8,'line'=4,'chip'=8,'core'=2] {'chip'}, dimensions={0} | all-to-all | bytes 524288 | tf_op jit(solution)/shard_map/all_to_all | solution.py:19
  92.9 3.8 %all-gather = f32[16,2,32,128]{3,2,1,0:T(8,128)S(1)} all-gather(f32[8,2,32,128]{3,2,1,0:T(8,128)S(1)} %all_to_all.28), channel_id=2, replica_groups=mesh['plane'=8,'line'=4,'chip'=8,'core'=2] {'core'}, dimensions={0}, use_global_device_ids=true | all-gather | bytes 786432 | tf_op jit(solution)/shard_map/all_gather | solution.py:216
  96.7 0.9 outputs.1
  (4 shorter events, 0.1 us)
Async XLA Ops:
  0.6 18.3 %copy-start = (f32[32,2048]{1,0:T(8,128)S(1)}, f32[32,2048]{1,0:T(8,128)}, u32[]{:S(2)}) copy-start(f32[32,2048]{1,0:T(8,128)} %signal.3) | copy-start | bytes 786436
  50.1 20.2 %all-to-all-start.2 = ((bf16[32,32,128]{2,1,0:T(8,128)(2,1)}), bf16[32,32,128]{2,1,0:T(8,128)(2,1)S(1)}, u32[]{:S(2)}, u32[]{:S(2)}) async-start(bf16[32,32,128]{2,1,0:T(8,128)(2,1)} %get-tuple-element.13), calls=%async_computation.2 | async-start | bytes 524288 | tf_op jit(solution)/shard_map/all_to_all | solution.py:19
  57.8 13.7 %collective-permute-start = (f32[32,128]{1,0:T(8,128)S(1)}, f32[32,128]{1,0:T(8,128)S(1)}, u32[]{:S(2)}, u32[]{:S(2)}) collective-permute-start(f32[32,128]{1,0:T(8,128)S(1)} %get-tuple-element.14), channel_id=1, source_target_pairs={{0,0},{64,1},{128,2},{192,3},{256,4},{320,5},{384,6},{448,7},{16,8... | collective-permute-start | bytes 49160 | tf_op jit(solution)/shard_map/ppermute | solution.py:202

commit v11 on v10

--- a/solution.py
+++ b/solution.py
@@ -102,15 +102,20 @@
         copies[target] = scaled
 
 
-def second_kernel(places, counts, column, held, out):
+def flip_kernel(held, out):
+    for slot in range(held.shape[0]):
+        out[slot] = held[slot].T
+
+
+def second_kernel(places, counts, column, flipped, out):
     for tile in range(out.shape[0]):
         out[tile] = jnp.zeros(out.shape[1:], jnp.float32)
-    for slot in range(held.shape[0]):
+    for slot in range(flipped.shape[0]):
         left = column[place(places, 1, slot)]
         left = jnp.where(slot < counts[0, 0], left, jnp.zeros_like(left))
         target = place(places, 0, slot)
         out[target] += lax.dot_general(
-            left, held[slot], (((1,), (1,)), ((), ())), preferred_element_type=jnp.float32
+            left, flipped[slot], (((1,), (0,)), ((), ())), preferred_element_type=jnp.float32
         )
 
 
@@ -198,6 +203,16 @@
         name="middle",
     )(received.reshape(row_size * (channels + 1), width))
 
+    scaled, held = lax.optimization_barrier((scaled, held))
+    flipped = pl.pallas_call(
+        flip_kernel,
+        out_shape=pltpu.VMEM(held.shape, held.dtype),
+        in_specs=[in_vmem()],
+        out_specs=in_vmem(),
+        input_output_aliases={0: 0},
+        compiler_params=params,
+        name="flip",
+    )(held)
     column = exchange(scaled, ROW)
     walked_piece = lax.ppermute(walked_piece, ("plane", "line") + COL, to_row)
     partials = pl.pallas_call(
@@ -207,7 +222,7 @@
         out_specs=in_vmem(),
         compiler_params=params,
         name="second",
-    )(places, tile_counts, column, held)
+    )(places, tile_counts, column, flipped)
     partials, walked_piece = lax.optimization_barrier((partials, walked_piece))
     spread = jnp.sum(exchange(partials, COL), axis=0)
     lowpass_piece = 0.5 * (walked_piece + spread)

time: 98 us -> 97.8 us (level)
  waiting for transfers between devices: 4.08 us -> 2.66 us
    pallas_call x0 -> x1, Pallas kernels: none -> 1.45 us  [on_device(): pl.pallas_call(flip_kernel, out_shape=pltpu.VMEM(held.shape, held.dtype),...]
    all_to_all x1, waiting for transfers between devices: 4.08 us -> 2.66 us  [exchange(): return lax.all_to_all(partials, axis, 0, 0, tiled=True)]
  transfers between devices with their start and end apart: 2 -> 2, of which waited for: 1 -> 1; matrix products, arithmetic and copies ran while one was open for 0% -> 0% of each run, Pallas kernels for 1% -> 2%
where the time goes in v11:
time: 97.8 us; the launch traced here: 97.1 us
  blocking collectives  70 us (72%)
  starting transfers between devices  16.2 us (17%)
  Pallas kernels  6.74 us (7%)
  waiting for transfers between devices  2.66 us (3%)
  between operations  1.39 us (1%)
    all_to_all x4, blocking collectives, exchange(): return lax.all_to_all(partials, axis, 0, 0, tiled=True)  66.3 us
    ppermute x1, starting transfers between devices, on_device(): walked_piece = lax.ppermute(walked_piece, ('plane', 'line') + COL, to_row)  8.44 us
    all_to_all x1, starting transfers between devices, exchange(): return lax.all_to_all(partials, axis, 0, 0, tiled=True)  7.75 us
    all_gather x1, blocking collectives, on_device(): both = lax.all_gather(both, 'core')  3.77 us
    all_to_all x1, waiting for transfers between devices, exchange(): return lax.all_to_all(partials, axis, 0, 0, tiled=True)  2.66 us
    pallas_call x1, Pallas kernels, on_device(): pl.pallas_call(degree_kernel, out_shape=(pltpu.VMEM((slot_count, width, w...  2.16 us
  transfers between devices with their start and end apart: 2, of which 1 were waited for; matrix products, arithmetic and copies ran while one was open for 0% of the time, Pallas kernels for 2%

profile of v11, /device:TPU:1, one launch (start us, length us, event | category | flops | bytes accessed | tf_op | source)
XLA Modules:
  0.0 97.1 jit_solution(6192129172426679160)
XLA Ops:
  0.6 0.0 copy-start
  1.3 2.2 %degree.1 = (bf16[64,128,128]{2,1,0:T(8,128)(2,1)S(1)}, f32[16,16,128]{2,1,0:T(8,128)S(1)}, s32[1,1,2,64]{3,2,1,0:T(2,128)S(4)}) custom-call(s32[1,1]{1,0:T(1,128)S(6)} %copy.10.counts, s32[1,1,2,64]{3,2,1,0:T(2,128)} %places_hbm.1, bf16[1,1,64,128,128]{4,3,2,1,0:T(8,128)(2,1)} %tiles.1), custom_call_target="tpu_custom_call" | custom-call | tf_op jit(solution)/shard_map/degree/pallas_call | solution.py:157
  3.5 15.5 %all_to_all.25.gathered = f32[16,16,128]{2,1,0:T(8,128)S(1)} all-to-all(f32[16,16,128]{2,1,0:T(8,128)S(1)} %get-tuple-element.13), channel_id=1, replica_groups=mesh['plane'=8,'line'=4,'chip'=8,'core'=2] {'chip','core'}, dimensions={0} | all-to-all | bytes 262144 | tf_op jit(solution)/shard_map/all_to_all | solution.py:19
  19.0 0.0 copy-done
  19.0 0.7 first.1
  19.7 29.5 %all_to_all.26 = f32[32,33,1,128]{3,2,1,0:T(1,128)S(1)} all-to-all(f32[32,33,1,128]{3,2,1,0:T(1,128)S(1)} %bitcast.7), channel_id=1, replica_groups=mesh['plane'=8,'line'=4,'chip'=8,'core'=2] {'line','plane'}, dimensions={0} | all-to-all | bytes 1081344 | tf_op jit(solution)/shard_map/all_to_all | solution.py:19
  49.2 0.8 middle.1
  50.0 7.7 %all-to-all-start.2 = ((bf16[32,32,128]{2,1,0:T(8,128)(2,1)}), bf16[32,32,128]{2,1,0:T(8,128)(2,1)S(1)}, u32[]{:S(2)}, u32[]{:S(2)}) async-start(bf16[32,32,128]{2,1,0:T(8,128)(2,1)} %get-tuple-element.16), calls=%async_computation.2 | async-start | bytes 524288 | tf_op jit(solution)/shard_map/all_to_all | solution.py:19
  57.7 8.4 %collective-permute-start = (f32[32,128]{1,0:T(8,128)S(1)}, f32[32,128]{1,0:T(8,128)S(1)}, u32[]{:S(2)}, u32[]{:S(2)}) collective-permute-start(f32[32,128]{1,0:T(8,128)S(1)} %get-tuple-element.18), channel_id=1, source_target_pairs={{0,0},{64,1},{128,2},{192,3},{256,4},{320,5},{384,6},{448,7},{16,8... | collective-permute-start | bytes 49160 | tf_op jit(solution)/shard_map/ppermute | solution.py:217
  66.2 1.4 %flip.1.flipped = bf16[64,128,128]{2,1,0:T(8,128)(2,1)S(1)} custom-call(bf16[64,128,128]{2,1,0:T(8,128)(2,1)S(1)} %get-tuple-element.17.held), custom_call_target="tpu_custom_call", output_to_operand_aliasing={{}: (0, {})} | custom-call | tf_op jit(solution)/shard_map/flip/pallas_call | solution.py:207
  67.6 2.7 %all-to-all-done.2.column = bf16[32,32,128]{2,1,0:T(8,128)(2,1)S(1)} async-done(((bf16[32,32,128]{2,1,0:T(8,128)(2,1)}), bf16[32,32,128]{2,1,0:T(8,128)(2,1)S(1)}, u32[]{:S(2)}, u32[]{:S(2)}) %all-to-all-start.2) | async-done | bytes 262176 | tf_op jit(solution)/shard_map/all_to_all | solution.py:19
  70.3 0.7 second.1
  71.0 0.0 collective-permute-done
  71.0 12.5 %all_to_all.27 = f32[16,32,128]{2,1,0:T(8,128)S(1)} all-to-all(f32[16,32,128]{2,1,0:T(8,128)S(1)} %second.1), channel_id=1, replica_groups=mesh['plane'=8,'line'=4,'chip'=8,'core'=2] {'chip','core'}, dimensions={0} | all-to-all | bytes 524288 | tf_op jit(solution)/shard_map/all_to_all | solution.py:19
  83.5 8.8 %all_to_all.28 = f32[8,2,32,128]{3,2,1,0:T(8,128)S(1)} all-to-all(f32[8,2,32,128]{3,2,1,0:T(8,128)S(1)} %broadcast_in_dim.2), channel_id=1, replica_groups=mesh['plane'=8,'line'=4,'chip'=8,'core'=2] {'chip'}, dimensions={0} | all-to-all | bytes 524288 | tf_op jit(solution)/shard_map/all_to_all | solution.py:19
  92.4 3.8 %all-gather = f32[16,2,32,128]{3,2,1,0:T(8,128)S(1)} all-gather(f32[8,2,32,128]{3,2,1,0:T(8,128)S(1)} %all_to_all.28), channel_id=2, replica_groups=mesh['plane'=8,'line'=4,'chip'=8,'core'=2] {'core'}, dimensions={0}, use_global_device_ids=true | all-gather | bytes 786432 | tf_op jit(solution)/shard_map/all_gather | solution.py:231
  96.1 0.9 outputs.1
  (4 shorter events, 0.1 us)
Async XLA Ops:
  0.6 18.3 %copy-start = (f32[32,2048]{1,0:T(8,128)S(1)}, f32[32,2048]{1,0:T(8,128)}, u32[]{:S(2)}) copy-start(f32[32,2048]{1,0:T(8,128)} %signal.3) | copy-start | bytes 786436
  50.0 20.3 %all-to-all-start.2 = ((bf16[32,32,128]{2,1,0:T(8,128)(2,1)}), bf16[32,32,128]{2,1,0:T(8,128)(2,1)S(1)}, u32[]{:S(2)}, u32[]{:S(2)}) async-start(bf16[32,32,128]{2,1,0:T(8,128)(2,1)} %get-tuple-element.16), calls=%async_computation.2 | async-start | bytes 524288 | tf_op jit(solution)/shard_map/all_to_all | solution.py:19
  57.7 13.2 %collective-permute-start = (f32[32,128]{1,0:T(8,128)S(1)}, f32[32,128]{1,0:T(8,128)S(1)}, u32[]{:S(2)}, u32[]{:S(2)}) collective-permute-start(f32[32,128]{1,0:T(8,128)S(1)} %get-tuple-element.18), channel_id=1, source_target_pairs={{0,0},{64,1},{128,2},{192,3},{256,4},{320,5},{384,6},{448,7},{16,8... | collective-permute-start | bytes 49160 | tf_op jit(solution)/shard_map/ppermute | solution.py:217

commit v12 on v11

--- a/solution.py
+++ b/solution.py
@@ -8,6 +8,7 @@
 from jax.sharding import Mesh, PartitionSpec as P
 
 CHUNKS = 2
+BATCH = 4
 CORES = 2
 LINES = 4
 COL = ("chip", "core")
@@ -103,8 +104,10 @@
 
 
 def flip_kernel(held, out):
-    for slot in range(held.shape[0]):
-        out[slot] = held[slot].T
+    for start in range(0, held.shape[0], BATCH):
+        tiles = [held[slot].T for slot in range(start, start + BATCH)]
+        for index, tile in enumerate(tiles):
+            out[start + index] = tile
 
 
 def second_kernel(places, counts, column, flipped, out):

time: 97.8 us -> 97.7 us (level)
  no operation moved by 1% of the time
where the time goes in v12:
time: 97.7 us; the launch traced here: 97.2 us
  blocking collectives  70.2 us (72%)
  starting transfers between devices  16.2 us (17%)
  Pallas kernels  6.73 us (7%)
  waiting for transfers between devices  2.7 us (3%)
  between operations  1.39 us (1%)
    all_to_all x4, blocking collectives, exchange(): return lax.all_to_all(partials, axis, 0, 0, tiled=True)  66.4 us
    ppermute x1, starting transfers between devices, on_device(): walked_piece = lax.ppermute(walked_piece, ('plane', 'line') + COL, to_row)  8.42 us
    all_to_all x1, starting transfers between devices, exchange(): return lax.all_to_all(partials, axis, 0, 0, tiled=True)  7.74 us
    all_gather x1, blocking collectives, on_device(): both = lax.all_gather(both, 'core')  3.77 us
    all_to_all x1, waiting for transfers between devices, exchange(): return lax.all_to_all(partials, axis, 0, 0, tiled=True)  2.7 us
    pallas_call x1, Pallas kernels, on_device(): pl.pallas_call(degree_kernel, out_shape=(pltpu.VMEM((slot_count, width, w...  2.16 us
  transfers between devices with their start and end apart: 2, of which 1 were waited for; matrix products, arithmetic and copies ran while one was open for 0% of the time, Pallas kernels for 2%

profile of v12, /device:TPU:1, one launch (start us, length us, event | category | flops | bytes accessed | tf_op | source)
XLA Modules:
  0.0 97.2 jit_solution(6192129172426679160)
XLA Ops:
  0.6 0.0 copy-start
  1.3 2.2 %degree.1 = (bf16[64,128,128]{2,1,0:T(8,128)(2,1)S(1)}, f32[16,16,128]{2,1,0:T(8,128)S(1)}, s32[1,1,2,64]{3,2,1,0:T(2,128)S(4)}) custom-call(s32[1,1]{1,0:T(1,128)S(6)} %copy.10.counts, s32[1,1,2,64]{3,2,1,0:T(2,128)} %places_hbm.1, bf16[1,1,64,128,128]{4,3,2,1,0:T(8,128)(2,1)} %tiles.1), custom_call_target="tpu_custom_call" | custom-call | tf_op jit(solution)/shard_map/degree/pallas_call | solution.py:160
  3.5 15.5 %all_to_all.25.gathered = f32[16,16,128]{2,1,0:T(8,128)S(1)} all-to-all(f32[16,16,128]{2,1,0:T(8,128)S(1)} %get-tuple-element.13), channel_id=1, replica_groups=mesh['plane'=8,'line'=4,'chip'=8,'core'=2] {'chip','core'}, dimensions={0} | all-to-all | bytes 262144 | tf_op jit(solution)/shard_map/all_to_all | solution.py:20
  19.0 0.0 copy-done
  19.0 0.7 first.1
  19.7 29.5 %all_to_all.26 = f32[32,33,1,128]{3,2,1,0:T(1,128)S(1)} all-to-all(f32[32,33,1,128]{3,2,1,0:T(1,128)S(1)} %bitcast.7), channel_id=1, replica_groups=mesh['plane'=8,'line'=4,'chip'=8,'core'=2] {'line','plane'}, dimensions={0} | all-to-all | bytes 1081344 | tf_op jit(solution)/shard_map/all_to_all | solution.py:20
  49.3 0.8 middle.1
  50.0 7.7 %all-to-all-start.2 = ((bf16[32,32,128]{2,1,0:T(8,128)(2,1)}), bf16[32,32,128]{2,1,0:T(8,128)(2,1)S(1)}, u32[]{:S(2)}, u32[]{:S(2)}) async-start(bf16[32,32,128]{2,1,0:T(8,128)(2,1)} %get-tuple-element.16), calls=%async_computation.2 | async-start | bytes 524288 | tf_op jit(solution)/shard_map/all_to_all | solution.py:20
  57.8 8.4 %collective-permute-start = (f32[32,128]{1,0:T(8,128)S(1)}, f32[32,128]{1,0:T(8,128)S(1)}, u32[]{:S(2)}, u32[]{:S(2)}) collective-permute-start(f32[32,128]{1,0:T(8,128)S(1)} %get-tuple-element.18), channel_id=1, source_target_pairs={{0,0},{64,1},{128,2},{192,3},{256,4},{320,5},{384,6},{448,7},{16,8... | collective-permute-start | bytes 49160 | tf_op jit(solution)/shard_map/ppermute | solution.py:220
  66.2 1.4 %flip.1.flipped = bf16[64,128,128]{2,1,0:T(8,128)(2,1)S(1)} custom-call(bf16[64,128,128]{2,1,0:T(8,128)(2,1)S(1)} %get-tuple-element.17.held), custom_call_target="tpu_custom_call", output_to_operand_aliasing={{}: (0, {})} | custom-call | tf_op jit(solution)/shard_map/flip/pallas_call | solution.py:210
  67.7 2.7 %all-to-all-done.2.column = bf16[32,32,128]{2,1,0:T(8,128)(2,1)S(1)} async-done(((bf16[32,32,128]{2,1,0:T(8,128)(2,1)}), bf16[32,32,128]{2,1,0:T(8,128)(2,1)S(1)}, u32[]{:S(2)}, u32[]{:S(2)}) %all-to-all-start.2) | async-done | bytes 262176 | tf_op jit(solution)/shard_map/all_to_all | solution.py:20
  70.4 0.7 second.1
  71.0 0.0 collective-permute-done
  71.0 12.5 %all_to_all.27 = f32[16,32,128]{2,1,0:T(8,128)S(1)} all-to-all(f32[16,32,128]{2,1,0:T(8,128)S(1)} %second.1), channel_id=1, replica_groups=mesh['plane'=8,'line'=4,'chip'=8,'core'=2] {'chip','core'}, dimensions={0} | all-to-all | bytes 524288 | tf_op jit(solution)/shard_map/all_to_all | solution.py:20
  83.7 8.8 %all_to_all.28 = f32[8,2,32,128]{3,2,1,0:T(8,128)S(1)} all-to-all(f32[8,2,32,128]{3,2,1,0:T(8,128)S(1)} %broadcast_in_dim.2), channel_id=1, replica_groups=mesh['plane'=8,'line'=4,'chip'=8,'core'=2] {'chip'}, dimensions={0} | all-to-all | bytes 524288 | tf_op jit(solution)/shard_map/all_to_all | solution.py:20
  92.5 3.8 %all-gather = f32[16,2,32,128]{3,2,1,0:T(8,128)S(1)} all-gather(f32[8,2,32,128]{3,2,1,0:T(8,128)S(1)} %all_to_all.28), channel_id=2, replica_groups=mesh['plane'=8,'line'=4,'chip'=8,'core'=2] {'core'}, dimensions={0}, use_global_device_ids=true | all-gather | bytes 786432 | tf_op jit(solution)/shard_map/all_gather | solution.py:234
  96.3 0.9 outputs.1
  (4 shorter events, 0.1 us)
Async XLA Ops:
  0.6 18.3 %copy-start = (f32[32,2048]{1,0:T(8,128)S(1)}, f32[32,2048]{1,0:T(8,128)}, u32[]{:S(2)}) copy-start(f32[32,2048]{1,0:T(8,128)} %signal.3) | copy-start | bytes 786436
  50.0 20.3 %all-to-all-start.2 = ((bf16[32,32,128]{2,1,0:T(8,128)(2,1)}), bf16[32,32,128]{2,1,0:T(8,128)(2,1)S(1)}, u32[]{:S(2)}, u32[]{:S(2)}) async-start(bf16[32,32,128]{2,1,0:T(8,128)(2,1)} %get-tuple-element.16), calls=%async_computation.2 | async-start | bytes 524288 | tf_op jit(solution)/shard_map/all_to_all | solution.py:20
  57.8 13.3 %collective-permute-start = (f32[32,128]{1,0:T(8,128)S(1)}, f32[32,128]{1,0:T(8,128)S(1)}, u32[]{:S(2)}, u32[]{:S(2)}) collective-permute-start(f32[32,128]{1,0:T(8,128)S(1)} %get-tuple-element.18), channel_id=1, source_target_pairs={{0,0},{64,1},{128,2},{192,3},{256,4},{320,5},{384,6},{448,7},{16,8... | collective-permute-start | bytes 49160 | tf_op jit(solution)/shard_map/ppermute | solution.py:220

commit v13 on v11

--- a/solution.py
+++ b/solution.py
@@ -10,8 +10,11 @@
 CHUNKS = 2
 CORES = 2
 LINES = 4
-COL = ("chip", "core")
+SIDES = 2
+CHIP = ("lane", "side")
+COL = CHIP + ("core",)
 ROW = ("line", "plane")
+MESH = ("plane", "line", "side", "lane", "core")
 VMEM_BYTES = 12 * 1024 * 1024
 
 
@@ -61,7 +64,9 @@
     rows = gathered.shape[1]
     channels = signal.shape[0]
     row_index = lax.axis_index("plane") * LINES + lax.axis_index("line")
-    col_index = lax.axis_index("chip") * CORES + lax.axis_index("core")
+    lanes = lax.axis_size("lane")
+    col_index = lax.axis_index("side") * lanes + lax.axis_index("lane")
+    col_index = col_index * CORES + lax.axis_index("core")
     total = gathered[0]
     for source in range(1, gathered.shape[0]):
         total += gathered[source]
@@ -147,10 +152,13 @@
     col_size = lax.axis_size(COL)
     halves = row_size // col_size
     params = pltpu.CompilerParams(vmem_limit_bytes=VMEM_BYTES)
+    lanes = lax.axis_size("lane")
     to_row = []
     for row in range(row_size):
         for col in range(col_size):
-            piece = (row % halves) * rows + col
+            chip, core = divmod(col, CORES)
+            tile = ((chip % lanes) * SIDES + chip // lanes) * CORES + core
+            piece = (row % halves) * rows + tile
             source = (piece % planes) * LINES + piece // planes
             to_row.append((source * col_size + row // halves, row * col_size + col))
 
@@ -214,7 +222,7 @@
         name="flip",
     )(held)
     column = exchange(scaled, ROW)
-    walked_piece = lax.ppermute(walked_piece, ("plane", "line") + COL, to_row)
+    walked_piece = lax.ppermute(walked_piece, MESH, to_row)
     partials = pl.pallas_call(
         second_kernel,
         out_shape=jax.ShapeDtypeStruct((rows, channels, width), jnp.float32),
@@ -227,7 +235,7 @@
     spread = jnp.sum(exchange(partials, COL), axis=0)
     lowpass_piece = 0.5 * (walked_piece + spread)
 
-    both = all_gather(jnp.stack([walked_piece, lowpass_piece]), "chip")
+    both = all_gather(jnp.stack([walked_piece, lowpass_piece]), CHIP)
     both = lax.all_gather(both, "core")
     return pl.pallas_call(
         output_kernel,
@@ -241,14 +249,14 @@
 
 def solution(mesh):
     row_size, col_size = mesh.devices.shape
-    shape = (row_size // LINES, LINES, col_size // CORES, CORES)
-    mesh = Mesh(mesh.devices.reshape(shape), ("plane", "line") + COL)
-    rows = ("plane", "line")
+    shape = (row_size // LINES, LINES, SIDES, col_size // (SIDES * CORES), CORES)
+    mesh = Mesh(mesh.devices.reshape(shape), MESH)
+    rows, cols = MESH[:2], MESH[2:]
     in_specs = (
         P(None, rows),
-        P(rows, COL, None, None, None),
-        P(rows, COL, None, None),
-        P(rows, COL),
+        P(rows, cols, None, None, None),
+        P(rows, cols, None, None),
+        P(rows, cols),
     )
     out_specs = (P(None, rows), P(None, rows), P(None, rows))
     return jax.shard_map(

time: 97.8 us -> 98.4 us (level)
  no operation moved by 1% of the time
where the time goes in v13:
time: 98.4 us; the launch traced here: 97 us
  blocking collectives  70 us (71%)
  starting transfers between devices  16.1 us (16%)
  Pallas kernels  6.72 us (7%)
  waiting for transfers between devices  2.67 us (3%)
  between operations  1.39 us (1%)
    all_to_all x4, blocking collectives, exchange(): return lax.all_to_all(partials, axis, 0, 0, tiled=True)  66.2 us
    ppermute x1, starting transfers between devices, on_device(): walked_piece = lax.ppermute(walked_piece, MESH, to_row)  8.45 us
    all_to_all x1, starting transfers between devices, exchange(): return lax.all_to_all(partials, axis, 0, 0, tiled=True)  7.68 us
    all_gather x1, blocking collectives, on_device(): both = lax.all_gather(both, 'core')  3.82 us
    all_to_all x1, waiting for transfers between devices, exchange(): return lax.all_to_all(partials, axis, 0, 0, tiled=True)  2.67 us
    pallas_call x1, Pallas kernels, on_device(): pl.pallas_call(degree_kernel, out_shape=(pltpu.VMEM((slot_count, width, w...  2.15 us
  transfers between devices with their start and end apart: 2, of which 1 were waited for; matrix products, arithmetic and copies ran while one was open for 0% of the time, Pallas kernels for 2%

profile of v13, /device:TPU:1, one launch (start us, length us, event | category | flops | bytes accessed | tf_op | source)
XLA Modules:
  0.0 97.0 jit_solution(16004963577882529303)
XLA Ops:
  0.6 0.0 copy-start
  1.3 2.2 %degree.1 = (bf16[64,128,128]{2,1,0:T(8,128)(2,1)S(1)}, f32[16,16,128]{2,1,0:T(8,128)S(1)}, s32[1,1,2,64]{3,2,1,0:T(2,128)S(4)}) custom-call(s32[1,1]{1,0:T(1,128)S(6)} %copy.10.counts, s32[1,1,2,64]{3,2,1,0:T(2,128)} %places_hbm.1, bf16[1,1,64,128,128]{4,3,2,1,0:T(8,128)(2,1)} %tiles.1), custom_call_target="tpu_custom_call" | custom-call | tf_op jit(solution)/shard_map/degree/pallas_call | solution.py:165
  3.5 15.5 %all_to_all.25.gathered = f32[16,16,128]{2,1,0:T(8,128)S(1)} all-to-all(f32[16,16,128]{2,1,0:T(8,128)S(1)} %get-tuple-element.13), channel_id=1, replica_groups=mesh['plane'=8,'line'=4,'side'=2,'lane'=4,'core'=2] {'lane','side','core'}, dimensions={0} | all-to-all | bytes 262144 | tf_op jit(solution)/shard_map/all_to_all | solution.py:22
  19.0 0.0 copy-done
  19.0 0.8 first.1
  19.7 29.6 %all_to_all.26 = f32[32,33,1,128]{3,2,1,0:T(1,128)S(1)} all-to-all(f32[32,33,1,128]{3,2,1,0:T(1,128)S(1)} %bitcast.7), channel_id=1, replica_groups=mesh['plane'=8,'line'=4,'side'=2,'lane'=4,'core'=2] {'line','plane'}, dimensions={0} | all-to-all | bytes 1081344 | tf_op jit(solution)/shard_map/all_to_all | solution.py:22
  49.3 0.8 middle.1
  50.1 7.7 %all-to-all-start.2 = ((bf16[32,32,128]{2,1,0:T(8,128)(2,1)}), bf16[32,32,128]{2,1,0:T(8,128)(2,1)S(1)}, u32[]{:S(2)}, u32[]{:S(2)}) async-start(bf16[32,32,128]{2,1,0:T(8,128)(2,1)} %get-tuple-element.16), calls=%async_computation.2 | async-start | bytes 524288 | tf_op jit(solution)/shard_map/all_to_all | solution.py:22
  57.8 8.4 %collective-permute-start = (f32[32,128]{1,0:T(8,128)S(1)}, f32[32,128]{1,0:T(8,128)S(1)}, u32[]{:S(2)}, u32[]{:S(2)}) collective-permute-start(f32[32,128]{1,0:T(8,128)S(1)} %get-tuple-element.18), channel_id=1, source_target_pairs={{0,0},{64,1},{256,2},{320,3},{16,4},{80,5},{272,6},{336,7},{128,8}... | collective-permute-start | bytes 49160 | tf_op jit(solution)/shard_map/ppermute | solution.py:225
  66.2 1.4 %flip.1.flipped = bf16[64,128,128]{2,1,0:T(8,128)(2,1)S(1)} custom-call(bf16[64,128,128]{2,1,0:T(8,128)(2,1)S(1)} %get-tuple-element.17.held), custom_call_target="tpu_custom_call", output_to_operand_aliasing={{}: (0, {})} | custom-call | tf_op jit(solution)/shard_map/flip/pallas_call | solution.py:215
  67.7 2.7 %all-to-all-done.2.column = bf16[32,32,128]{2,1,0:T(8,128)(2,1)S(1)} async-done(((bf16[32,32,128]{2,1,0:T(8,128)(2,1)}), bf16[32,32,128]{2,1,0:T(8,128)(2,1)S(1)}, u32[]{:S(2)}, u32[]{:S(2)}) %all-to-all-start.2) | async-done | bytes 262176 | tf_op jit(solution)/shard_map/all_to_all | solution.py:22
  70.3 0.7 second.1
  71.0 0.0 collective-permute-done
  71.0 12.4 %all_to_all.27 = f32[16,32,128]{2,1,0:T(8,128)S(1)} all-to-all(f32[16,32,128]{2,1,0:T(8,128)S(1)} %second.1), channel_id=1, replica_groups=mesh['plane'=8,'line'=4,'side'=2,'lane'=4,'core'=2] {'lane','side','core'}, dimensions={0} | all-to-all | bytes 524288 | tf_op jit(solution)/shard_map/all_to_all | solution.py:22
  83.5 8.8 %all_to_all.28 = f32[8,2,32,128]{3,2,1,0:T(8,128)S(1)} all-to-all(f32[8,2,32,128]{3,2,1,0:T(8,128)S(1)} %broadcast_in_dim.2), channel_id=1, replica_groups=mesh['plane'=8,'line'=4,'side'=2,'lane'=4,'core'=2] {'lane','side'}, dimensions={0} | all-to-all | bytes 524288 | tf_op jit(solution)/shard_map/all_to_all | solution.py:22
  92.2 3.8 %all-gather = f32[16,2,32,128]{3,2,1,0:T(8,128)S(1)} all-gather(f32[8,2,32,128]{3,2,1,0:T(8,128)S(1)} %all_to_all.28), channel_id=2, replica_groups=mesh['plane'=8,'line'=4,'side'=2,'lane'=4,'core'=2] {'core'}, dimensions={0}, use_global_device_ids=true | all-gather | bytes 786432 | tf_op jit(solution)/shard_map/all_gather | solution.py:239
  96.0 0.9 outputs.1
  (4 shorter events, 0.1 us)
Async XLA Ops:
  0.6 18.3 %copy-start = (f32[32,2048]{1,0:T(8,128)S(1)}, f32[32,2048]{1,0:T(8,128)}, u32[]{:S(2)}) copy-start(f32[32,2048]{1,0:T(8,128)} %signal.3) | copy-start | bytes 786436
  50.1 20.3 %all-to-all-start.2 = ((bf16[32,32,128]{2,1,0:T(8,128)(2,1)}), bf16[32,32,128]{2,1,0:T(8,128)(2,1)S(1)}, u32[]{:S(2)}, u32[]{:S(2)}) async-start(bf16[32,32,128]{2,1,0:T(8,128)(2,1)} %get-tuple-element.16), calls=%async_computation.2 | async-start | bytes 524288 | tf_op jit(solution)/shard_map/all_to_all | solution.py:22
  57.8 13.3 %collective-permute-start = (f32[32,128]{1,0:T(8,128)S(1)}, f32[32,128]{1,0:T(8,128)S(1)}, u32[]{:S(2)}, u32[]{:S(2)}) collective-permute-start(f32[32,128]{1,0:T(8,128)S(1)} %get-tuple-element.18), channel_id=1, source_target_pairs={{0,0},{64,1},{256,2},{320,3},{16,4},{80,5},{272,6},{336,7},{128,8}... | collective-permute-start | bytes 49160 | tf_op jit(solution)/shard_map/ppermute | solution.py:225

commit v14 on v11

--- a/solution.py
+++ b/solution.py
@@ -214,6 +214,7 @@
         name="flip",
     )(held)
     column = exchange(scaled, ROW)
+    flipped, walked_piece = lax.optimization_barrier((flipped, walked_piece))
     walked_piece = lax.ppermute(walked_piece, ("plane", "line") + COL, to_row)
     partials = pl.pallas_call(
         second_kernel,

time: 97.8 us -> 99.2 us (1.014)
  the two profiles are of different devices: /device:TPU:1 before, /device:TPU:33 now
where the time goes in v14:
time: 99.2 us; the launch traced here: 98.8 us
  blocking collectives  72.5 us (73%)
  starting transfers between devices  12.4 us (12%)
  Pallas kernels  6.68 us (7%)
  waiting for transfers between devices  5.83 us (6%)
  between operations  1.39 us (1%)
    all_to_all x4, blocking collectives, exchange(): return lax.all_to_all(partials, axis, 0, 0, tiled=True)  68.7 us
    all_to_all x1, starting transfers between devices, exchange(): return lax.all_to_all(partials, axis, 0, 0, tiled=True)  8.79 us
    all_to_all x1, waiting for transfers between devices, exchange(): return lax.all_to_all(partials, axis, 0, 0, tiled=True)  5.82 us
    all_gather x1, blocking collectives, on_device(): both = lax.all_gather(both, 'core')  3.77 us
    ppermute x1, starting transfers between devices, on_device(): walked_piece = lax.ppermute(walked_piece, ('plane', 'line') + COL, to_row)  3.62 us
    pallas_call x1, Pallas kernels, on_device(): pl.pallas_call(degree_kernel, out_shape=(pltpu.VMEM((slot_count, width, w...  2.11 us
  transfers between devices with their start and end apart: 2, of which 1 were waited for; matrix products, arithmetic and copies ran while one was open for 0% of the time, Pallas kernels for 2%

profile of v14, /device:TPU:33, one launch (start us, length us, event | category | flops | bytes accessed | tf_op | source)
XLA Modules:
  0.0 98.8 jit_solution(7169446807738913061)
XLA Ops:
  0.6 0.0 copy-start
  1.3 2.1 %degree.1 = (bf16[64,128,128]{2,1,0:T(8,128)(2,1)S(1)}, f32[16,16,128]{2,1,0:T(8,128)S(1)}, s32[1,1,2,64]{3,2,1,0:T(2,128)S(4)}) custom-call(s32[1,1]{1,0:T(1,128)S(6)} %copy.10.counts, s32[1,1,2,64]{3,2,1,0:T(2,128)} %places_hbm.1, bf16[1,1,64,128,128]{4,3,2,1,0:T(8,128)(2,1)} %tiles.1), custom_call_target="tpu_custom_call" | custom-call | tf_op jit(solution)/shard_map/degree/pallas_call | solution.py:157
  3.4 11.1 %all_to_all.25.gathered = f32[16,16,128]{2,1,0:T(8,128)S(1)} all-to-all(f32[16,16,128]{2,1,0:T(8,128)S(1)} %get-tuple-element.15), channel_id=1, replica_groups=mesh['plane'=8,'line'=4,'chip'=8,'core'=2] {'chip','core'}, dimensions={0} | all-to-all | bytes 262144 | tf_op jit(solution)/shard_map/all_to_all | solution.py:19
  14.5 0.0 copy-done
  14.5 0.7 first.1
  15.3 31.7 %all_to_all.26 = f32[32,33,1,128]{3,2,1,0:T(1,128)S(1)} all-to-all(f32[32,33,1,128]{3,2,1,0:T(1,128)S(1)} %bitcast.7), channel_id=1, replica_groups=mesh['plane'=8,'line'=4,'chip'=8,'core'=2] {'line','plane'}, dimensions={0} | all-to-all | bytes 1081344 | tf_op jit(solution)/shard_map/all_to_all | solution.py:19
  47.0 0.8 middle.1
  47.7 8.8 %all-to-all-start.2 = ((bf16[32,32,128]{2,1,0:T(8,128)(2,1)}), bf16[32,32,128]{2,1,0:T(8,128)(2,1)S(1)}, u32[]{:S(2)}, u32[]{:S(2)}) async-start(bf16[32,32,128]{2,1,0:T(8,128)(2,1)} %get-tuple-element.18), calls=%async_computation.2 | async-start | bytes 524288 | tf_op jit(solution)/shard_map/all_to_all | solution.py:19
  56.5 1.4 %flip.1.flipped = bf16[64,128,128]{2,1,0:T(8,128)(2,1)S(1)} custom-call(bf16[64,128,128]{2,1,0:T(8,128)(2,1)S(1)} %get-tuple-element.19.held), custom_call_target="tpu_custom_call", output_to_operand_aliasing={{}: (0, {})} | custom-call | tf_op jit(solution)/shard_map/flip/pallas_call | solution.py:207
  58.0 3.6 %collective-permute-start = (f32[32,128]{1,0:T(8,128)S(1)}, f32[32,128]{1,0:T(8,128)S(1)}, u32[]{:S(2)}, u32[]{:S(2)}) collective-permute-start(f32[32,128]{1,0:T(8,128)S(1)} %get-tuple-element.22), channel_id=1, source_target_pairs={{0,0},{64,1},{128,2},{192,3},{256,4},{320,5},{384,6},{448,7},{16,8... | collective-permute-start | bytes 49160 | tf_op jit(solution)/shard_map/ppermute | solution.py:218
  61.6 5.8 %all-to-all-done.2.column = bf16[32,32,128]{2,1,0:T(8,128)(2,1)S(1)} async-done(((bf16[32,32,128]{2,1,0:T(8,128)(2,1)}), bf16[32,32,128]{2,1,0:T(8,128)(2,1)S(1)}, u32[]{:S(2)}, u32[]{:S(2)}) %all-to-all-start.2) | async-done | bytes 262176 | tf_op jit(solution)/shard_map/all_to_all | solution.py:19
  67.4 0.7 second.1
  68.1 0.0 collective-permute-done
  68.1 17.1 %all_to_all.27 = f32[16,32,128]{2,1,0:T(8,128)S(1)} all-to-all(f32[16,32,128]{2,1,0:T(8,128)S(1)} %second.1), channel_id=1, replica_groups=mesh['plane'=8,'line'=4,'chip'=8,'core'=2] {'chip','core'}, dimensions={0} | all-to-all | bytes 524288 | tf_op jit(solution)/shard_map/all_to_all | solution.py:19
  85.3 8.8 %all_to_all.28 = f32[8,2,32,128]{3,2,1,0:T(8,128)S(1)} all-to-all(f32[8,2,32,128]{3,2,1,0:T(8,128)S(1)} %broadcast_in_dim.2), channel_id=1, replica_groups=mesh['plane'=8,'line'=4,'chip'=8,'core'=2] {'chip'}, dimensions={0} | all-to-all | bytes 524288 | tf_op jit(solution)/shard_map/all_to_all | solution.py:19
  94.1 3.8 %all-gather = f32[16,2,32,128]{3,2,1,0:T(8,128)S(1)} all-gather(f32[8,2,32,128]{3,2,1,0:T(8,128)S(1)} %all_to_all.28), channel_id=2, replica_groups=mesh['plane'=8,'line'=4,'chip'=8,'core'=2] {'core'}, dimensions={0}, use_global_device_ids=true | all-gather | bytes 786432 | tf_op jit(solution)/shard_map/all_gather | solution.py:232
  97.9 0.9 outputs.1
  (4 shorter events, 0.1 us)
Async XLA Ops:
  0.6 13.9 %copy-start = (f32[32,2048]{1,0:T(8,128)S(1)}, f32[32,2048]{1,0:T(8,128)}, u32[]{:S(2)}) copy-start(f32[32,2048]{1,0:T(8,128)} %signal.3) | copy-start | bytes 786436
  47.7 19.7 %all-to-all-start.2 = ((bf16[32,32,128]{2,1,0:T(8,128)(2,1)}), bf16[32,32,128]{2,1,0:T(8,128)(2,1)S(1)}, u32[]{:S(2)}, u32[]{:S(2)}) async-start(bf16[32,32,128]{2,1,0:T(8,128)(2,1)} %get-tuple-element.18), calls=%async_computation.2 | async-start | bytes 524288 | tf_op jit(solution)/shard_map/all_to_all | solution.py:19
  58.0 10.1 %collective-permute-start = (f32[32,128]{1,0:T(8,128)S(1)}, f32[32,128]{1,0:T(8,128)S(1)}, u32[]{:S(2)}, u32[]{:S(2)}) collective-permute-start(f32[32,128]{1,0:T(8,128)S(1)} %get-tuple-element.22), channel_id=1, source_target_pairs={{0,0},{64,1},{128,2},{192,3},{256,4},{320,5},{384,6},{448,7},{16,8... | collective-permute-start | bytes 49160 | tf_op jit(solution)/shard_map/ppermute | solution.py:218

commit v15 on v11

--- a/solution.py
+++ b/solution.py
@@ -27,7 +27,12 @@
     return places[0, 0, which, slot]
 
 
-def degree_kernel(counts, places_hbm, tiles, held, out, places, sums, small, sems):
+def keeper(tile, rows, planes):
+    half, tile = tile // rows, tile % rows
+    return (2 * (tile // planes) + 1 - half) * planes + tile % planes
+
+
+def degree_kernel(planes, counts, places_hbm, tiles, held, out, places, sums, small, sems):
     slot_count = tiles.shape[2]
     copy_places = pltpu.make_async_copy(places_hbm, places, small)
     copy_places.start()
@@ -50,6 +55,11 @@
         for index in range(step):
             slot = chunk * step + index
             row = jnp.where(slot < counts[0, 0], place(places, 0, slot), rows)
+            tile = place(places, 1, slot)
+            half = jnp.where(tile < rows, 0, 1)
+            tile = tile - half * rows
+            upper = jnp.where(tile < planes, 0, 1)
+            places[0, 0, 1, slot] = (upper + 1 - half) * planes + tile
             sums[row] += found[:, index * width : (index + 1) * width]
     for row in range(rows):
         for target in range(targets):
@@ -72,8 +82,9 @@
         scaled[tile] = (block / nodes).astype(jnp.bfloat16)
         for half in range(halves):
             own = row_index == col_index * halves + half
-            sums[half * rows + tile] = jnp.where(own, block, 0.0)
-            end = (half * rows + tile + 1) * (channels + 1)
+            piece = keeper(half * rows + tile, rows, out.shape[0] // (channels + 1) // LINES)
+            sums[piece] = jnp.where(own, block, 0.0)
+            end = (piece + 1) * (channels + 1)
             out[end - 1 : end, :] = jnp.where(own, nodes, 0.0)
     for slot in range(slot_count):
         left = scaled[place(places, 0, slot)]
@@ -150,12 +161,12 @@
     to_row = []
     for row in range(row_size):
         for col in range(col_size):
-            piece = (row % halves) * rows + col
+            piece = keeper((row % halves) * rows + col, rows, planes)
             source = (piece % planes) * LINES + piece // planes
             to_row.append((source * col_size + row // halves, row * col_size + col))
 
     held, degree_part, places = pl.pallas_call(
-        degree_kernel,
+        functools.partial(degree_kernel, planes),
         out_shape=(
             pltpu.VMEM((slot_count, width, width), jnp.bfloat16),
             jax.ShapeDtypeStruct((col_size, rows, width), jnp.float32),

time: 97.8 us -> 99.3 us (1.015)
  blocking collectives: 70 us -> 71.9 us
  waiting for transfers between devices: 2.66 us -> 4.47 us
  starting transfers between devices: 16.2 us -> 14.4 us
    all_to_all x4, blocking collectives: 66.3 us -> 68.2 us  [exchange(): return lax.all_to_all(partials, axis, 0, 0, tiled=True)]
    all_to_all x1, waiting for transfers between devices: 2.66 us -> 4.47 us  [exchange(): return lax.all_to_all(partials, axis, 0, 0, tiled=True)]
    ppermute x1, starting transfers between devices: 8.44 us -> 6.67 us  [on_device(): walked_piece = lax.ppermute(walked_piece, ('plane', 'line') + COL, to_row)]
where the time goes in v15:
time: 99.3 us; the launch traced here: 99 us
  blocking collectives  71.9 us (72%)
  starting transfers between devices  14.4 us (15%)
  Pallas kernels  6.72 us (7%)
  waiting for transfers between devices  4.47 us (5%)
  between operations  1.39 us (1%)
    all_to_all x4, blocking collectives, exchange(): return lax.all_to_all(partials, axis, 0, 0, tiled=True)  68.2 us
    all_to_all x1, starting transfers between devices, exchange(): return lax.all_to_all(partials, axis, 0, 0, tiled=True)  7.72 us
    ppermute x1, starting transfers between devices, on_device(): walked_piece = lax.ppermute(walked_piece, ('plane', 'line') + COL, to_row)  6.67 us
    all_to_all x1, waiting for transfers between devices, exchange(): return lax.all_to_all(partials, axis, 0, 0, tiled=True)  4.47 us
    all_gather x1, blocking collectives, on_device(): both = lax.all_gather(both, 'core')  3.77 us
    pallas_call x1, Pallas kernels, on_device(): pl.pallas_call(functools.partial(degree_kernel, planes), out_shape=(pltpu...  2.15 us
  transfers between devices with their start and end apart: 2, of which 1 were waited for; matrix products, arithmetic and copies ran while one was open for 0% of the time, Pallas kernels for 2%

profile of v15, /device:TPU:1, one launch (start us, length us, event | category | flops | bytes accessed | tf_op | source)
XLA Modules:
  0.0 99.0 jit_solution(10918475206846912153)
XLA Ops:
  0.6 0.0 copy-start
  1.3 2.2 %degree.1 = (bf16[64,128,128]{2,1,0:T(8,128)(2,1)S(1)}, f32[16,16,128]{2,1,0:T(8,128)S(1)}, s32[1,1,2,64]{3,2,1,0:T(2,128)S(4)}) custom-call(s32[1,1]{1,0:T(1,128)S(6)} %copy.10.counts, s32[1,1,2,64]{3,2,1,0:T(2,128)} %places_hbm.1, bf16[1,1,64,128,128]{4,3,2,1,0:T(8,128)(2,1)} %tiles.1), custom_call_target="tpu_custom_call" | custom-call | tf_op jit(solution)/shard_map/degree/pallas_call | solution.py:168
  3.5 15.5 %all_to_all.25.gathered = f32[16,16,128]{2,1,0:T(8,128)S(1)} all-to-all(f32[16,16,128]{2,1,0:T(8,128)S(1)} %get-tuple-element.13), channel_id=1, replica_groups=mesh['plane'=8,'line'=4,'chip'=8,'core'=2] {'chip','core'}, dimensions={0} | all-to-all | bytes 262144 | tf_op jit(solution)/shard_map/all_to_all | solution.py:19
  19.0 0.0 copy-done
  19.0 0.7 first.1
  19.7 29.6 %all_to_all.26 = f32[32,33,1,128]{3,2,1,0:T(1,128)S(1)} all-to-all(f32[32,33,1,128]{3,2,1,0:T(1,128)S(1)} %bitcast.7), channel_id=1, replica_groups=mesh['plane'=8,'line'=4,'chip'=8,'core'=2] {'line','plane'}, dimensions={0} | all-to-all | bytes 1081344 | tf_op jit(solution)/shard_map/all_to_all | solution.py:19
  49.3 0.8 middle.1
  50.1 7.7 %all-to-all-start.2 = ((bf16[32,32,128]{2,1,0:T(8,128)(2,1)}), bf16[32,32,128]{2,1,0:T(8,128)(2,1)S(1)}, u32[]{:S(2)}, u32[]{:S(2)}) async-start(bf16[32,32,128]{2,1,0:T(8,128)(2,1)} %get-tuple-element.16), calls=%async_computation.2 | async-start | bytes 524288 | tf_op jit(solution)/shard_map/all_to_all | solution.py:19
  57.8 6.7 %collective-permute-start = (f32[32,128]{1,0:T(8,128)S(1)}, f32[32,128]{1,0:T(8,128)S(1)}, u32[]{:S(2)}, u32[]{:S(2)}) collective-permute-start(f32[32,128]{1,0:T(8,128)S(1)} %get-tuple-element.18), channel_id=1, source_target_pairs={{16,0},{80,1},{144,2},{208,3},{272,4},{336,5},{400,6},{464,7},{48,... | collective-permute-start | bytes 49160 | tf_op jit(solution)/shard_map/ppermute | solution.py:228
  64.5 1.4 %flip.1.flipped = bf16[64,128,128]{2,1,0:T(8,128)(2,1)S(1)} custom-call(bf16[64,128,128]{2,1,0:T(8,128)(2,1)S(1)} %get-tuple-element.17.held), custom_call_target="tpu_custom_call", output_to_operand_aliasing={{}: (0, {})} | custom-call | tf_op jit(solution)/shard_map/flip/pallas_call | solution.py:218
  65.9 4.5 %all-to-all-done.2.column = bf16[32,32,128]{2,1,0:T(8,128)(2,1)S(1)} async-done(((bf16[32,32,128]{2,1,0:T(8,128)(2,1)}), bf16[32,32,128]{2,1,0:T(8,128)(2,1)S(1)}, u32[]{:S(2)}, u32[]{:S(2)}) %all-to-all-start.2) | async-done | bytes 262176 | tf_op jit(solution)/shard_map/all_to_all | solution.py:19
  70.4 0.7 second.1
  71.1 0.0 collective-permute-done
  71.1 14.2 %all_to_all.27 = f32[16,32,128]{2,1,0:T(8,128)S(1)} all-to-all(f32[16,32,128]{2,1,0:T(8,128)S(1)} %second.1), channel_id=1, replica_groups=mesh['plane'=8,'line'=4,'chip'=8,'core'=2] {'chip','core'}, dimensions={0} | all-to-all | bytes 524288 | tf_op jit(solution)/shard_map/all_to_all | solution.py:19
  85.4 8.8 %all_to_all.28 = f32[8,2,32,128]{3,2,1,0:T(8,128)S(1)} all-to-all(f32[8,2,32,128]{3,2,1,0:T(8,128)S(1)} %broadcast_in_dim.2), channel_id=1, replica_groups=mesh['plane'=8,'line'=4,'chip'=8,'core'=2] {'chip'}, dimensions={0} | all-to-all | bytes 524288 | tf_op jit(solution)/shard_map/all_to_all | solution.py:19
  94.2 3.8 %all-gather = f32[16,2,32,128]{3,2,1,0:T(8,128)S(1)} all-gather(f32[8,2,32,128]{3,2,1,0:T(8,128)S(1)} %all_to_all.28), channel_id=2, replica_groups=mesh['plane'=8,'line'=4,'chip'=8,'core'=2] {'core'}, dimensions={0}, use_global_device_ids=true | all-gather | bytes 786432 | tf_op jit(solution)/shard_map/all_gather | solution.py:242
  98.0 0.9 outputs.1
  (4 shorter events, 0.1 us)
Async XLA Ops:
  0.6 18.3 %copy-start = (f32[32,2048]{1,0:T(8,128)S(1)}, f32[32,2048]{1,0:T(8,128)}, u32[]{:S(2)}) copy-start(f32[32,2048]{1,0:T(8,128)} %signal.3) | copy-start | bytes 786436
  50.1 20.3 %all-to-all-start.2 = ((bf16[32,32,128]{2,1,0:T(8,128)(2,1)}), bf16[32,32,128]{2,1,0:T(8,128)(2,1)S(1)}, u32[]{:S(2)}, u32[]{:S(2)}) async-start(bf16[32,32,128]{2,1,0:T(8,128)(2,1)} %get-tuple-element.16), calls=%async_computation.2 | async-start | bytes 524288 | tf_op jit(solution)/shard_map/all_to_all | solution.py:19
  57.8 13.3 %collective-permute-start = (f32[32,128]{1,0:T(8,128)S(1)}, f32[32,128]{1,0:T(8,128)S(1)}, u32[]{:S(2)}, u32[]{:S(2)}) collective-permute-start(f32[32,128]{1,0:T(8,128)S(1)} %get-tuple-element.18), channel_id=1, source_target_pairs={{16,0},{80,1},{144,2},{208,3},{272,4},{336,5},{400,6},{464,7},{48,... | collective-permute-start | bytes 49160 | tf_op jit(solution)/shard_map/ppermute | solution.py:228

commit v16 on v11

--- a/solution.py
+++ b/solution.py
@@ -8,6 +8,7 @@
 from jax.sharding import Mesh, PartitionSpec as P
 
 CHUNKS = 2
+COPIES = 2
 CORES = 2
 LINES = 4
 COL = ("chip", "core")
@@ -33,16 +34,18 @@
     copy_places.start()
     step = slot_count // CHUNKS
     copies = []
-    for chunk in range(CHUNKS):
-        span = pl.ds(chunk * step, step)
-        copies.append(pltpu.make_async_copy(tiles.at[0, 0, span], held.at[span], sems.at[chunk]))
+    part = step // COPIES
+    for index in range(CHUNKS * COPIES):
+        span = pl.ds(index * part, part)
+        copies.append(pltpu.make_async_copy(tiles.at[0, 0, span], held.at[span], sems.at[index]))
         copies[-1].start()
     targets, rows, width = out.shape
     sums[...] = jnp.zeros_like(sums)
     ones = jnp.ones((8, width), jnp.bfloat16)
     copy_places.wait()
     for chunk in range(CHUNKS):
-        copies[chunk].wait()
+        for copy in copies[chunk * COPIES : (chunk + 1) * COPIES]:
+            copy.wait()
         block = held[chunk * step : (chunk + 1) * step].reshape(step * width, width)
         found = lax.dot_general(
             ones, block, (((1,), (1,)), ((), ())), preferred_element_type=jnp.float32
@@ -166,7 +169,7 @@
         scratch_shapes=[
             pltpu.VMEM((rows + 1, 8, width), jnp.float32),
             pltpu.SemaphoreType.DMA,
-            pltpu.SemaphoreType.DMA((CHUNKS,)),
+            pltpu.SemaphoreType.DMA((CHUNKS * COPIES,)),
         ],
         compiler_params=params,
         name="degree",

time: 97.8 us -> 97.8 us (level)
  no operation moved by 1% of the time
where the time goes in v16:
time: 97.8 us; the launch traced here: 97.1 us
  blocking collectives  70.1 us (72%)
  starting transfers between devices  16.1 us (16%)
  Pallas kernels  6.72 us (7%)
  waiting for transfers between devices  2.69 us (3%)
  between operations  1.39 us (1%)
    all_to_all x4, blocking collectives, exchange(): return lax.all_to_all(partials, axis, 0, 0, tiled=True)  66.3 us
    ppermute x1, starting transfers between devices, on_device(): walked_piece = lax.ppermute(walked_piece, ('plane', 'line') + COL, to_row)  8.43 us
    all_to_all x1, starting transfers between devices, exchange(): return lax.all_to_all(partials, axis, 0, 0, tiled=True)  7.72 us
    all_gather x1, blocking collectives, on_device(): both = lax.all_gather(both, 'core')  3.77 us
    all_to_all x1, waiting for transfers between devices, exchange(): return lax.all_to_all(partials, axis, 0, 0, tiled=True)  2.69 us
    pallas_call x1, Pallas kernels, on_device(): pl.pallas_call(degree_kernel, out_shape=(pltpu.VMEM((slot_count, width, w...  2.15 us
  transfers between devices with their start and end apart: 2, of which 1 were waited for; matrix products, arithmetic and copies ran while one was open for 0% of the time, Pallas kernels for 2%

profile of v16, /device:TPU:1, one launch (start us, length us, event | category | flops | bytes accessed | tf_op | source)
XLA Modules:
  0.0 97.1 jit_solution(5073883968855788476)
XLA Ops:
  0.6 0.0 copy-start
  1.3 2.2 %degree.1 = (bf16[64,128,128]{2,1,0:T(8,128)(2,1)S(1)}, f32[16,16,128]{2,1,0:T(8,128)S(1)}, s32[1,1,2,64]{3,2,1,0:T(2,128)S(4)}) custom-call(s32[1,1]{1,0:T(1,128)S(6)} %copy.10.counts, s32[1,1,2,64]{3,2,1,0:T(2,128)} %places_hbm.1, bf16[1,1,64,128,128]{4,3,2,1,0:T(8,128)(2,1)} %tiles.1), custom_call_target="tpu_custom_call" | custom-call | tf_op jit(solution)/shard_map/degree/pallas_call | solution.py:160
  3.5 15.5 %all_to_all.25.gathered = f32[16,16,128]{2,1,0:T(8,128)S(1)} all-to-all(f32[16,16,128]{2,1,0:T(8,128)S(1)} %get-tuple-element.13), channel_id=1, replica_groups=mesh['plane'=8,'line'=4,'chip'=8,'core'=2] {'chip','core'}, dimensions={0} | all-to-all | bytes 262144 | tf_op jit(solution)/shard_map/all_to_all | solution.py:20
  19.0 0.0 copy-done
  19.0 0.7 first.1
  19.7 29.6 %all_to_all.26 = f32[32,33,1,128]{3,2,1,0:T(1,128)S(1)} all-to-all(f32[32,33,1,128]{3,2,1,0:T(1,128)S(1)} %bitcast.7), channel_id=1, replica_groups=mesh['plane'=8,'line'=4,'chip'=8,'core'=2] {'line','plane'}, dimensions={0} | all-to-all | bytes 1081344 | tf_op jit(solution)/shard_map/all_to_all | solution.py:20
  49.3 0.8 middle.1
  50.0 7.7 %all-to-all-start.2 = ((bf16[32,32,128]{2,1,0:T(8,128)(2,1)}), bf16[32,32,128]{2,1,0:T(8,128)(2,1)S(1)}, u32[]{:S(2)}, u32[]{:S(2)}) async-start(bf16[32,32,128]{2,1,0:T(8,128)(2,1)} %get-tuple-element.16), calls=%async_computation.2 | async-start | bytes 524288 | tf_op jit(solution)/shard_map/all_to_all | solution.py:20
  57.8 8.4 %collective-permute-start = (f32[32,128]{1,0:T(8,128)S(1)}, f32[32,128]{1,0:T(8,128)S(1)}, u32[]{:S(2)}, u32[]{:S(2)}) collective-permute-start(f32[32,128]{1,0:T(8,128)S(1)} %get-tuple-element.18), channel_id=1, source_target_pairs={{0,0},{64,1},{128,2},{192,3},{256,4},{320,5},{384,6},{448,7},{16,8... | collective-permute-start | bytes 49160 | tf_op jit(solution)/shard_map/ppermute | solution.py:220
  66.2 1.4 %flip.1.flipped = bf16[64,128,128]{2,1,0:T(8,128)(2,1)S(1)} custom-call(bf16[64,128,128]{2,1,0:T(8,128)(2,1)S(1)} %get-tuple-element.17.held), custom_call_target="tpu_custom_call", output_to_operand_aliasing={{}: (0, {})} | custom-call | tf_op jit(solution)/shard_map/flip/pallas_call | solution.py:210
  67.7 2.7 %all-to-all-done.2.column = bf16[32,32,128]{2,1,0:T(8,128)(2,1)S(1)} async-done(((bf16[32,32,128]{2,1,0:T(8,128)(2,1)}), bf16[32,32,128]{2,1,0:T(8,128)(2,1)S(1)}, u32[]{:S(2)}, u32[]{:S(2)}) %all-to-all-start.2) | async-done | bytes 262176 | tf_op jit(solution)/shard_map/all_to_all | solution.py:20
  70.3 0.7 second.1
  71.0 0.0 collective-permute-done
  71.0 12.4 %all_to_all.27 = f32[16,32,128]{2,1,0:T(8,128)S(1)} all-to-all(f32[16,32,128]{2,1,0:T(8,128)S(1)} %second.1), channel_id=1, replica_groups=mesh['plane'=8,'line'=4,'chip'=8,'core'=2] {'chip','core'}, dimensions={0} | all-to-all | bytes 524288 | tf_op jit(solution)/shard_map/all_to_all | solution.py:20
  83.6 8.8 %all_to_all.28 = f32[8,2,32,128]{3,2,1,0:T(8,128)S(1)} all-to-all(f32[8,2,32,128]{3,2,1,0:T(8,128)S(1)} %broadcast_in_dim.2), channel_id=1, replica_groups=mesh['plane'=8,'line'=4,'chip'=8,'core'=2] {'chip'}, dimensions={0} | all-to-all | bytes 524288 | tf_op jit(solution)/shard_map/all_to_all | solution.py:20
  92.4 3.8 %all-gather = f32[16,2,32,128]{3,2,1,0:T(8,128)S(1)} all-gather(f32[8,2,32,128]{3,2,1,0:T(8,128)S(1)} %all_to_all.28), channel_id=2, replica_groups=mesh['plane'=8,'line'=4,'chip'=8,'core'=2] {'core'}, dimensions={0}, use_global_device_ids=true | all-gather | bytes 786432 | tf_op jit(solution)/shard_map/all_gather | solution.py:234
  96.2 0.9 outputs.1
  (4 shorter events, 0.1 us)
Async XLA Ops:
  0.6 18.3 %copy-start = (f32[32,2048]{1,0:T(8,128)S(1)}, f32[32,2048]{1,0:T(8,128)}, u32[]{:S(2)}) copy-start(f32[32,2048]{1,0:T(8,128)} %signal.3) | copy-start | bytes 786436
  50.0 20.3 %all-to-all-start.2 = ((bf16[32,32,128]{2,1,0:T(8,128)(2,1)}), bf16[32,32,128]{2,1,0:T(8,128)(2,1)S(1)}, u32[]{:S(2)}, u32[]{:S(2)}) async-start(bf16[32,32,128]{2,1,0:T(8,128)(2,1)} %get-tuple-element.16), calls=%async_computation.2 | async-start | bytes 524288 | tf_op jit(solution)/shard_map/all_to_all | solution.py:20
  57.8 13.3 %collective-permute-start = (f32[32,128]{1,0:T(8,128)S(1)}, f32[32,128]{1,0:T(8,128)S(1)}, u32[]{:S(2)}, u32[]{:S(2)}) collective-permute-start(f32[32,128]{1,0:T(8,128)S(1)} %get-tuple-element.18), channel_id=1, source_target_pairs={{0,0},{64,1},{128,2},{192,3},{256,4},{320,5},{384,6},{448,7},{16,8... | collective-permute-start | bytes 49160 | tf_op jit(solution)/shard_map/ppermute | solution.py:220
